TPU v7x, 32 devices: a whole 2x2x4 slice. The times are simulated.
32 devices in a mesh: dp: 8 (over z, y), filt: 4 (over x, core).
Axes of the slice: x: 2, y: 2, z: 4, core: 2. Of those that a mesh axis runs over, the one named last changes fastest.
Arguments:
- chars: int32 [8, 512, 50], P('dp'), may hold values from 0 to 261
- lengths: int32 [8], P('dp'), may hold values from 385 to 512, as said below
- char_table: bfloat16 [262, 16], replicated, may hold values from -6 to 6
- conv_weight: bfloat16 [112, 2048], P(None, 'filt'), may hold values from -0.5 to 0.5
- conv_bias: bfloat16 [2048], P('filt'), may hold values from -3 to 3
- highway_weight: bfloat16 [1, 2048, 4096], P(None, 'dp'), may hold values from -0.125 to 0.125
- highway_bias: bfloat16 [1, 4096], P(None, 'dp'), may hold values from -3 to 3
- proj_weight: bfloat16 [2048, 768], P('dp'), may hold values from -0.125 to 0.125
- proj_bias: bfloat16 [768], P('dp'), may hold values from -3 to 3
- position: bfloat16 [512, 768], P('filt'), may hold values from -3 to 3
- norm_gain: bfloat16 [3, 768], P(None, 'dp'), may hold values from 0.099609375 to 1.8984375
- norm_bias: bfloat16 [3, 768], P(None, 'dp'), may hold values from -2 to 2
- query_key_value_weight: bfloat16 [768, 2304], P('dp'), may hold values from -0.21875 to 0.21875
- attention_output_weight: bfloat16 [768, 768], P('dp'), may hold values from -0.875 to 0.875
- feedforward_input_weight: bfloat16 [768, 3072], P('dp'), may hold values from -0.21875 to 0.21875
- feedforward_input_bias: bfloat16 [3072], P('dp'), may hold values from -3 to 3
- feedforward_output_weight: bfloat16 [3072, 768], P('dp'), may hold values from -0.109375 to 0.109375
- cotangent: bfloat16 [8, 512, 768], P('dp', 'filt'), may hold values from -6 to 6
Outputs:
- encoded: bfloat16 [8, 512, 768], P('dp', 'filt')
- grad_char_table: float32 [262, 16], replicated
- grad_conv_weight: float32 [112, 2048], P(None, 'filt')
- grad_conv_bias: float32 [2048], P('filt')
- grad_highway_weight: float32 [1, 2048, 4096], P(None, 'dp')
- grad_highway_bias: float32 [1, 4096], P(None, 'dp')
- grad_proj_weight: float32 [2048, 768], P('dp')
- grad_proj_bias: float32 [768], P('dp')
- grad_position: float32 [512, 768], P('filt')
- grad_norm_gain: float32 [3, 768], P(None, 'dp')
- grad_norm_bias: float32 [3, 768], P(None, 'dp')
- grad_qkv_weight: float32 [768, 2304], P('dp')
- grad_out_weight: float32 [768, 768], P('dp')
- grad_ffn_in_weight: float32 [768, 3072], P('dp')
- grad_ffn_in_bias: float32 [3072], P('dp')
- grad_ffn_out_weight: float32 [3072, 768], P('dp')
Inputs may be any that keep to these rules, and one draw needn't show every extreme that they name: `lengths`: every sequence fills more than three quarters of its 512 slots, and some sequence fills all of them.
All inputs are finite; a program needn't handle non-finite values.
Results may differ from a plain program's by a relative error of at most 0.017.
Values may be sent and summed in bfloat16 or wider, within the bound.
A program may use at most 256 MiB of HBM per device.

v0:
```python
import functools

import jax
import jax.numpy as jnp
from jax import lax
from jax.experimental import pallas as pl
from jax.experimental.pallas import tpu as pltpu
from jax.sharding import PartitionSpec as P

KW = 7
NF = 2048
HD = 64
EPS = 1e-12
ROOT_HALF = 0.7071067811865476
DENSITY = 0.3989422804014327

def nt_dot(left, right):
    return lax.dot_general(left, right, (((1,), (1,)), ((), ())), preferred_element_type=jnp.float32)

def nn_dot(left, right):
    return jnp.dot(left, right, preferred_element_type=jnp.float32)

def normal_cdf(values):
    return 0.5 * (1.0 + lax.erf(values * ROOT_HALF))

def char_parts(chars_ref, position, block):
    ids = chars_ref[pl.ds(position, 1), :]
    low = ids & 127
    group = ids >> 7
    onehot = (lax.broadcasted_iota(jnp.int32, (128, block), 0) == low)
    onehot = jnp.where(onehot, 1.0, 0.0).astype(jnp.bfloat16)
    return onehot, group

def conv_forward(letters, depth, chars_ref, table_ref, weight_ref, limit_ref, count_ref,
                 acts_ref, lse_ref, embed_ref, patch_ref, grid_ref):
    block = chars_ref.shape[1]
    filters = weight_ref.shape[0]
    groups = table_ref.shape[0] // depth
    lead = KW - 1
    rows = KW * depth

    @pl.when(pl.program_id(0) == 0)
    def _():
        patch_ref[:, :rows, :] = jnp.zeros((patch_ref.shape[0], rows, block), jnp.bfloat16)
        ones = lax.broadcasted_iota(jnp.int32, (128 - rows, block), 0) == 0
        tail = jnp.where(ones, 1.0, 0.0).astype(jnp.bfloat16)
        patch_ref[:, rows:, :] = jnp.broadcast_to(tail[None], (patch_ref.shape[0],) + tail.shape)

    def embed(position, carry):
        onehot, group = char_parts(chars_ref, position, block)
        looked = nn_dot(table_ref[...], onehot)
        row = looked[:depth]
        for index in range(1, groups):
            row = jnp.where(group == index, looked[index * depth : (index + 1) * depth], row)
        row = row.astype(jnp.bfloat16)
        embed_ref[pl.ds(pl.multiple_of(position * depth, depth), depth), :] = row
        for tap in range(KW):
            patch_ref[position + lead - tap, tap * depth : (tap + 1) * depth, :] = row
        return carry

    lax.fori_loop(0, letters, embed, 0, unroll=5)
    chunk = grid_ref.shape[1]
    always = letters - KW + 1
    for start in range(0, filters, chunk):
        weight = weight_ref[start : start + chunk, :]
        limit = limit_ref[start : start + chunk, :]

        def product(position, top):
            grid = nn_dot(weight, patch_ref[position + lead])
            grid_ref[position] = grid
            return jnp.maximum(top, grid)

        top = lax.fori_loop(0, always, product, jnp.full((chunk, block), -1e30, jnp.float32), unroll=11)
        for position in range(always, letters):
            grid = nn_dot(weight, patch_ref[position + lead])
            grid = jnp.where(limit >= position, grid, -1e30)
            grid_ref[position] = grid
            top = jnp.maximum(top, grid)

        def total(position, acc):
            return acc + jnp.exp(grid_ref[position] - top)

        acc = lax.fori_loop(0, letters, total, jnp.zeros((chunk, block), jnp.float32), unroll=10)
        lse = top + jnp.log(acc)
        lse_ref[start : start + chunk, :] = lse
        pooled = lse - count_ref[start : start + chunk, :]
        acts_ref[:, start : start + chunk] = (pooled * normal_cdf(pooled)).astype(jnp.bfloat16).T

def conv_backward(letters, depth, chars_ref, embed_ref, lse_ref, up_ref, weight_ref, back_ref,
                  limit_ref, count_ref, wgrad_ref, tgrad_ref, patch_ref, down_ref, pull_ref):
    block = chars_ref.shape[1]
    filters = weight_ref.shape[0]
    lead = KW - 1
    rows = KW * depth
    groups = tgrad_ref.shape[0] // (2 * depth)
    step = pl.program_id(0)

    @pl.when(step == 0)
    def _():
        wgrad_ref[...] = jnp.zeros(wgrad_ref.shape, jnp.float32)
        tgrad_ref[...] = jnp.zeros(tgrad_ref.shape, jnp.float32)
        patch_ref[letters * depth :, :] = jnp.zeros((patch_ref.shape[0] - letters * depth, block), jnp.bfloat16)

    patch_ref[: letters * depth, :] = embed_ref[...]
    down_ref[...] = jnp.zeros(down_ref.shape, jnp.float32)
    pooled = lse_ref[...] - count_ref[...]
    slope = normal_cdf(pooled) + pooled * (DENSITY * jnp.exp(-0.5 * pooled * pooled))
    pull_ref[...] = slope * up_ref[...].T.astype(jnp.float32)
    ones = jnp.where(lax.broadcasted_iota(jnp.int32, (128 - rows, block), 0) == 0, 1.0, 0.0).astype(jnp.bfloat16)

    def one(position, masked):
        start = position * depth
        if not isinstance(position, int):
            start = pl.multiple_of(start, depth)
        patch = jnp.concatenate([patch_ref[pl.ds(start, rows), :], ones], axis=0)
        grid = nn_dot(weight_ref[...], patch)
        spread = jnp.exp(grid - lse_ref[...]) * pull_ref[...]
        if masked:
            spread = jnp.where(limit_ref[...] >= position, spread, 0.0)
        spread = spread.astype(jnp.bfloat16)
        down = nn_dot(back_ref[...], spread)
        down_ref[pl.ds(start, rows), :] += down[:rows]
        wgrad_ref[...] += nt_dot(spread, patch)

    always = letters - KW + 1

    def body(position, carry):
        one(position, False)
        return carry

    lax.fori_loop(0, always, body, 0, unroll=2)
    for position in range(always, letters):
        one(position, True)

    def table(position, carry):
        onehot, group = char_parts(chars_ref, position, block)
        down = down_ref[pl.ds(pl.multiple_of(position * depth, depth), depth), :]
        high = down.astype(jnp.bfloat16)
        low = (down - high.astype(jnp.float32)).astype(jnp.bfloat16)
        zero = jnp.zeros_like(high)
        parts = [jnp.where(group == index, item, zero) for item in (high, low) for index in range(groups)]
        tgrad_ref[...] += nt_dot(jnp.concatenate(parts, axis=0), onehot)
        return carry

    lax.fori_loop(0, letters, table, 0, unroll=5)

def conv_prep(chars, char_table, conv_weight, conv_bias, widths):
    letters = chars.shape[1]
    vocab, depth = char_table.shape
    groups = -(-vocab // 128)
    table = jnp.pad(char_table, ((0, groups * 128 - vocab), (0, 0)))
    table = table.reshape(groups, 128, depth).transpose(0, 2, 1).reshape(groups * depth, 128)
    tap = jnp.arange(conv_weight.shape[0], dtype=jnp.int32) // depth
    masked = jnp.where(tap[:, None] < widths[None, :], conv_weight, 0)
    back = jnp.concatenate([masked, conv_bias[None, :], jnp.zeros((127 - masked.shape[0], masked.shape[1]), masked.dtype)], axis=0)
    limit = (letters - widths)[:, None].astype(jnp.int32)
    count = jnp.log((letters - widths + 1).astype(jnp.float32))[:, None]
    ids = jnp.pad(chars, ((0, 0), (0, -letters % 8))).T
    return ids, table, back.T, back, limit, count

def conv_forward_call(ids, table, weight, limit, count, letters, depth, block=256):
    words = ids.shape[1]
    filters = weight.shape[0]
    full = lambda a: pl.BlockSpec(a.shape, lambda i: (0,) * a.ndim)
    return pl.pallas_call(
        functools.partial(conv_forward, letters, depth),
        grid=(words // block,),
        in_specs=[pl.BlockSpec((ids.shape[0], block), lambda i: (0, i)), full(table), full(weight), full(limit), full(count)],
        out_specs=[pl.BlockSpec((block, filters), lambda i: (i, 0)), pl.BlockSpec((filters, block), lambda i: (0, i)),
                   pl.BlockSpec((letters * depth, block), lambda i: (0, i))],
        out_shape=[jax.ShapeDtypeStruct((words, filters), jnp.bfloat16), jax.ShapeDtypeStruct((filters, words), jnp.float32),
                   jax.ShapeDtypeStruct((letters * depth, words), jnp.bfloat16)],
        scratch_shapes=[pltpu.VMEM((letters + KW - 1, 128, block), jnp.bfloat16), pltpu.VMEM((letters, 128, block), jnp.float32)],
        compiler_params=pltpu.CompilerParams(vmem_limit_bytes=48 << 20),
        name="conv_forward",
    )(ids, table, weight, limit, count)

def conv_backward_call(ids, embed, lse, up, weight, back, limit, count, groups, letters, depth, block=256):
    words = ids.shape[1]
    filters = weight.shape[0]
    full = lambda a: pl.BlockSpec(a.shape, lambda i: (0,) * a.ndim)
    return pl.pallas_call(
        functools.partial(conv_backward, letters, depth),
        grid=(words // block,),
        in_specs=[pl.BlockSpec((ids.shape[0], block), lambda i: (0, i)), pl.BlockSpec((letters * depth, block), lambda i: (0, i)),
                  pl.BlockSpec((filters, block), lambda i: (0, i)), pl.BlockSpec((block, filters), lambda i: (i, 0)),
                  full(weight), full(back), full(limit), full(count)],
        out_specs=[pl.BlockSpec((filters, 128), lambda i: (0, 0)), pl.BlockSpec((2 * groups * depth, 128), lambda i: (0, 0))],
        out_shape=[jax.ShapeDtypeStruct((filters, 128), jnp.float32), jax.ShapeDtypeStruct((2 * groups * depth, 128), jnp.float32)],
        scratch_shapes=[pltpu.VMEM(((letters + KW - 1) * depth, block), jnp.bfloat16), pltpu.VMEM(((letters + KW - 1) * depth, block), jnp.float32),
                        pltpu.VMEM((filters, block), jnp.float32)],
        compiler_params=pltpu.CompilerParams(vmem_limit_bytes=48 << 20),
        name="conv_backward",
    )(ids, embed, lse, up, weight, back, limit, count)


MESH = pl.DeviceIdType.MESH

def greet(peers):
    barrier = pltpu.get_barrier_semaphore()
    for peer in peers:
        pl.semaphore_signal(barrier, inc=1, device_id=peer, device_id_type=MESH)
    pl.semaphore_wait(barrier, len(peers))

def remote(source, target, send, recv, peer):
    return pltpu.make_async_remote_copy(
        src_ref=source, dst_ref=target, send_sem=send, recv_sem=recv,
        device_id=peer, device_id_type=MESH)

def comm_call(kernel, out_shape, scratch, ident, *args, name):
    vmem = pl.BlockSpec(memory_space=pltpu.VMEM)
    return pl.pallas_call(
        kernel, out_shape=out_shape, in_specs=[vmem] * len(args), out_specs=jax.tree.map(lambda _: vmem, out_shape),
        scratch_shapes=scratch,
        compiler_params=pltpu.CompilerParams(collective_id=ident, has_side_effects=True, vmem_limit_bytes=40 << 20),
        name=name)(*args)

DMA = pltpu.SemaphoreType.DMA

def scatter_sum(part_ref, inbox, send, recv, me):
    copies = []
    for hop in (3, 2, 1):
        copy = remote(part_ref.at[me ^ hop], inbox.at[hop - 1], send.at[hop - 1], recv.at[hop - 1], {"filt": me ^ hop})
        copy.start()
        copies.append(copy)
    total = part_ref[me].astype(jnp.float32)
    for copy, hop in reversed(list(zip(copies, (3, 2, 1)))):
        copy.wait()
        total = total + inbox[hop - 1].astype(jnp.float32)
    return total

def gather_blocks(low, all_ref, send, recv, me):
    all_ref[me] = low
    far = remote(all_ref.at[me], all_ref.at[me], send.at[0], recv.at[0], {"filt": me ^ 2})
    near = remote(all_ref.at[me], all_ref.at[me], send.at[1], recv.at[1], {"filt": me ^ 1})
    far.start()
    near.start()
    far.wait_recv()
    relay = remote(all_ref.at[me ^ 2], all_ref.at[me ^ 2], send.at[2], recv.at[2], {"filt": me ^ 1})
    relay.start()
    far.wait_send()
    near.wait()
    relay.wait()

def norm(values, gain, shift, eps):
    center = values - jnp.mean(values, axis=-1, keepdims=True)
    scale = lax.rsqrt(jnp.mean(center * center, axis=-1, keepdims=True) + eps)
    unit = center * scale
    return unit * gain + shift, unit, scale

def norm_back(upstream, unit, scale, gain):
    lifted = upstream * gain
    drop = jnp.mean(lifted, axis=-1, keepdims=True)
    lean = jnp.mean(lifted * unit, axis=-1, keepdims=True)
    return scale * (lifted - drop - unit * lean)

def forward_stage(part_ref, base_ref, gain_ref, shift_ref, value_ref, unit_ref, scale_ref, all_ref, inbox, send, recv, eps):
    me = lax.axis_index("filt")
    greet([{"filt": me ^ hop} for hop in (1, 2, 3)])
    total = scatter_sum(part_ref, inbox, send, recv, me) + base_ref[...]
    value, unit, scale = norm(total, gain_ref[...], shift_ref[...], eps)
    value_ref[...] = value
    unit_ref[...] = unit
    scale_ref[...] = scale
    gather_blocks(value.astype(jnp.bfloat16), all_ref, send.at[pl.ds(3, 3)], recv.at[pl.ds(3, 3)], me)

def top_stage(part_ref, base_ref, up_ref, gain_ref, shift_ref, top_ref, down_ref, dgain_ref, dshift_ref, all_ref, inbox, send, recv, eps):
    me = lax.axis_index("filt")
    greet([{"filt": me ^ hop} for hop in (1, 2, 3)])
    total = scatter_sum(part_ref, inbox, send, recv, me) + base_ref[...]
    top, unit, scale = norm(total, gain_ref[...], shift_ref[...], eps)
    top_ref[...] = top.astype(jnp.bfloat16)
    up = up_ref[...].astype(jnp.float32)
    dgain_ref[...] = jnp.sum(up * unit, axis=0, keepdims=True)
    dshift_ref[...] = jnp.sum(up, axis=0, keepdims=True)
    down = norm_back(up, unit, scale, gain_ref[...])
    down_ref[...] = down
    gather_blocks(down.astype(jnp.bfloat16), all_ref, send.at[pl.ds(3, 3)], recv.at[pl.ds(3, 3)], me)

def backward_stage(kind, part_ref, base_ref, unit_ref, scale_ref, gain_ref, *refs):
    job_in, job_out, job_send, job_recv = None, None, None, None
    if kind is not None:
        (job_in, down_ref, dgain_ref, dshift_ref, dlow_ref, all_ref, job_out, inbox, send, recv, job_send, job_recv) = refs
    else:
        (down_ref, dgain_ref, dshift_ref, dlow_ref, all_ref, inbox, send, recv) = refs
    me = lax.axis_index("filt")
    slot = lax.axis_index("dp")
    others = [] if kind is None else [{"dp": slot ^ hop} for hop in job_hops(kind)]
    greet([{"filt": me ^ hop} for hop in (1, 2, 3)] + others)
    copies = [] if kind is None else start_job(kind, job_in, job_out, job_send, job_recv)
    up = scatter_sum(part_ref, inbox, send, recv, me) + base_ref[...]
    unit = unit_ref[...]
    dgain_ref[...] = jnp.sum(up * unit, axis=0, keepdims=True)
    dshift_ref[...] = jnp.sum(up, axis=0, keepdims=True)
    down = norm_back(up, unit, scale_ref[...], gain_ref[...])
    down_ref[...] = down
    low = down.astype(jnp.bfloat16)
    dlow_ref[...] = jnp.sum(low.astype(jnp.float32), axis=0, keepdims=True)
    gather_blocks(low, all_ref, send.at[pl.ds(3, 3)], recv.at[pl.ds(3, 3)], me)
    for copy in copies:
        copy.wait()

def start_job(kind, source, target, send, recv):
    slot = lax.axis_index("dp")
    ring, side = slot // 2, slot % 2
    if kind == "side":
        moves = [(source.at[:, 1 - side], target, 1)]
    else:
        moves = [(source.at[ring ^ hop], target.at[hop - 1], 2 * hop) for hop in (2, 3, 1)]
    copies = []
    for index, (piece, place, hop) in enumerate(moves):
        copy = remote(piece, place, send.at[index], recv.at[index], {"dp": slot ^ hop})
        copy.start()
        copies.append(copy)
    return copies

def job_hops(kind):
    return (1,) if kind == "side" else (2, 4, 6)

def stage_scratch(block):
    return [pltpu.VMEM((3,) + block, jnp.bfloat16), DMA((6,)), DMA((6,))]

def f32(*shape): return jax.ShapeDtypeStruct(shape, jnp.float32)
def bf16(*shape): return jax.ShapeDtypeStruct(shape, jnp.bfloat16)

def forward_stage_call(part, base, gain, shift, eps, ident):
    parts, rows, cols = part.shape
    return comm_call(functools.partial(forward_stage, eps=eps),
        (f32(rows, cols), f32(rows, cols), f32(rows, 1), bf16(parts, rows, cols)), stage_scratch((rows, cols)), ident,
        part, base, gain, shift, name="forward_stage")

def top_stage_call(part, base, up, gain, shift, eps, ident):
    parts, rows, cols = part.shape
    return comm_call(functools.partial(top_stage, eps=eps),
        (bf16(rows, cols), f32(rows, cols), f32(1, cols), f32(1, cols), bf16(parts, rows, cols)), stage_scratch((rows, cols)), ident,
        part, base, up, gain, shift, name="top_stage")

def backward_stage_call(part, base, unit, scale, gain, ident, kind=None, job=None):
    parts, rows, cols = part.shape
    vmem = pl.BlockSpec(memory_space=pltpu.VMEM)
    hbm = pl.BlockSpec(memory_space=pl.ANY)
    args = (part, base, unit, scale, gain)
    out_shape = [f32(rows, cols), f32(1, cols), f32(1, cols), f32(1, cols), bf16(parts, rows, cols)]
    in_specs, out_specs, scratch = [vmem] * 5, [vmem] * 5, stage_scratch((rows, cols))
    if kind is not None:
        ring = job.shape[0]
        args += (job,)
        in_specs.append(hbm)
        out_specs.append(hbm)
        out_shape.append(bf16(ring, *job.shape[2:]) if kind == "side" else bf16(ring - 1, *job.shape[1:]))
        scratch += [DMA((3,)), DMA((3,))]
    return pl.pallas_call(
        functools.partial(backward_stage, kind), out_shape=out_shape, in_specs=in_specs, out_specs=out_specs,
        scratch_shapes=scratch,
        compiler_params=pltpu.CompilerParams(collective_id=ident, has_side_effects=True, vmem_limit_bytes=24 << 20),
        name="backward_stage")(*args)

def gather_channels(own_ref, all_ref, send, recv, *, chunks):
    me = lax.axis_index("filt")
    greet([{"filt": me ^ hop} for hop in (1, 2)])
    rows, cols = own_ref.shape
    size = rows // chunks

    def lanes(index):
        return pl.ds(pl.multiple_of(index * cols, cols), cols)

    far, near, relay = [], [], []
    for chunk in range(chunks):
        span = pl.ds(chunk * size, size)
        copy = remote(own_ref.at[span, :], all_ref.at[span, lanes(me)], send.at[0, chunk], recv.at[0, chunk], {"filt": me ^ 2})
        copy.start()
        far.append(copy)
    for chunk in range(chunks):
        span = pl.ds(chunk * size, size)
        copy = remote(own_ref.at[span, :], all_ref.at[span, lanes(me)], send.at[1, chunk], recv.at[1, chunk], {"filt": me ^ 1})
        copy.start()
        near.append(copy)
    all_ref[:, lanes(me)] = own_ref[...]
    for chunk in range(chunks):
        span = pl.ds(chunk * size, size)
        far[chunk].wait_recv()
        piece = all_ref.at[span, lanes(me ^ 2)]
        copy = remote(piece, piece, send.at[2, chunk], recv.at[2, chunk], {"filt": me ^ 1})
        copy.start()
        relay.append(copy)
    for chunk in range(chunks):
        far[chunk].wait_send()
        near[chunk].wait()
        relay[chunk].wait()

def gather_channels_call(own, parts, ident, chunks=4):
    rows, cols = own.shape
    return comm_call(functools.partial(gather_channels, chunks=chunks), bf16(rows, cols * parts),
        [DMA((3, chunks)), DMA((3, chunks))], ident, own, name="gather_channels")

def scatter_channels(part_ref, base_ref, out_ref, inbox, merged, send, recv, *, chunks):
    me = lax.axis_index("filt")
    greet([{"filt": me ^ hop} for hop in (1, 2)])
    rows, cols = base_ref.shape
    size = rows // chunks

    def lanes(index):
        return pl.ds(pl.multiple_of(index * cols, cols), cols)

    def hop(source, slot, chunk, peer):
        span = pl.ds(chunk * size, size)
        copy = remote(source, inbox.at[slot, span, :], send.at[slot, chunk], recv.at[slot, chunk], {"filt": peer})
        copy.start()
        return copy

    first, second, third = [], [], []
    for chunk in range(chunks):
        span = pl.ds(chunk * size, size)
        first.append(hop(part_ref.at[span, lanes(me ^ 3)], 0, chunk, me ^ 1))
    for chunk in range(chunks):
        span = pl.ds(chunk * size, size)
        second.append(hop(part_ref.at[span, lanes(me ^ 1)], 1, chunk, me ^ 1))
    for chunk in range(chunks):
        span = pl.ds(chunk * size, size)
        first[chunk].wait_recv()
        both = part_ref[span, lanes(me ^ 2)].astype(jnp.float32) + inbox[0, span, :].astype(jnp.float32)
        merged[span, :] = both.astype(jnp.bfloat16)
        third.append(hop(merged.at[span, :], 2, chunk, me ^ 2))
    for chunk in range(chunks):
        span = pl.ds(chunk * size, size)
        second[chunk].wait_recv()
        third[chunk].wait_recv()
        total = part_ref[span, lanes(me)].astype(jnp.float32) + inbox[1, span, :].astype(jnp.float32)
        total = total + inbox[2, span, :].astype(jnp.float32) + base_ref[span, :]
        out_ref[span, :] = total.astype(jnp.bfloat16)
    for copy in first + second + third:
        copy.wait_send()

def scatter_channels_call(part, base, ident, chunks=4):
    rows, cols = base.shape
    return comm_call(functools.partial(scatter_channels, chunks=chunks), bf16(rows, cols),
        [pltpu.VMEM((3, rows, cols), jnp.bfloat16), pltpu.VMEM((rows, cols), jnp.bfloat16), DMA((3, chunks)), DMA((3, chunks))],
        ident, part, base, name="scatter_channels")

def total_all(rows_ref, table_ref, rows_out, table_out, inbox, tbox, sbox, low, tlow, tsum, send, recv):
    count = lax.axis_size("dp")
    slot = lax.axis_index("dp")
    me = lax.axis_index("filt")
    size = rows_out.shape[1]
    tsize = table_out.shape[1]
    low[...] = rows_ref[...].astype(jnp.bfloat16)
    tlow[...] = table_ref[...].astype(jnp.bfloat16)
    greet([{"dp": slot ^ hop} for hop in range(1, count)] + [{"filt": me ^ hop} for hop in (1, 2, 3)])
    copies = []
    for hop in range(1, count):
        peer = {"dp": slot ^ hop}
        copy = remote(low.at[slot ^ hop], inbox.at[hop - 1], send.at[0, hop - 1], recv.at[0, hop - 1], peer)
        copy.start()
        also = remote(tlow.at[slot ^ hop], tbox.at[hop - 1], send.at[1, hop - 1], recv.at[1, hop - 1], peer)
        also.start()
        copies += [copy, also]
    total = rows_ref[slot]
    part = table_ref[slot]
    for hop in range(1, count):
        copies[2 * hop - 2].wait()
        copies[2 * hop - 1].wait()
        total = total + inbox[hop - 1].astype(jnp.float32)
        part = part + tbox[hop - 1].astype(jnp.float32)
    rows_out[slot] = total.astype(jnp.bfloat16)
    tsum[...] = part.astype(jnp.bfloat16)
    sides = []
    for hop in (1, 2, 3):
        copy = remote(tsum, sbox.at[hop - 1], send.at[2, hop - 1], recv.at[2, hop - 1], {"filt": me ^ hop})
        copy.start()
        sides.append(copy)
    outs = []
    for hop in range(1, count):
        copy = remote(rows_out.at[slot], rows_out.at[slot], send.at[3, hop - 1], recv.at[3, hop - 1], {"dp": slot ^ hop})
        copy.start()
        outs.append(copy)
    for hop in (1, 2, 3):
        sides[hop - 1].wait()
    ordered = tsum[...].astype(jnp.float32)
    near = sbox[0].astype(jnp.float32)
    ordered = (ordered + near) + (sbox[1].astype(jnp.float32) + sbox[2].astype(jnp.float32))
    table_out[slot] = ordered.astype(jnp.bfloat16)
    for hop in range(1, count):
        copy = remote(table_out.at[slot], table_out.at[slot], send.at[4, hop - 1], recv.at[4, hop - 1], {"dp": slot ^ hop})
        copy.start()
        outs.append(copy)
    for copy in outs:
        copy.wait()

def total_all_call(rows, table, ident):
    count, size, lanes = rows.shape
    tsize = table.shape[1]
    return comm_call(total_all, (bf16(count, size, lanes), bf16(count, tsize, lanes)),
        [pltpu.VMEM((count - 1, size, lanes), jnp.bfloat16), pltpu.VMEM((count - 1, tsize, lanes), jnp.bfloat16),
         pltpu.VMEM((3, tsize, lanes), jnp.bfloat16), pltpu.VMEM((count, size, lanes), jnp.bfloat16), pltpu.VMEM((count, tsize, lanes), jnp.bfloat16),
         pltpu.VMEM((tsize, lanes), jnp.bfloat16), DMA((5, count - 1)), DMA((5, count - 1))],
        ident, rows, table, name="total_all")


def prologue(letters, depth, block, chunks, window, first, chars_ref, table_ref, weight_ref, limit_ref, count_ref, shard_ref,
             acts_ref, lse_ref, embed_ref, all_ref, full_ref, patch_ref, grid_ref,
             zsend, zrecv, local, ysend, yrecv, fsend, frecv):
    words = chars_ref.shape[1]
    filters = weight_ref.shape[0]
    me = lax.axis_index("filt")
    slot = lax.axis_index("dp")
    ring, side = slot // 2, slot % 2
    greet([{"filt": me ^ hop} for hop in (1, 2)] + [{"dp": slot ^ hop} for hop in (1, 2, 4, 6)])
    parts = all_ref.shape[1] // filters
    span = shard_ref.shape[0] // (chunks // 2)

    def spot(chunk):
        return pl.ds((chunk // 2) * span, span), chunk % 2

    own, far = [], []

    def start_chunk(chunk):
        if chunk >= chunks:
            return
        rows, half = spot(chunk)
        source = shard_ref.at[rows, pl.ds(pl.multiple_of(half * filters * parts + me * filters, filters), filters)]
        target = full_ref.at[half, ring, side, rows, :]
        copy = pltpu.make_async_copy(source, target, local.at[chunk])
        copy.start()
        own.append(copy)
        for hop in (2, 1, 3):
            copy = remote(source, target, zsend.at[chunk, hop - 1], zrecv.at[chunk, hop - 1], {"dp": slot ^ (2 * hop)})
            copy.start()
            far.append(copy)

    for chunk in range(window):
        start_chunk(chunk)
    cross = []

    def forward_chunk(chunk):
        rows, half = spot(chunk)
        own[chunk].wait()
        for copy in far[3 * chunk : 3 * chunk + 3]:
            copy.wait_recv()
        start_chunk(chunk + window)
        piece = full_ref.at[half, :, side, rows, :]
        copy = remote(piece, piece, ysend.at[chunk], yrecv.at[chunk], {"dp": slot ^ 1})
        copy.start()
        cross.append(copy)

    lead = KW - 1
    rows = KW * depth
    groups = table_ref.shape[0] // depth
    patch_ref[:, :rows, :] = jnp.zeros((patch_ref.shape[0], rows, block), jnp.bfloat16)
    ones = lax.broadcasted_iota(jnp.int32, (128 - rows, block), 0) == 0
    tail = jnp.where(ones, 1.0, 0.0).astype(jnp.bfloat16)
    patch_ref[:, rows:, :] = jnp.broadcast_to(tail[None], (patch_ref.shape[0],) + tail.shape)
    chunk = grid_ref.shape[1]
    always = letters - KW + 1
    steps = filters // chunk
    polls = {(step // steps, step % steps): step - first for step in range(first, min(first + chunks, words // block * steps))}
    gathers = ChannelGather(acts_ref, all_ref, fsend, frecv, words // block)
    for index in range(words // block):
        cols = pl.ds(index * block, block)

        def embed(position, carry):
            ids = chars_ref[pl.ds(position, 1), cols]
            low = ids & 127
            group = ids >> 7
            onehot = lax.broadcasted_iota(jnp.int32, (128, block), 0) == low
            onehot = jnp.where(onehot, 1.0, 0.0).astype(jnp.bfloat16)
            looked = nn_dot(table_ref[...], onehot)
            row = looked[:depth]
            for part in range(1, groups):
                row = jnp.where(group == part, looked[part * depth : (part + 1) * depth], row)
            row = row.astype(jnp.bfloat16)
            embed_ref[pl.ds(pl.multiple_of(position * depth, depth), depth), cols] = row
            for tap in range(KW):
                patch_ref[position + lead - tap, tap * depth : (tap + 1) * depth, :] = row
            return carry

        lax.fori_loop(0, letters, embed, 0, unroll=5)
        for start in range(0, filters, chunk):
            weight = weight_ref[start : start + chunk, :]
            limit = limit_ref[start : start + chunk, :]

            def product(position, top):
                grid = nn_dot(weight, patch_ref[position + lead])
                grid_ref[position] = grid
                return jnp.maximum(top, grid)

            top = lax.fori_loop(0, always, product, jnp.full((chunk, block), -1e30, jnp.float32), unroll=11)
            for position in range(always, letters):
                grid = nn_dot(weight, patch_ref[position + lead])
                grid = jnp.where(limit >= position, grid, -1e30)
                grid_ref[position] = grid
                top = jnp.maximum(top, grid)

            def total(position, acc):
                return acc + jnp.exp(grid_ref[position] - top)

            acc = lax.fori_loop(0, letters, total, jnp.zeros((chunk, block), jnp.float32), unroll=10)
            lse = top + jnp.log(acc)
            lse_ref[start : start + chunk, cols] = lse
            pooled = lse - count_ref[start : start + chunk, :]
            acts_ref[cols, start : start + chunk] = (pooled * normal_cdf(pooled)).astype(jnp.bfloat16).T
            poll = polls.get((index, start // chunk))
            if poll is not None:
                forward_chunk(poll)
        gathers.send(index)
    for index in range(len(polls), chunks):
        forward_chunk(index)
    for index in range(words // block):
        gathers.relay(index)
    gathers.finish()
    for copy in far:
        copy.wait_send()
    for copy in cross:
        copy.wait()

class ChannelGather:
    def __init__(self, own_ref, all_ref, send, recv, pieces):
        self.me = lax.axis_index("filt")
        self.own, self.all, self.sems = own_ref, all_ref, (send, recv)
        self.size = own_ref.shape[0] // pieces
        self.copies = []

    def view(self, index, piece):
        cols = self.own.shape[1]
        return self.all.at[pl.ds(piece * self.size, self.size), pl.ds(pl.multiple_of(index * cols, cols), cols)]

    def push(self, source, target, kind, piece, hop):
        send, recv = self.sems
        copy = remote(source, target, send.at[kind, piece], recv.at[kind, piece], {"filt": self.me ^ hop})
        copy.start()
        self.copies.append(copy)
        return copy

    def send(self, piece):
        source = self.own.at[pl.ds(piece * self.size, self.size), :]
        target = self.view(self.me, piece)
        self.push(source, target, 0, piece, 2)
        self.push(source, target, 1, piece, 1)
        cols = self.own.shape[1]
        self.all[pl.ds(piece * self.size, self.size), pl.ds(pl.multiple_of(self.me * cols, cols), cols)] = self.own[pl.ds(piece * self.size, self.size), :]

    def relay(self, piece):
        self.copies[2 * piece].wait_recv()
        view = self.view(self.me ^ 2, piece)
        self.push(view, view, 2, piece, 1)

    def finish(self):
        for index, copy in enumerate(self.copies):
            copy.wait_send()
            if index % 2 == 1 or index >= 2 * (len(self.copies) // 3):
                copy.wait_recv()

def prologue_call(ids, table, weight, limit, count, shard, parts, letters, depth, ident, block=256, chunks=8, window=2, first=2):
    words = ids.shape[1]
    filters = weight.shape[0]
    rows = shard.shape[0]
    vmem = pl.BlockSpec(memory_space=pltpu.VMEM)
    hbm = pl.BlockSpec(memory_space=pl.ANY)
    pieces = words // block
    return pl.pallas_call(
        functools.partial(prologue, letters, depth, block, chunks, window, first),
        in_specs=[vmem] * 5 + [hbm],
        out_specs=[vmem] * 4 + [hbm],
        out_shape=[bf16(words, filters), f32(filters, words), bf16(letters * depth, words), bf16(words, filters * parts),
                   bf16(2, 4, 2, rows, filters)],
        scratch_shapes=[pltpu.VMEM((letters + KW - 1, 128, block), jnp.bfloat16), pltpu.VMEM((letters, 128, block), jnp.float32),
                        DMA((chunks, 3)), DMA((chunks, 3)), DMA((chunks,)), DMA((chunks,)), DMA((chunks,)), DMA((3, pieces)), DMA((3, pieces))],
        compiler_params=pltpu.CompilerParams(collective_id=ident, has_side_effects=True, vmem_limit_bytes=48 << 20),
        name="prologue",
    )(ids, table, weight, limit, count, shard)


class RowReduce:
    def __init__(self, grad, yin, pair, zin, joined, span, sems):
        self.grad, self.yin, self.pair, self.zin, self.joined = grad, yin, pair, zin, joined
        self.span, self.sems = span, sems
        self.me, self.slot = lax.axis_index("filt"), lax.axis_index("dp")
        self.ring, self.side = self.slot // 2, self.slot % 2
        self.copies = []

    def push(self, source, target, index, peer):
        send, recv = self.sems
        copy = remote(source, target, send.at[index], recv.at[index], peer)
        copy.start()
        self.copies.append(copy)
        return copy

    def across(self):
        span = self.span
        self.first = self.push(
            self.grad.at[:, 1 - self.side, span, :], self.yin.at[:, span, :], 0, {"dp": self.slot ^ 1}
        )

    def along(self):
        span = self.span
        self.first.wait_recv()
        both = self.grad[:, self.side, span, :].astype(jnp.float32) + self.yin[:, span, :].astype(jnp.float32)
        self.pair[:, span, :] = both.astype(jnp.bfloat16)
        self.rest = [
            self.push(self.pair.at[self.ring ^ hop, span, :], self.zin.at[hop - 1, span, :], hop, {"dp": self.slot ^ (2 * hop)})
            for hop in (2, 3, 1)
        ]

    def join(self):
        span = self.span
        for copy in self.rest:
            copy.wait_recv()
        total = self.pair[self.ring, span, :].astype(jnp.float32)
        for hop in (1, 2, 3):
            total = total + self.zin[hop - 1, span, :].astype(jnp.float32)
        self.joined[self.me, span, :] = total.astype(jnp.bfloat16)
        self.share()

    def share(self):
        piece = self.joined.at[self.me, self.span, :]
        self.far = self.push(piece, piece, 4, {"filt": self.me ^ 2})
        self.near = self.push(piece, piece, 5, {"filt": self.me ^ 1})

    def relay(self):
        self.far.wait_recv()
        piece = self.joined.at[self.me ^ 2, self.span, :]
        self.last = self.push(piece, piece, 6, {"filt": self.me ^ 1})

    def finish(self):
        self.near.wait_recv()
        self.last.wait_recv()
        for copy in self.copies:
            copy.wait_send()


def epilogue(letters, depth, block, plan, *refs):
    (part_ref, base_ref, chars_ref, embed_ref, lse_ref, weight_ref, back_ref, limit_ref, count_ref, wide_ref, slim_ref, ffn_ref,
     wgrad_ref, tgrad_ref, wide_out, slim_out, ffn_out,
     inbox, merged, up_ref, patch_ref, down_ref, pull_ref, wide_y, wide_p, wide_z, slim_y, slim_p, slim_z,
     csend, crecv, rsend, rrecv) = refs
    me = lax.axis_index("filt")
    slot = lax.axis_index("dp")
    greet([{"filt": me ^ hop} for hop in (1, 2)] + [{"dp": slot ^ hop} for hop in (1, 2, 4, 6)])
    items = []
    slim_rows = slim_out.shape[1] // 2
    wide_rows = wide_out.shape[1] // 4
    for index in range(2):
        items.append(RowReduce(slim_ref, slim_y, slim_p, slim_z, slim_out, pl.ds(index * slim_rows, slim_rows),
                               (rsend.at[index], rrecv.at[index])))
    for index in range(4):
        items.append(RowReduce(wide_ref, wide_y, wide_p, wide_z, wide_out, pl.ds(index * wide_rows, wide_rows),
                               (rsend.at[2 + index], rrecv.at[2 + index])))
    for item in items:
        item.across()
    ffn = RowReduce(None, None, None, None, ffn_out, pl.ds(0, ffn_out.shape[1]), (rsend.at[6], rrecv.at[6]))
    ffn_out[me] = ffn_ref[...]
    scatter = ChannelScatter(part_ref, base_ref, up_ref, inbox, merged, csend, crecv)
    scatter.run()
    ffn.share()
    steps = iter([(ffn, "relay") if code == "F" else (items[int(code[1:])], {"A": "along", "J": "join", "R": "relay"}[code[0]])
                  for code in plan])

    def advance(many):
        for unused in range(many):
            step = next(steps, None)
            if step is not None:
                getattr(*step)()

    filters = weight_ref.shape[0]
    rows = KW * depth
    groups = tgrad_ref.shape[0] // (2 * depth)
    wgrad_ref[...] = jnp.zeros(wgrad_ref.shape, jnp.float32)
    tgrad_ref[...] = jnp.zeros(tgrad_ref.shape, jnp.float32)
    patch_ref[letters * depth :, :] = jnp.zeros((patch_ref.shape[0] - letters * depth, block), jnp.bfloat16)
    ones = jnp.where(lax.broadcasted_iota(jnp.int32, (128 - rows, block), 0) == 0, 1.0, 0.0).astype(jnp.bfloat16)
    always = letters - KW + 1
    quarter = always // 4
    for index in range(chars_ref.shape[1] // block):
        cols = pl.ds(index * block, block)
        patch_ref[: letters * depth, :] = embed_ref[:, cols]
        down_ref[...] = jnp.zeros(down_ref.shape, jnp.float32)
        pooled = lse_ref[:, cols] - count_ref[...]
        slope = normal_cdf(pooled) + pooled * (DENSITY * jnp.exp(-0.5 * pooled * pooled))
        pull_ref[...] = slope * up_ref[cols, :].T.astype(jnp.float32)

        def one(position, masked):
            start = position * depth
            if not isinstance(position, int):
                start = pl.multiple_of(start, depth)
            patch = jnp.concatenate([patch_ref[pl.ds(start, rows), :], ones], axis=0)
            grid = nn_dot(weight_ref[...], patch)
            spread = jnp.exp(grid - lse_ref[:, cols]) * pull_ref[...]
            if masked:
                spread = jnp.where(limit_ref[...] >= position, spread, 0.0)
            spread = spread.astype(jnp.bfloat16)
            down = nn_dot(back_ref[...], spread)
            down_ref[pl.ds(start, rows), :] += down[:rows]
            wgrad_ref[...] += nt_dot(spread, patch)

        def body(position, carry):
            one(position, False)
            return carry

        for lap in range(4):
            stop = always if lap == 3 else (lap + 1) * quarter
            lax.fori_loop(lap * quarter, stop, body, 0)
            advance(2)
        for position in range(always, letters):
            one(position, True)

        def table(position, carry):
            ids = chars_ref[pl.ds(position, 1), cols]
            low = ids & 127
            group = ids >> 7
            onehot = lax.broadcasted_iota(jnp.int32, (128, block), 0) == low
            onehot = jnp.where(onehot, 1.0, 0.0).astype(jnp.bfloat16)
            down = down_ref[pl.ds(pl.multiple_of(position * depth, depth), depth), :]
            high = down.astype(jnp.bfloat16)
            rest = (down - high.astype(jnp.float32)).astype(jnp.bfloat16)
            zero = jnp.zeros_like(high)
            parts = [jnp.where(group == part, item, zero) for item in (high, rest) for part in range(groups)]
            tgrad_ref[...] += nt_dot(jnp.concatenate(parts, axis=0), onehot)
            return carry

        lax.fori_loop(0, letters, table, 0, unroll=5)
        advance(2)
    advance(len(plan))
    ffn.finish()
    for item in items:
        item.finish()


class ChannelScatter:
    def __init__(self, part_ref, base_ref, out_ref, inbox, merged, send, recv):
        self.part, self.base, self.out, self.inbox, self.merged = part_ref, base_ref, out_ref, inbox, merged
        self.sems = (send, recv)
        self.me = lax.axis_index("filt")

    def run(self):
        me = self.me
        rows, cols = self.base.shape
        pieces = self.sems[0].shape[1]
        size = rows // pieces

        def lanes(index):
            return pl.ds(pl.multiple_of(index * cols, cols), cols)

        def hop(source, kind, piece, peer):
            span = pl.ds(piece * size, size)
            send, recv = self.sems
            copy = remote(source, self.inbox.at[kind, span, :], send.at[kind, piece], recv.at[kind, piece], {"filt": peer})
            copy.start()
            return copy

        spans = [pl.ds(piece * size, size) for piece in range(pieces)]
        first = [hop(self.part.at[span, lanes(me ^ 3)], 0, piece, me ^ 1) for piece, span in enumerate(spans)]
        second = [hop(self.part.at[span, lanes(me ^ 1)], 1, piece, me ^ 1) for piece, span in enumerate(spans)]
        third = []
        for piece, span in enumerate(spans):
            first[piece].wait_recv()
            both = self.part[span, lanes(me ^ 2)].astype(jnp.float32) + self.inbox[0, span, :].astype(jnp.float32)
            self.merged[span, :] = both.astype(jnp.bfloat16)
            third.append(hop(self.merged.at[span, :], 2, piece, me ^ 2))
        for piece, span in enumerate(spans):
            second[piece].wait_recv()
            third[piece].wait_recv()
            total = self.part[span, lanes(me)].astype(jnp.float32) + self.inbox[1, span, :].astype(jnp.float32)
            total = total + self.inbox[2, span, :].astype(jnp.float32) + self.base[span, :]
            self.out[span, :] = total.astype(jnp.bfloat16)
        for copy in first + second + third:
            copy.wait_send()


PLAN = ("A0", "F", "A1", "J0", "A2", "J1", "R0", "A3", "J2", "R1", "A4", "J3", "R2", "A5", "J4", "R3", "J5", "R4", "R5")


def epilogue_call(part, base, ids, embed, lse, weight, back, limit, count, wide, slim, ffn, letters, depth, groups, ident, block=256):
    filters, words = lse.shape
    args = (part, base, ids, embed, lse, weight, back, limit, count, wide, slim, ffn)
    parts = part.shape[1] // filters
    pieces = 4
    vmem = pl.BlockSpec(memory_space=pltpu.VMEM)

    def space(shape, dtype=jnp.bfloat16):
        return pltpu.VMEM(shape, dtype)

    def stages(array):
        ring, side, rows, cols = array.shape
        return [space((ring, rows, cols)), space((ring, rows, cols)), space((ring - 1, rows, cols))]

    out_shape = [f32(filters, 128), f32(2 * groups * depth, 128), bf16(parts, *wide.shape[2:]), bf16(parts, *slim.shape[2:]),
                 bf16(parts, *ffn.shape)]
    padded = (letters + KW - 1) * depth
    return pl.pallas_call(
        functools.partial(epilogue, letters, depth, block, PLAN),
        in_specs=[vmem] * len(args),
        out_specs=[vmem] * len(out_shape),
        out_shape=out_shape,
        scratch_shapes=[space((3, words, filters)), space((words, filters)), space((words, filters)), space((padded, block)),
                        space((padded, block), jnp.float32), space((filters, block), jnp.float32)]
        + stages(wide) + stages(slim) + [DMA((3, pieces)), DMA((3, pieces)), DMA((7, 7)), DMA((7, 7))],
        compiler_params=pltpu.CompilerParams(collective_id=ident, has_side_effects=True, vmem_limit_bytes=56 << 20),
        name="epilogue",
    )(*args)


def exact_gaussian_activation(values):
    return jax.nn.gelu(values, approximate=False)


def gelu_back(values, upstream):
    return jax.vjp(exact_gaussian_activation, values)[1](upstream)[0]


def channel_widths(channels):
    widths = jnp.ones_like(channels)
    for power in range(6):
        widths = widths + (channels >= NF * 2**power // 64).astype(jnp.int32)
    return widths


def highway_mix(hidden, gates):
    width = hidden.shape[1]
    carry_gate = jax.nn.sigmoid(gates[:, width:])
    return carry_gate * hidden + (1.0 - carry_gate) * exact_gaussian_activation(gates[:, :width])


def tn_dot(left, right):
    return lax.dot_general(left, right, (((0,), (0,)), ((), ())), preferred_element_type=jnp.float32)


def swap(array, axis, bit):
    size = lax.axis_size(axis)
    return lax.ppermute(array, axis, [(index, index ^ bit) for index in range(size)])


def reduce_rows(array):
    count = lax.axis_size("dp")
    slot = lax.axis_index("dp")
    bits = count.bit_length() - 1
    rows, cols = array.shape
    if count != 1 << bits:
        return lax.psum_scatter(array.astype(jnp.bfloat16), "dp", scatter_dimension=0, tiled=True)
    array = array.reshape((2,) * bits + (rows // count, cols))
    for bit in range(bits):
        axis = bits - 1 - bit
        mine = (slot >> bit) & 1
        keep = lax.dynamic_index_in_dim(array, mine, axis, keepdims=False)
        give = lax.dynamic_index_in_dim(array, 1 - mine, axis, keepdims=False)
        got = swap(give.astype(jnp.bfloat16), "dp", 1 << bit)
        array = (keep.astype(jnp.float32) + got.astype(jnp.float32)).astype(jnp.bfloat16)
    return array


def join_parts(array):
    part = lax.axis_index("filt")
    low = (part & 1) == 1
    high = (part >> 1) == 1
    far = swap(array, "filt", 2)
    near = swap(array, "filt", 1)
    both = swap(far, "filt", 1)
    here = (jnp.where(low, near, array), jnp.where(low, array, near))
    there = (jnp.where(low, both, far), jnp.where(low, far, both))
    first = [jnp.where(high, b, a) for a, b in zip(here, there)]
    second = [jnp.where(high, a, b) for a, b in zip(here, there)]
    return first + second


def per_device(
    chars,
    lengths,
    char_table,
    conv_weight,
    conv_bias,
    highway_weight,
    highway_bias,
    proj_weight,
    proj_bias,
    position,
    norm_gain,
    norm_bias,
    query_key_value_weight,
    attention_output_weight,
    feedforward_input_weight,
    feedforward_input_bias,
    feedforward_output_weight,
    cotangent,
):
    parts = lax.axis_size("filt")
    slices = lax.axis_size("dp")
    part = lax.axis_index("filt")
    slot = lax.axis_index("dp")
    seqs, quarter, dmodel = cotangent.shape
    full_len = chars.shape[1]
    letters = chars.shape[2]
    words = seqs * full_len
    tokens = seqs * quarter
    filters = conv_weight.shape[1]
    depth = char_table.shape[1]
    heads = dmodel // HD // parts
    width = heads * HD
    inner_rows = feedforward_input_weight.shape[0]
    unit_rows = feedforward_output_weight.shape[0] // parts

    def own_columns(array, blocks):
        rows = array.shape[0]
        split = array.reshape(rows, blocks, parts, -1)
        return lax.dynamic_index_in_dim(split, part, 2, keepdims=False).reshape(rows, -1)

    def gather_rows(array):
        return lax.all_gather(array, "dp", axis=0, tiled=True)

    def rows_from_columns(proj_cols, out_cols):
        stack = jnp.concatenate([item.reshape(parts, -1, width) for item in (proj_cols, out_cols)], axis=1)
        stack = lax.all_to_all(stack, "filt", split_axis=0, concat_axis=0, tiled=True)
        whole = stack.transpose(1, 0, 2).reshape(-1, dmodel)
        return whole[: proj_cols.shape[0] // parts], whole[proj_cols.shape[0] // parts :]

    def columns_from_rows(proj_rows, out_rows):
        stack = jnp.concatenate([proj_rows, out_rows], axis=0).astype(jnp.bfloat16)
        stack = stack.reshape(-1, parts, width).transpose(1, 0, 2)
        stack = lax.all_to_all(stack, "filt", split_axis=0, concat_axis=0, tiled=True)
        split = proj_rows.shape[0]
        return stack[:, :split].reshape(-1, width), stack[:, split:].reshape(-1, width)

    fast = slices == 8 and parts == 4
    hb, pb, nd = highway_bias.shape[1], proj_bias.shape[0], norm_gain.shape[1]
    small = jnp.concatenate(
        [
            highway_bias.reshape(-1),
            proj_bias,
            norm_gain.reshape(-1),
            norm_bias.reshape(-1),
            feedforward_input_bias,
        ]
    )
    small_size = small.shape[0]
    small = jnp.pad(small, (0, -small_size % dmodel))
    slim_parts = [
        item.reshape(-1, dmodel)
        for item in (
            own_columns(query_key_value_weight, 3),
            own_columns(proj_weight, 1),
            own_columns(attention_output_weight, 1),
            small,
        )
    ]
    slim_cuts = [slim_parts[0].shape[0]]
    for item in slim_parts[1:3]:
        slim_cuts.append(slim_cuts[-1] + item.shape[0])
    slim_all = lax.all_gather(jnp.concatenate(slim_parts, axis=0), "dp", axis=0, tiled=False)
    qkv_own, proj_cols, out_cols, small = jnp.split(slim_all, slim_cuts, axis=1)
    qkv_own = qkv_own.reshape(dmodel, 3 * width)
    proj_own, out_own = rows_from_columns(proj_cols.reshape(-1, width), out_cols.reshape(-1, width))
    small = small.reshape(slices, -1)[:, :small_size].astype(jnp.float32)
    cuts = [hb, hb + pb, hb + pb + 3 * nd, hb + pb + 6 * nd]
    highway_b, proj_b, gain, shift, inner_b = jnp.split(small, cuts, axis=1)
    highway_b_own = own_columns(highway_b.reshape(1, -1), 2)
    proj_b = proj_b.reshape(-1)
    gain = gain.reshape(slices, 3, nd).transpose(1, 0, 2).reshape(3, dmodel)
    shift = shift.reshape(slices, 3, nd).transpose(1, 0, 2).reshape(3, dmodel)
    inner_b_own = own_columns(inner_b.reshape(1, -1), slices)
    ffn_own = jnp.concatenate(
        [
            own_columns(feedforward_input_weight, slices),
            lax.dynamic_slice_in_dim(feedforward_output_weight, part * unit_rows, unit_rows, 0),
        ],
        axis=0,
    )

    def blocks_of(array):
        return array.astype(jnp.bfloat16).reshape(parts, tokens, -1)

    widths = channel_widths(part * filters + jnp.arange(filters, dtype=jnp.int32))
    ids, table, weight, back, limit, count = conv_prep(
        chars.reshape(words, letters), char_table, conv_weight, conv_bias, widths
    )
    if fast:
        acts, lse, embed, features, highway_own = prologue_call(
            ids, table, weight, limit, count, highway_weight[0], parts, letters, depth, 0
        )
        highway_own = highway_own.reshape(2, -1, filters)
        gates = jnp.concatenate([nn_dot(features, item) for item in highway_own], axis=1) + highway_b_own
    else:
        acts, lse, embed = conv_forward_call(ids, table, weight, limit, count, letters, depth)
        features = gather_channels_call(acts, parts, 0)
        highway_own = gather_rows(own_columns(highway_weight[0], 2))
        gates = nn_dot(features, highway_own) + highway_b_own
    ffn_own, features = lax.optimization_barrier((ffn_own, features))
    ffn_all = lax.all_gather(ffn_own, "dp", axis=0, tiled=False)
    inner_own = ffn_all[:, : inner_rows].reshape(dmodel, -1)
    outer_own = ffn_all[:, inner_rows :].reshape(-1, dmodel)
    feature_own = acts.astype(jnp.float32)
    hidden_low = highway_mix(feature_own, gates).astype(jnp.bfloat16)
    base = position.astype(jnp.float32) + proj_b[None, :]
    first, unit_zero, scale_zero, first_all = forward_stage_call(
        blocks_of(nn_dot(hidden_low, proj_own)), base, gain[0:1], shift[0:1], EPS, 1
    )
    first_all = first_all.reshape(words, dmodel)
    packed = nn_dot(first_all, qkv_own).astype(jnp.bfloat16)
    queries, keys, values = (
        packed[:, block * width : (block + 1) * width].reshape(seqs, full_len, heads, HD)
        for block in range(3)
    )
    key_ok = jnp.arange(full_len, dtype=jnp.int32)[None, :] < lengths[:, None]
    scale = HD ** (-0.5)
    scores = (
        jnp.einsum("sqhd,skhd->shqk", queries, keys, preferred_element_type=jnp.float32) * scale
    )
    scores = jnp.where(key_ok[:, None, None, :], scores, -1e30)
    row_top = jnp.max(scores, axis=-1, keepdims=True)
    log_total = row_top + jnp.log(jnp.sum(jnp.exp(scores - row_top), axis=-1, keepdims=True))
    probs = jnp.exp(scores - log_total)
    probs_low = probs.astype(jnp.bfloat16)
    attended = (
        jnp.einsum("shqk,skhd->sqhd", probs_low, values, preferred_element_type=jnp.float32)
        .astype(jnp.bfloat16)
        .reshape(words, width)
    )
    second, unit_one, scale_one, second_all = forward_stage_call(
        blocks_of(nn_dot(attended, out_own)), first, gain[1:2], shift[1:2], EPS, 2
    )
    second_all = second_all.reshape(words, dmodel)
    inner = nn_dot(second_all, inner_own) + inner_b_own
    active = exact_gaussian_activation(inner).astype(jnp.bfloat16)
    top, d_res_two, d_gain_two, d_shift_two, d_outer = top_stage_call(
        blocks_of(nn_dot(active, outer_own)),
        second,
        cotangent.reshape(tokens, dmodel),
        gain[2:3],
        shift[2:3],
        EPS,
        3,
    )
    encoded = top.reshape(seqs, quarter, dmodel)
    d_outer = d_outer.reshape(words, dmodel)
    grad_outer = tn_dot(active, d_outer)
    d_active = nt_dot(d_outer, outer_own)
    d_inner = gelu_back(inner, d_active).astype(jnp.bfloat16)
    grad_inner = tn_dot(second_all, d_inner)
    grad_ffn = jnp.concatenate(
        [item.astype(jnp.bfloat16).reshape(slices, -1, dmodel) for item in (grad_inner, grad_outer)], axis=1
    )
    kinds = ("side", "ring") if fast else (None, None)
    if fast:
        grad_ffn = grad_ffn.reshape(4, 2, -1, dmodel)
    grad_inner_b = jnp.sum(d_inner.astype(jnp.float32), axis=0)
    d_res_one, d_gain_one, d_shift_one, unused_sum, d_mixed, *got = backward_stage_call(
        blocks_of(nt_dot(d_inner, inner_own)), d_res_two, unit_one, scale_one, gain[1:2], 4, kinds[0], grad_ffn
    )
    if fast:
        keep = lax.dynamic_index_in_dim(grad_ffn, slot % 2, 1, keepdims=False)
        grad_ffn = (keep.astype(jnp.float32) + got[0].astype(jnp.float32)).astype(jnp.bfloat16)
    d_mixed = d_mixed.reshape(words, dmodel)
    grad_out = tn_dot(attended, d_mixed)
    d_attended = nt_dot(d_mixed, out_own).astype(jnp.bfloat16)
    d_attended = d_attended.reshape(seqs, full_len, heads, HD)
    d_values = jnp.einsum(
        "shqk,sqhd->skhd", probs_low, d_attended, preferred_element_type=jnp.float32
    )
    d_probs = jnp.einsum(
        "sqhd,skhd->shqk", d_attended, values, preferred_element_type=jnp.float32
    )
    row_inner = jnp.sum(d_probs * probs, axis=-1, keepdims=True)
    d_scores = (probs * (d_probs - row_inner)).astype(jnp.bfloat16)
    d_queries = (
        jnp.einsum("shqk,skhd->sqhd", d_scores, keys, preferred_element_type=jnp.float32) * scale
    )
    d_keys = (
        jnp.einsum("shqk,sqhd->skhd", d_scores, queries, preferred_element_type=jnp.float32) * scale
    )
    d_packed = jnp.concatenate(
        [item.reshape(words, width) for item in (d_queries, d_keys, d_values)], axis=1
    ).astype(jnp.bfloat16)
    grad_qkv = tn_dot(first_all, d_packed)
    d_summed, d_gain_zero, d_shift_zero, grad_proj_b, d_projected, *got = backward_stage_call(
        blocks_of(nt_dot(d_packed, qkv_own)), d_res_one, unit_zero, scale_zero, gain[0:1], 5, kinds[1], grad_ffn
    )
    if fast:
        keep = lax.dynamic_index_in_dim(grad_ffn, slot // 2, 0, keepdims=False)
        grad_ffn = sum([item.astype(jnp.float32) for item in got[0]], keep.astype(jnp.float32))
        grad_ffn = grad_ffn.astype(jnp.bfloat16)
    grad_pos = jnp.sum(d_summed.reshape(seqs, quarter, dmodel), axis=0)
    d_projected = d_projected.reshape(words, dmodel)
    grad_proj = tn_dot(hidden_low, d_projected)
    grad_slim = jnp.concatenate(
        [
            item.astype(jnp.bfloat16).reshape(slices, -1, dmodel)
            for item in (grad_qkv, *columns_from_rows(grad_proj, grad_out))
        ],
        axis=1,
    )
    d_hidden = nt_dot(d_projected, proj_own)
    d_in, d_gates = jax.vjp(highway_mix, feature_own, gates)[1](d_hidden)
    d_gates = d_gates.astype(jnp.bfloat16)
    grad_highway = tn_dot(features, d_gates).astype(jnp.bfloat16)
    grad_highway_b = jnp.sum(d_gates.astype(jnp.float32), axis=0)
    if fast:
        d_partial = nt_dot(d_gates[:, :filters], highway_own[0]) + nt_dot(d_gates[:, filters:], highway_own[1])
    else:
        d_partial = nt_dot(d_gates, highway_own)
    d_partial = d_partial.astype(jnp.bfloat16)
    groups = table.shape[0] // depth
    if fast:
        conv_sums, table_sums, wide_all, slim_all, ffn_all = epilogue_call(
            d_partial,
            d_in,
            ids,
            embed,
            lse,
            weight,
            back,
            limit,
            count,
            grad_highway.reshape(4, 2, -1, 2 * filters),
            grad_slim.reshape(4, 2, -1, dmodel),
            grad_ffn,
            letters,
            depth,
            groups,
            6,
        )
    else:
        d_features = scatter_channels_call(d_partial, d_in, 6)
        conv_sums, table_sums = conv_backward_call(
            ids, embed, lse, d_features, weight, back, limit, count, groups, letters, depth
        )
        wide_all = jnp.stack(join_parts(reduce_rows(grad_highway)))
        slim_all = jnp.stack(join_parts(reduce_rows(grad_slim.reshape(-1, dmodel))))
        ffn_all = jnp.stack(join_parts(reduce_rows(grad_ffn.reshape(-1, dmodel))))
    table_sums = table_sums.reshape(2, groups * depth, -1).sum(0)

    def place_columns(own, blocks):
        piece = own.reshape(blocks, 1, -1)
        whole = jnp.zeros((blocks, parts, piece.shape[2]), own.dtype)
        return lax.dynamic_update_slice_in_dim(whole, piece, part, 1).reshape(-1)

    d_gain = jnp.concatenate([d_gain_zero, d_gain_one, d_gain_two])
    d_shift = jnp.concatenate([d_shift_zero, d_shift_one, d_shift_two])
    pieces = [
        place_columns(grad_highway_b, 2).reshape(slices, -1),
        grad_proj_b.reshape(slices, -1),
        d_gain.reshape(3, slices, nd).transpose(1, 0, 2).reshape(slices, -1),
        d_shift.reshape(3, slices, nd).transpose(1, 0, 2).reshape(slices, -1),
        place_columns(grad_inner_b, slices).reshape(slices, -1),
    ]
    rows = jnp.concatenate(pieces, axis=1)
    if fast:
        table_rows = -(-table_sums.shape[0] // slices)
        table_rows = -(-table_rows // 8) * 8
        padded = jnp.pad(table_sums, ((0, table_rows * slices - table_sums.shape[0]), (0, 0)))
        small_rows = -(-rows.shape[1] // 1024) * 8
        packed_rows = jnp.pad(rows, ((0, 0), (0, small_rows * 128 - rows.shape[1])))
        few = jnp.concatenate(
            [padded.reshape(slices, table_rows, 128), packed_rows.reshape(slices, small_rows, 128)], axis=1
        )
        conv_rows = filters // slices
        many = jnp.concatenate(
            [conv_sums.reshape(slices, conv_rows, 128), grad_pos.reshape(slices, -1, 128)], axis=1
        )
        many, few = total_all_call(many, few, 7)
        conv_all = many[:, :conv_rows].reshape(filters, 128).astype(jnp.float32)
        grad_pos = many[:, conv_rows:].reshape(grad_pos.shape).astype(jnp.float32)
        table_all = few[:, :table_rows].reshape(-1, 128)[: table_sums.shape[0]].astype(jnp.float32)
        own = lax.dynamic_index_in_dim(few[:, table_rows:].reshape(slices, -1), slot, 0, keepdims=False)
        own = own[: rows.shape[1]].astype(jnp.float32)
    else:
        conv_all = lax.psum(conv_sums, "dp")
        table_all, sums = lax.psum((table_sums, rows), ("dp", "filt"))
        grad_pos = lax.psum(grad_pos, "dp")
        own = lax.dynamic_index_in_dim(sums, slot, 0, keepdims=False)
    tap_rows = conv_weight.shape[0]
    tap_keep = (jnp.arange(tap_rows, dtype=jnp.int32) // depth)[:, None] < widths[None, :]
    conv_grad_w = jnp.where(tap_keep, conv_all[:, :tap_rows].T, 0.0)
    conv_grad_b = conv_all[:, tap_rows]
    g_table = table_all.reshape(groups, depth, 128).transpose(0, 2, 1).reshape(-1, depth)
    g_table = g_table[: char_table.shape[0]]

    g_highway_b, g_proj_b, g_gain, g_shift, g_inner_b = jnp.split(own, cuts)

    def join_columns(array, blocks, rows_here):
        split = array.reshape(parts, rows_here, blocks, -1).transpose(1, 2, 0, 3)
        return split.reshape(rows_here, -1).astype(jnp.float32)

    g_outer = ffn_all[:, inner_rows:].reshape(-1, dmodel).astype(jnp.float32)
    g_inner = join_columns(ffn_all[:, :inner_rows], slices, inner_rows)
    slim_list = jnp.split(slim_all, slim_cuts[:2], axis=1)
    g_qkv = join_columns(slim_list[0], 3, query_key_value_weight.shape[0])
    g_proj = join_columns(slim_list[1], 1, proj_weight.shape[0])
    g_out = join_columns(slim_list[2], 1, attention_output_weight.shape[0])
    g_highway = join_columns(wide_all, 2, highway_weight.shape[1])
    return (
        encoded,
        g_table,
        conv_grad_w,
        conv_grad_b,
        g_highway[None],
        g_highway_b[None],
        g_proj,
        g_proj_b,
        grad_pos,
        g_gain.reshape(3, nd),
        g_shift.reshape(3, nd),
        g_qkv,
        g_out,
        g_inner,
        g_inner_b,
        g_outer,
    )


def solution(mesh):
    return jax.shard_map(
        per_device,
        mesh=mesh,
        in_specs=(
            P("dp", None, None),
            P("dp"),
            P(),
            P(None, "filt"),
            P("filt"),
            P(None, "dp", None),
            P(None, "dp"),
            P("dp", None),
            P("dp"),
            P("filt", None),
            P(None, "dp"),
            P(None, "dp"),
            P("dp", None),
            P("dp", None),
            P("dp", None),
            P("dp"),
            P("dp", None),
            P("dp", "filt", None),
        ),
        out_specs=(
            P("dp", "filt", None),
            P(),
            P(None, "filt"),
            P("filt"),
            P(None, "dp", None),
            P(None, "dp"),
            P("dp", None),
            P("dp"),
            P("filt", None),
            P(None, "dp"),
            P(None, "dp"),
            P("dp", None),
            P("dp", None),
            P("dp", None),
            P("dp"),
            P("dp", None),
        ),
        check_vma=False,
    )
```

profile of v0, /device:TPU:0, one launch (start us, length us, event | category | flops | bytes accessed | tf_op | source)
XLA Modules:
  0.0 536.7 jit_solution(8093474162266234511)
XLA Ops:
  16.4 84.0 %prologue.1 = (bf16[512,512]{1,0:T(8,128)(2,1)S(1)}, f32[512,512]{1,0:T(8,128)S(1)}, bf16[800,512]{1,0:T(8,128)(2,1)S(1)}, bf16[512,2048]{1,0:T(8,128)(2,1)S(1)}, bf16[2,4,2,256,512]{4,3,2,1,0:T(8,128)(2,1)}) custom-call(s32[56,512]{1,0:T(8,128)S(1)} %pad_bitcast_fusion.chars_ref.refs_2_, bf16[48,128]{1,0:T(8,128)(2,1)S(1)} %bitcast.203, ...), custom_call_target="tpu_custom_call" | custom-call | tf_op jit(solution)/shard_map/prologue/pallas_call | solution.py:659
  105.3 2.6 fusion.50
  108.1 2.2 fusion.55
  110.4 2.2 fusion.56
  118.6 3.7 all-to-all-start
  124.2 3.5 fusion.14
  128.9 2.4 reshape.536
  131.8 28.7 %all-gather.6.cloned.1.call-done = bf16[1536,768]{1,0:T(8,128)(2,1)} async-done(((bf16[192,768]{1,0:T(8,128)(2,1)}), bf16[1536,768]{1,0:T(8,128)(2,1)}) %all-gather.6.cloned.1.call-update) | async-done | bytes 2359312 | tf_op jit(solution)/shard_map/all_gather | solution.py:1084
  160.5 2.8 fusion.51
  165.3 19.1 %forward_stage.2 = (f32[128,768]{1,0:T(8,128)S(1)}, f32[128,768]{1,0:T(8,128)S(1)}, f32[128,1]{1,0:T(8,128)S(1)}, bf16[4,128,768]{2,1,0:T(8,128)(2,1)S(1)}) custom-call(bf16[4,128,768]{2,1,0:T(8,128)(2,1)S(1)} %bitcast.197, f32[128,768]{1,0:T(8,128)S(1)} %convert_add_fusion.1.base_ref, f32[1,768]{1,0:T(1,128)S(1)} %slice.140.gain_ref, ...), custom_call_target="tpu_custom_call" | custom-call | tf_op jit(solution)/shard_map/forward_stage/pallas_call | solution.py:212
  188.2 18.2 %forward_stage.3 = (f32[128,768]{1,0:T(8,128)S(1)}, f32[128,768]{1,0:T(8,128)S(1)}, f32[128,1]{1,0:T(8,128)S(1)}, bf16[4,128,768]{2,1,0:T(8,128)(2,1)S(1)}) custom-call(bf16[4,128,768]{2,1,0:T(8,128)(2,1)S(1)} %bitcast.194, f32[128,768]{1,0:T(8,128)S(1)} %get-tuple-element.58.base_ref, f32[1,768]{1,0:T(1,128)S(1)} %slice.149.gain_ref, ...), custom_call_target="tpu_custom_call" | custom-call | tf_op jit(solution)/shard_map/forward_stage/pallas_call | solution.py:212
  206.4 10.6 %multiply_convert_fusion.1 = (bf16[512,768]{1,0:T(8,128)(2,1)S(1)}, f32[512,768]{1,0:T(8,128)S(1)}, f32[512,768]{1,0:T(8,128)S(1)}) fusion(f32[768]{0:T(1024)S(1)} %add.278, bf16[512,768]{1,0:T(8,128)(2,1)S(1)} %bitcast.206, bf16[768,768]{1,0:T(8,128)(2,1)S(1)} %bitcast.243), kind=kOutput, calls=%fused_computation.22 | convolution fusion | flops 629932032 | bytes 5901312 | tf_op jit(solution)/shard_map/dot_general | solution.py:21
  218.0 19.2 %top_stage.1 = (bf16[128,768]{1,0:T(8,128)(2,1)S(1)}, f32[128,768]{1,0:T(8,128)S(1)}, f32[1,768]{1,0:T(1,128)S(1)}, f32[1,768]{1,0:T(1,128)S(1)}, bf16[4,128,768]{2,1,0:T(8,128)(2,1)S(1)}) custom-call(bf16[4,128,768]{2,1,0:T(8,128)(2,1)S(1)} %bitcast.199, f32[128,768]{1,0:T(8,128)S(1)} %get-tuple-element.61.base_ref, bf16[128,768]{1,0:T(8,128)(2,1)S(1)} %bitcast.202, ...), custom_call_target="tpu_custom_call" | custom-call | tf_op jit(solution)/shard_map/top_stage/pallas_call | solution.py:212
  238.1 1.8 convert_reduce_fusion.1
  242.3 29.0 %backward_stage.2 = (f32[128,768]{1,0:T(8,128)S(1)}, f32[1,768]{1,0:T(1,128)S(1)}, f32[1,768]{1,0:T(1,128)S(1)}, f32[1,768]{1,0:T(1,128)}, bf16[4,128,768]{2,1,0...) custom-call(bf16[4,128,768]{2,1,0:T(8,128)(2,1)S(1)} %bitcast.200, f32[128,768]{1,0:T(8,128)S(1)} %get-tuple-element.64.base_ref, ...), custom_call_target="tpu_custom_call" | custom-call | tf_op jit(solution)/shard_map/backward_stage/pallas_call | solution.py:352
  280.4 2.2 concatenate.70
  284.3 23.2 %backward_stage.3 = (f32[128,768]{1,0:T(8,128)S(1)}, f32[1,768]{1,0:T(1,128)S(1)}, f32[1,768]{1,0:T(1,128)S(1)}, f32[1,768]{1,0:T(1,128)S(1)}, bf16[4,128,768]{2...) custom-call(bf16[4,128,768]{2,1,0:T(8,128)(2,1)S(1)} %bitcast.198, f32[128,768]{1,0:T(8,128)S(1)} %copy-done.16, ...), custom_call_target="tpu_custom_call" | custom-call | tf_op jit(solution)/shard_map/backward_stage/pallas_call | solution.py:352
  309.7 2.3 copy.183
  312.0 2.8 convolution_convert_fusion.6
  318.7 4.4 all-to-all-start.1
  323.1 4.4 multiply_add_fusion
  331.1 2.6 add_convert_fusion.refs_0_
  335.6 6.2 %convolution_convert_fusion = bf16[2048,1024]{1,0:T(8,128)(2,1)} fusion(bf16[512,2048]{1,0:T(8,128)(2,1)} %copy-done.30, bf16[512,1024]{1,0:T(8,128)(2,1)} %copy-done.37), kind=kOutput, calls=%fused_computation.1 | convolution fusion | flops 2149580800 | bytes 7340032 | tf_op jit(solution)/shard_map/dot_general | solution.py:923
  348.0 107.6 %epilogue.1 = (f32[512,128]{1,0:T(8,128)}, f32[96,128]{1,0:T(8,128)}, bf16[4,256,1024]{2,1,0:T(8,128)(2,1)}, bf16[4,160,768]{2,1,0:T(8,128)(2,1)}, bf16[4,192,768]{2,1,0:T(8,128)(2,1)}) custom-call(bf16[512,2048]{1,0:T(8,128)(2,1)} %add_convert_fusion.refs_0_, f32[512,512]{1,0:T(8,128)} %get-tuple-element.176.refs_1_, s32[56,512]{1,0:T(8,128)} %copy-done.6, ...), custom_call_target="tpu_custom_call" | custom-call | tf_op jit(solution)/shard_map/epilogue/pallas_call | solution.py:888
  455.6 2.0 slice_convert_fusion.1
  457.6 1.9 slice_convert_fusion.2
  459.6 25.9 %total_all.1 = (bf16[8,160,128]{2,1,0:T(8,128)(2,1)S(1)}, bf16[8,24,128]{2,1,0:T(8,128)(2,1)S(1)}) custom-call(f32[8,160,128]{2,1,0:T(8,128)S(1)} %pad_maximum_fusion.3.rows_ref, f32[8,24,128]{2,1,0:T(8,128)S(1)} %pad_maximum_fusion.8.table_ref), custom_call_target="tpu_custom_call" | custom-call | tf_op jit(solution)/shard_map/total_all/pallas_call | solution.py:212
  491.1 5.4 reshape.585
  496.5 6.9 %copy.193 = f32[256,2,4,512]{3,2,1,0:T(4,128)} copy(f32[256,2,4,512]{3,1,0,2:T(2,128)} %bitcast.210) | data formatting | bytes 8388608 | tf_op jit(solution)/shard_map/convert_element_type | solution.py:1277
  503.4 6.1 %reshape.578 = f32[1,256,4096]{2,1,0:T(8,128)} reshape(f32[256,2,4,512]{3,2,1,0:T(4,128)} %copy.193) | data formatting | bytes 8388608 | tf_op jit(solution)/shard_map/convert_element_type | solution.py:1277
  512.2 2.6 reshape.583
  514.8 2.3 reshape.587
  (338 shorter events, 80.7 us)
Async XLA Ops:
  7.2 95.2 %copy-start = (bf16[384,768]{1,0:T(8,128)(2,1)S(1)}, bf16[384,768]{1,0:T(8,128)(2,1)}, u32[]{:S(2)}) copy-start(bf16[384,768]{1,0:T(8,128)(2,1)} %param.34) | copy-start | bytes 1769476
  7.2 105.4 %all-gather.8.cloned.1.call-start = ((), (), s32[]{:S(2)}) async-start(), calls=%async_computation.3 | async-start | bytes 2322432 | tf_op jit(solution)/shard_map/all_gather | solution.py:1045
  7.3 3.5 copy-start.61
  12.5 148.0 %all-gather.6.cloned.1.call-start = ((), (), s32[]{:S(2)}) async-start(), calls=%async_computation.2 | async-start | bytes 2654208 | tf_op jit(solution)/shard_map/all_gather | solution.py:1084
  16.0 84.5 %copy-start.6 = (s32[56,512]{1,0:T(8,128)}, s32[56,512]{1,0:T(8,128)S(1)}, u32[]{:S(2)}) copy-start(s32[56,512]{1,0:T(8,128)S(1)} %pad_bitcast_fusion.chars_ref.refs_2_) | copy-start | bytes 344068
  16.2 84.3 %copy-start.2 = (s32[512,1]{1,0:T(8,128)}, s32[512,1]{1,0:T(8,128)S(1)}, u32[]{:S(2)}) copy-start(s32[512,1]{1,0:T(8,128)S(1)} %broadcast_subtract_fusion.limit_ref.refs_7_) | copy-start | bytes 6148
  16.4 86.0 %copy-start.3 = (f32[512,1]{1,0:T(8,128)}, f32[512,1]{1,0:T(8,128)S(1)}, u32[]{:S(2)}) copy-start(f32[512,1]{1,0:T(8,128)S(1)} %convert_log_fusion.count_ref.refs_8_) | copy-start | bytes 6148
  102.4 21.8 %copy-start.11 = (bf16[512,512]{1,0:T(8,128)(2,1)}, bf16[512,512]{1,0:T(8,128)(2,1)S(1)}, u32[]{:S(2)}) copy-start(bf16[512,512]{1,0:T(8,128)(2,1)S(1)} %get-tuple-element.56) | copy-start | bytes 1572868
  105.3 81.4 %copy-start.67 = (pred[512]{0:T(512)(128)(4,1)}, pred[512]{0:T(512)(128)(4,1)S(1)}, u32[]{:S(2)}) copy-start(pred[512]{0:T(512)(128)(4,1)S(1)} %iota_compare_fusion) | copy-start | bytes 1540
  118.6 44.7 %all-to-all-start = ((bf16[4,704,192]{1,2,0:T(8,128)(2,1)}), bf16[4,704,192]{1,2,0:T(8,128)(2,1)S(1)}, u32[]{:S(2)}, u32[]{:S(2)}) async-start(bf16[4,704,192]{1,2,0:T(8,128)(2,1)} %copy.172), calls=%async_computation | async-start | bytes 2359296 | tf_op jit(solution)/shard_map/all_to_all | solution.py:1009
  124.2 3.5 copy-start.32
  128.3 3.5 copy-start.60
  163.3 43.1 %copy-start.48 = (bf16[8,96,768]{2,1,0:T(8,128)(2,1)}, bf16[8,96,768]{2,1,0:T(8,128)(2,1)S(1)}, u32[]{:S(2)}) copy-start(bf16[8,96,768]{2,1,0:T(8,128)(2,1)S(1)} %get-tuple-element.178) | copy-start | bytes 3538948
  163.4 21.1 %copy-start.53 = (bf16[512,4,192]{0,2,1:T(8,128)(2,1)}, bf16[512,4,192]{0,2,1:T(8,128)(2,1)S(1)}, u32[]{:S(2)}) copy-start(bf16[512,4,192]{0,2,1:T(8,128)(2,1)S(1)} %slice.176) | copy-start | bytes 2359300
  164.7 19.8 %copy-start.52 = (bf16[768,576]{1,0:T(8,128)(2,1)S(1)}, bf16[768,576]{1,0:T(8,128)(2,1)}, u32[]{:S(2)}) copy-start(bf16[768,576]{1,0:T(8,128)(2,1)} %reshape.536) | copy-start | bytes 2654212
  187.8 29.3 %copy-start.44 = (bf16[3,64,512]{2,1,0:T(8,128)(2,1)}, bf16[3,64,512]{2,1,0:T(8,128)(2,1)S(1)}, u32[]{:S(2)}) copy-start(bf16[3,64,512]{2,1,0:T(8,128)(2,1)S(1)} %convolution_convert_fusion.14) | copy-start | bytes 589828
  206.4 10.7 %copy-start.50 = (bf16[8,96,768]{2,1,0:T(8,128)(2,1)S(1)}, bf16[8,96,768]{2,1,0:T(8,128)(2,1)}, u32[]{:S(2)}) copy-start(bf16[8,96,768]{2,1,0:T(8,128)(2,1)} %get-tuple-element.177) | copy-start | bytes 3538948
  238.1 3.9 copy-start.38
  242.3 29.5 %copy-start.68 = (pred[512]{0:T(512)(128)(4,1)S(1)}, pred[512]{0:T(512)(128)(4,1)}, u32[]{:S(2)}) copy-start(pred[512]{0:T(512)(128)(4,1)} %copy-done.67) | copy-start | bytes 1540
  309.7 5.1 copy-start.28
  312.0 4.0 copy-start.45
  318.7 4.4 copy-start.9
  318.7 4.4 copy-start.12
  318.7 23.1 %all-to-all-start.1 = ((bf16[4,704,192]{1,2,0:T(8,128)(2,1)}), bf16[4,704,192]{1,2,0:T(8,128)(2,1)}, u32[]{:S(2)}, u32[]{:S(2)}) async-start(bf16[4,704,192]{1,2,0:T(8,128)(2,1)} %maximum_bitcast_fusion), calls=%async_computation.1 | async-start | bytes 2359296 | tf_op jit(solution)/shard_map/all_to_all | solution.py:1016
  331.1 3.6 copy-start.14
  455.5 4.0 copy-start.64
  455.6 4.0 copy-start.59
  459.6 31.6 %copy-start.43 = (bf16[4,256,1024]{2,1,0:T(8,128)(2,1)S(1)}, bf16[4,256,1024]{2,1,0:T(8,128)(2,1)}, u32[]{:S(2)}) copy-start(bf16[4,256,1024]{2,1,0:T(8,128)(2,1)} %get-tuple-element.89) | copy-start | bytes 6291460
  503.4 6.1 %copy-start.51 = (bf16[4,192,768]{2,1,0:T(8,128)(2,1)S(1)}, bf16[4,192,768]{2,1,0:T(8,128)(2,1)}, u32[]{:S(2)}) copy-start(bf16[4,192,768]{2,1,0:T(8,128)(2,1)} %get-tuple-element.91) | copy-start | bytes 3538948
  522.7 4.6 copy-start.47
  523.8 4.9 copy-start.18
  523.8 5.5 %copy-start.1 = (bf16[384,768]{1,0:T(8,128)(2,1)S(1)}, bf16[384,768]{1,0:T(8,128)(2,1)}, u32[]{:S(2)}) copy-start(bf16[384,768]{1,0:T(8,128)(2,1)} %param.34) | copy-start | bytes 1769476
  (55 other events, 105.6 us)
Sparse Core Ops, SparseCore 0:
  12.6 78.2 all-gather.7
  104.7 55.7 all-gather.5
where the time goes:
time: 543 us; the launch traced here: 537 us
  Pallas kernels  326 us (60%)
  local copies, waits for them, and re-layouts  81.5 us (15%)
  matrix products  48.2 us (9%)
  waiting for transfers between devices  28.8 us (5%)
  other arithmetic  26.9 us (5%)
  between operations  16.7 us (3%)
  starting transfers between devices  8.22 us (2%)
    pallas_call x1, Pallas kernels, epilogue_call(): pl.pallas_call(functools.partial(epilogue, letters, depth, block, PLAN),...  108 us
    pallas_call x1, Pallas kernels, prologue_call(): pl.pallas_call(functools.partial(prologue, letters, depth, block, chunks,...  84 us
    pallas_call x4, Pallas kernels, comm_call(): pl.pallas_call(kernel, out_shape=out_shape, in_specs=[vmem] * len(args),...  82.5 us
    pallas_call x2, Pallas kernels, backward_stage_call(): pl.pallas_call(functools.partial(backward_stage, kind), out_shape=out_sha...  52.2 us
    convert_element_type x14, local copies, waits for them, and re-layouts, join_columns(): return split.reshape(rows_here, -1).astype(jnp.float32)  29.6 us
    all_gather x1, waiting for transfers between devices, per_device(): ffn_all = lax.all_gather(ffn_own, 'dp', axis=0, tiled=False)  28.7 us
    dot_general x7, matrix products, nn_dot(): return jnp.dot(left, right, preferred_element_type=jnp.float32)  17.6 us
    unnamed x173, local copies, waits for them, and re-layouts  13.9 us
  transfers between devices with their start and end apart: 4, of which 1 were waited for; matrix products, arithmetic and copies ran while one was open for 8% of the time, Pallas kernels for 16%

commit v1 on v0

--- a/solution.py
+++ b/solution.py
@@ -201,6 +201,11 @@
     for peer in peers:
         pl.semaphore_signal(barrier, inc=1, device_id=peer, device_id_type=MESH)
     pl.semaphore_wait(barrier, len(peers))
+
+def greet_all():
+    slot, me = lax.axis_index("dp"), lax.axis_index("filt")
+    count, parts = lax.axis_size("dp"), lax.axis_size("filt")
+    greet([{"dp": slot ^ far, "filt": me ^ near} for far in range(count) for near in range(parts) if far or near])
 
 def remote(source, target, send, recv, peer):
     return pltpu.make_async_remote_copy(
@@ -437,63 +442,58 @@
         [pltpu.VMEM((3, rows, cols), jnp.bfloat16), pltpu.VMEM((rows, cols), jnp.bfloat16), DMA((3, chunks)), DMA((3, chunks))],
         ident, part, base, name="scatter_channels")
 
-def total_all(rows_ref, table_ref, rows_out, table_out, inbox, tbox, sbox, low, tlow, tsum, send, recv):
-    count = lax.axis_size("dp")
-    slot = lax.axis_index("dp")
-    me = lax.axis_index("filt")
-    size = rows_out.shape[1]
-    tsize = table_out.shape[1]
-    low[...] = rows_ref[...].astype(jnp.bfloat16)
-    tlow[...] = table_ref[...].astype(jnp.bfloat16)
-    greet([{"dp": slot ^ hop} for hop in range(1, count)] + [{"filt": me ^ hop} for hop in (1, 2, 3)])
-    copies = []
-    for hop in range(1, count):
-        peer = {"dp": slot ^ hop}
-        copy = remote(low.at[slot ^ hop], inbox.at[hop - 1], send.at[0, hop - 1], recv.at[0, hop - 1], peer)
+
+class Total:
+    def __init__(self, low, inbox, out, send, recv, sides=None):
+        self.low, self.inbox, self.out, self.sides = low, inbox, out, sides
+        self.send, self.recv = send, recv
+        self.me, self.slot = lax.axis_index("filt"), lax.axis_index("dp")
+        self.count = low.shape[0]
+        self.copies = []
+
+    def push(self, source, target, kind, hop, peer):
+        copy = remote(source, target, self.send.at[kind, hop - 1], self.recv.at[kind, hop - 1], peer)
         copy.start()
-        also = remote(tlow.at[slot ^ hop], tbox.at[hop - 1], send.at[1, hop - 1], recv.at[1, hop - 1], peer)
-        also.start()
-        copies += [copy, also]
-    total = rows_ref[slot]
-    part = table_ref[slot]
-    for hop in range(1, count):
-        copies[2 * hop - 2].wait()
-        copies[2 * hop - 1].wait()
-        total = total + inbox[hop - 1].astype(jnp.float32)
-        part = part + tbox[hop - 1].astype(jnp.float32)
-    rows_out[slot] = total.astype(jnp.bfloat16)
-    tsum[...] = part.astype(jnp.bfloat16)
-    sides = []
-    for hop in (1, 2, 3):
-        copy = remote(tsum, sbox.at[hop - 1], send.at[2, hop - 1], recv.at[2, hop - 1], {"filt": me ^ hop})
-        copy.start()
-        sides.append(copy)
-    outs = []
-    for hop in range(1, count):
-        copy = remote(rows_out.at[slot], rows_out.at[slot], send.at[3, hop - 1], recv.at[3, hop - 1], {"dp": slot ^ hop})
-        copy.start()
-        outs.append(copy)
-    for hop in (1, 2, 3):
-        sides[hop - 1].wait()
-    ordered = tsum[...].astype(jnp.float32)
-    near = sbox[0].astype(jnp.float32)
-    ordered = (ordered + near) + (sbox[1].astype(jnp.float32) + sbox[2].astype(jnp.float32))
-    table_out[slot] = ordered.astype(jnp.bfloat16)
-    for hop in range(1, count):
-        copy = remote(table_out.at[slot], table_out.at[slot], send.at[4, hop - 1], recv.at[4, hop - 1], {"dp": slot ^ hop})
-        copy.start()
-        outs.append(copy)
-    for copy in outs:
-        copy.wait()
-
-def total_all_call(rows, table, ident):
-    count, size, lanes = rows.shape
-    tsize = table.shape[1]
-    return comm_call(total_all, (bf16(count, size, lanes), bf16(count, tsize, lanes)),
-        [pltpu.VMEM((count - 1, size, lanes), jnp.bfloat16), pltpu.VMEM((count - 1, tsize, lanes), jnp.bfloat16),
-         pltpu.VMEM((3, tsize, lanes), jnp.bfloat16), pltpu.VMEM((count, size, lanes), jnp.bfloat16), pltpu.VMEM((count, tsize, lanes), jnp.bfloat16),
-         pltpu.VMEM((tsize, lanes), jnp.bfloat16), DMA((5, count - 1)), DMA((5, count - 1))],
-        ident, rows, table, name="total_all")
+        self.copies.append(copy)
+        return copy
+
+    def start(self, value):
+        self.low[...] = value.astype(jnp.bfloat16)
+        self.first = [
+            self.push(self.low.at[self.slot ^ hop], self.inbox.at[hop - 1], 0, hop, {"dp": self.slot ^ hop})
+            for hop in range(1, self.count)
+        ]
+
+    def combine(self):
+        for copy in self.first:
+            copy.wait_recv()
+        total = self.low[self.slot].astype(jnp.float32)
+        for hop in range(1, self.count):
+            total = total + self.inbox[hop - 1].astype(jnp.float32)
+        self.out[self.slot] = total.astype(jnp.bfloat16)
+        if self.sides is None:
+            self.spread()
+            return
+        self.sides[0] = total.astype(jnp.bfloat16)
+        self.second = [self.push(self.sides.at[0], self.sides.at[hop], 1, hop, {"filt": self.me ^ hop}) for hop in (1, 2, 3)]
+
+    def across(self):
+        for copy in self.second:
+            copy.wait_recv()
+        left = self.sides[0].astype(jnp.float32) + self.sides[1].astype(jnp.float32)
+        right = self.sides[2].astype(jnp.float32) + self.sides[3].astype(jnp.float32)
+        self.out[self.slot] = (left + right).astype(jnp.bfloat16)
+        self.spread()
+
+    def spread(self):
+        piece = self.out.at[self.slot]
+        self.third = [self.push(piece, piece, 2, hop, {"dp": self.slot ^ hop}) for hop in range(1, self.count)]
+
+    def finish(self):
+        for copy in self.third:
+            copy.wait_recv()
+        for copy in self.copies:
+            copy.wait_send()
 
 
 def prologue(letters, depth, block, chunks, window, first, chars_ref, table_ref, weight_ref, limit_ref, count_ref, shard_ref,
@@ -693,6 +693,8 @@
     def along(self):
         span = self.span
         self.first.wait_recv()
+        if self.after is not None:
+            self.after.across()
         both = self.grad[:, self.side, span, :].astype(jnp.float32) + self.yin[:, span, :].astype(jnp.float32)
         self.pair[:, span, :] = both.astype(jnp.bfloat16)
         self.rest = [
@@ -727,38 +729,51 @@
             copy.wait_send()
 
 
-def epilogue(letters, depth, block, plan, *refs):
-    (part_ref, base_ref, chars_ref, embed_ref, lse_ref, weight_ref, back_ref, limit_ref, count_ref, wide_ref, slim_ref, ffn_ref,
-     wgrad_ref, tgrad_ref, wide_out, slim_out, ffn_out,
-     inbox, merged, up_ref, patch_ref, down_ref, pull_ref, wide_y, wide_p, wide_z, slim_y, slim_p, slim_z,
-     csend, crecv, rsend, rrecv) = refs
+AHEAD = 2
+
+
+def epilogue(letters, depth, block, *refs):
+    (part_ref, base_ref, chars_ref, embed_ref, lse_ref, weight_ref, back_ref, limit_ref, count_ref, wide_ref, slim_ref,
+     rows_ref, ffn_ref, pos_ref, few_ref,
+     wide_out, slim_out, rows_out, ffn_out, conv_out, table_out, pos_out, few_out,
+     inbox, merged, up_ref, patch_ref, down_ref, pull_ref, wgrad_ref, tgrad_ref, wide_y, wide_p, wide_z, slim_y, slim_p, slim_z,
+     rows_y, rows_p, rows_z, conv_low, conv_in, table_low, table_in, table_side, pos_low, pos_in, few_low, few_in, few_side,
+     csend, crecv, rsend, rrecv, tsend, trecv) = refs
     me = lax.axis_index("filt")
-    slot = lax.axis_index("dp")
-    greet([{"filt": me ^ hop} for hop in (1, 2)] + [{"dp": slot ^ hop} for hop in (1, 2, 4, 6)])
-    items = []
-    slim_rows = slim_out.shape[1] // 2
+    greet_all()
+    pos = Total(pos_low, pos_in, pos_out, tsend.at[0], trecv.at[0])
+    few = Total(few_low, few_in, few_out, tsend.at[1], trecv.at[1], few_side)
+    conv_total = Total(conv_low, conv_in, conv_out, tsend.at[2], trecv.at[2])
+    table_total = Total(table_low, table_in, table_out, tsend.at[3], trecv.at[3], table_side)
     wide_rows = wide_out.shape[1] // 4
-    for index in range(2):
-        items.append(RowReduce(slim_ref, slim_y, slim_p, slim_z, slim_out, pl.ds(index * slim_rows, slim_rows),
-                               (rsend.at[index], rrecv.at[index])))
-    for index in range(4):
-        items.append(RowReduce(wide_ref, wide_y, wide_p, wide_z, wide_out, pl.ds(index * wide_rows, wide_rows),
-                               (rsend.at[2 + index], rrecv.at[2 + index])))
-    for item in items:
+    slim = RowReduce(slim_ref, slim_y, slim_p, slim_z, slim_out, pl.ds(0, slim_out.shape[1]), (rsend.at[4], rrecv.at[4]))
+    both = RowReduce(rows_ref, rows_y, rows_p, rows_z, rows_out, pl.ds(0, rows_out.shape[1]), (rsend.at[6], rrecv.at[6]))
+    wide = [
+        RowReduce(wide_ref, wide_y, wide_p, wide_z, wide_out, pl.ds(index * wide_rows, wide_rows), (rsend.at[index], rrecv.at[index]))
+        for index in range(4)
+    ]
+    ffn = RowReduce(None, None, None, None, ffn_out, pl.ds(0, ffn_out.shape[1]), (rsend.at[5], rrecv.at[5]))
+    pos.start(pos_ref[...])
+    few.start(few_ref[...])
+    queue = [slim, both] + wide
+    for index, item in enumerate(queue):
+        item.after = queue[index + AHEAD] if index + AHEAD < len(queue) else None
+    for item in queue[:AHEAD]:
         item.across()
-    ffn = RowReduce(None, None, None, None, ffn_out, pl.ds(0, ffn_out.shape[1]), (rsend.at[6], rrecv.at[6]))
     ffn_out[me] = ffn_ref[...]
     scatter = ChannelScatter(part_ref, base_ref, up_ref, inbox, merged, csend, crecv)
     scatter.run()
+    pos.combine()
+    few.combine()
     ffn.share()
-    steps = iter([(ffn, "relay") if code == "F" else (items[int(code[1:])], {"A": "along", "J": "join", "R": "relay"}[code[0]])
-                  for code in plan])
-
-    def advance(many):
-        for unused in range(many):
-            step = next(steps, None)
-            if step is not None:
-                getattr(*step)()
+    steps = iter([
+        [slim.along, ffn.relay], [], [both.along, slim.join], [slim.relay], [wide[0].along, both.join],
+        [both.relay, few.across], [wide[1].along, wide[0].join], [wide[0].relay], [], [],
+    ])
+
+    def advance():
+        for step in next(steps):
+            step()
 
     filters = weight_ref.shape[0]
     rows = KW * depth
@@ -797,8 +812,8 @@
 
         for lap in range(4):
             stop = always if lap == 3 else (lap + 1) * quarter
-            lax.fori_loop(lap * quarter, stop, body, 0)
-            advance(2)
+            lax.fori_loop(lap * quarter, stop, body, 0, unroll=11)
+            advance()
         for position in range(always, letters):
             one(position, True)
 
@@ -817,10 +832,19 @@
             return carry
 
         lax.fori_loop(0, letters, table, 0, unroll=5)
-        advance(2)
-    advance(len(plan))
-    ffn.finish()
-    for item in items:
+        advance()
+    table_rows = tgrad_ref.shape[0] // 2
+    slices, size = table_low.shape[:2]
+    conv_total.start(wgrad_ref[...].reshape(conv_low.shape))
+    sums = tgrad_ref[:table_rows, :] + tgrad_ref[table_rows:, :]
+    sums = jnp.concatenate([sums, jnp.zeros((slices * size - table_rows, sums.shape[1]), jnp.float32)], axis=0)
+    table_total.start(sums.reshape(table_low.shape))
+    for step in (
+        wide[2].along, wide[1].join, wide[1].relay, wide[3].along, conv_total.combine, table_total.combine, wide[2].join,
+        wide[2].relay, table_total.across, wide[3].join, wide[3].relay,
+    ):
+        step()
+    for item in [ffn, slim, both, pos, few, conv_total, table_total] + wide:
         item.finish()
 
 
@@ -865,36 +889,82 @@
             copy.wait_send()
 
 
-PLAN = ("A0", "F", "A1", "J0", "A2", "J1", "R0", "A3", "J2", "R1", "A4", "J3", "R2", "A5", "J4", "R3", "J5", "R4", "R5")
-
-
-def epilogue_call(part, base, ids, embed, lse, weight, back, limit, count, wide, slim, ffn, letters, depth, groups, ident, block=256):
+def epilogue_call(part, base, ids, embed, lse, weight, back, limit, count, wide, slim, both, ffn, pos, few, letters, depth, groups, ident, block=256):
     filters, words = lse.shape
-    args = (part, base, ids, embed, lse, weight, back, limit, count, wide, slim, ffn)
+    args = (part, base, ids, embed, lse, weight, back, limit, count, wide, slim, both, ffn, pos, few)
     parts = part.shape[1] // filters
+    slices = pos.shape[0]
     pieces = 4
     vmem = pl.BlockSpec(memory_space=pltpu.VMEM)
+    table_size = -(-(-(-groups * depth // slices)) // 8) * 8
 
     def space(shape, dtype=jnp.bfloat16):
-        return pltpu.VMEM(shape, dtype)
+        return pltpu.VMEM(tuple(shape), dtype)
 
     def stages(array):
         ring, side, rows, cols = array.shape
         return [space((ring, rows, cols)), space((ring, rows, cols)), space((ring - 1, rows, cols))]
 
-    out_shape = [f32(filters, 128), f32(2 * groups * depth, 128), bf16(parts, *wide.shape[2:]), bf16(parts, *slim.shape[2:]),
-                 bf16(parts, *ffn.shape)]
+    def totals(shape, sides):
+        spaces = [space(shape), space((shape[0] - 1,) + shape[1:])]
+        return spaces + ([space((4,) + shape[1:])] if sides else [])
+
+    conv_shape = (slices, filters // slices, 128)
+    table_shape = (slices, table_size, 128)
+    out_shape = [bf16(parts, *wide.shape[2:]), bf16(parts, *slim.shape[2:]), bf16(parts, *both.shape[2:]), bf16(parts, *ffn.shape), bf16(*conv_shape), bf16(*table_shape), bf16(*pos.shape), bf16(*few.shape)]
     padded = (letters + KW - 1) * depth
     return pl.pallas_call(
-        functools.partial(epilogue, letters, depth, block, PLAN),
+        functools.partial(epilogue, letters, depth, block),
         in_specs=[vmem] * len(args),
         out_specs=[vmem] * len(out_shape),
         out_shape=out_shape,
         scratch_shapes=[space((3, words, filters)), space((words, filters)), space((words, filters)), space((padded, block)),
-                        space((padded, block), jnp.float32), space((filters, block), jnp.float32)]
-        + stages(wide) + stages(slim) + [DMA((3, pieces)), DMA((3, pieces)), DMA((7, 7)), DMA((7, 7))],
+                        space((padded, block), jnp.float32), space((filters, block), jnp.float32),
+                        space((filters, 128), jnp.float32), space((2 * groups * depth, 128), jnp.float32)]
+        + stages(wide) + stages(slim) + stages(both)
+        + totals(conv_shape, False) + totals(table_shape, True) + totals(pos.shape, False) + totals(few.shape, True)
+        + [DMA((3, pieces)), DMA((3, pieces)), DMA((7, 7)), DMA((7, 7)), DMA((4, 3, slices - 1)), DMA((4, 3, slices - 1))],
         compiler_params=pltpu.CompilerParams(collective_id=ident, has_side_effects=True, vmem_limit_bytes=56 << 20),
         name="epilogue",
+    )(*args)
+
+
+def assemble(wide_ref, slim_ref, both_ref, ffn_ref, wide_out, slim_out, proj_out, out_out, inner_out, outer_out):
+    parts = wide_ref.shape[0]
+    inner_rows = inner_out.shape[0]
+    proj_rows, out_rows = proj_out.shape[0] // parts, out_out.shape[0] // parts
+    filters = wide_ref.shape[2] // 2
+    width = slim_ref.shape[2] // 3
+    for part in range(parts):
+        for half in range(2):
+            start = (half * parts + part) * filters
+            wide_out[:, start : start + filters] = wide_ref[part, :, half * filters : (half + 1) * filters].astype(jnp.float32)
+        for block in range(3):
+            start = (block * parts + part) * width
+            slim_out[:, start : start + width] = slim_ref[part, :, block * width : (block + 1) * width].astype(jnp.float32)
+        cols = slice(part * width, (part + 1) * width)
+        for block in range(parts):
+            lanes = slice(block * width, (block + 1) * width)
+            proj_out[block * proj_rows : (block + 1) * proj_rows, cols] = both_ref[part, :proj_rows, lanes].astype(jnp.float32)
+            out_out[block * out_rows : (block + 1) * out_rows, cols] = both_ref[part, proj_rows:, lanes].astype(jnp.float32)
+        units = ffn_ref.shape[1] - inner_rows
+        outer_out[part * units : (part + 1) * units, :] = ffn_ref[part, inner_rows:, :].astype(jnp.float32)
+        for block in range(inner_out.shape[1] // (parts * units)):
+            start = (block * parts + part) * units
+            inner_out[:, start : start + units] = ffn_ref[part, :inner_rows, block * units : (block + 1) * units].astype(jnp.float32)
+
+
+def assemble_call(wide, slim, both, ffn, inner_rows, out_rows):
+    args = (wide, slim, both, ffn)
+    parts = wide.shape[0]
+    vmem = pl.BlockSpec(memory_space=pltpu.VMEM)
+    units = ffn.shape[1] - inner_rows
+    dmodel = both.shape[2]
+    out_shape = [f32(wide.shape[1], wide.shape[2] * parts), f32(slim.shape[1], slim.shape[2] * parts),
+                 f32(both.shape[1] * parts - out_rows, dmodel), f32(out_rows, dmodel), f32(inner_rows, dmodel * parts), f32(units * parts, dmodel)]
+    return pl.pallas_call(
+        assemble, in_specs=[vmem] * 4, out_specs=[vmem] * 6, out_shape=out_shape,
+        compiler_params=pltpu.CompilerParams(vmem_limit_bytes=32 << 20), name="assemble",
     )(*args)
 
 
@@ -1004,18 +1074,23 @@
     def gather_rows(array):
         return lax.all_gather(array, "dp", axis=0, tiled=True)
 
-    def rows_from_columns(proj_cols, out_cols):
-        stack = jnp.concatenate([item.reshape(parts, -1, width) for item in (proj_cols, out_cols)], axis=1)
-        stack = lax.all_to_all(stack, "filt", split_axis=0, concat_axis=0, tiled=True)
-        whole = stack.transpose(1, 0, 2).reshape(-1, dmodel)
-        return whole[: proj_cols.shape[0] // parts], whole[proj_cols.shape[0] // parts :]
-
-    def columns_from_rows(proj_rows, out_rows):
-        stack = jnp.concatenate([proj_rows, out_rows], axis=0).astype(jnp.bfloat16)
-        stack = stack.reshape(-1, parts, width).transpose(1, 0, 2)
-        stack = lax.all_to_all(stack, "filt", split_axis=0, concat_axis=0, tiled=True)
-        split = proj_rows.shape[0]
-        return stack[:, :split].reshape(-1, width), stack[:, split:].reshape(-1, width)
+    def rows_from_columns(both, split):
+        rows = both.shape[1]
+        both = lax.all_to_all(both.reshape(parts, -1, dmodel), "filt", split_axis=0, concat_axis=0, tiled=True)
+        both = both.reshape(parts, slices // parts, rows, parts, width)
+        return [
+            item.transpose(1, 2, 3, 0, 4).reshape(-1, dmodel) for item in (both[:, :, :split], both[:, :, split:])
+        ]
+
+    def columns_from_rows(*grads):
+        items = [
+            item.astype(jnp.bfloat16).reshape(slices // parts, parts, -1, parts, width).transpose(3, 0, 2, 1, 4)
+            for item in grads
+        ]
+        both = jnp.concatenate([item.reshape(parts, slices // parts, -1, dmodel) for item in items], axis=2)
+        rows = both.shape[2]
+        both = lax.all_to_all(both.reshape(parts, -1, dmodel), "filt", split_axis=0, concat_axis=0, tiled=True)
+        return both.reshape(slices, rows, dmodel)
 
     fast = slices == 8 and parts == 4
     hb, pb, nd = highway_bias.shape[1], proj_bias.shape[0], norm_gain.shape[1]
@@ -1043,9 +1118,9 @@
     for item in slim_parts[1:3]:
         slim_cuts.append(slim_cuts[-1] + item.shape[0])
     slim_all = lax.all_gather(jnp.concatenate(slim_parts, axis=0), "dp", axis=0, tiled=False)
-    qkv_own, proj_cols, out_cols, small = jnp.split(slim_all, slim_cuts, axis=1)
-    qkv_own = qkv_own.reshape(dmodel, 3 * width)
-    proj_own, out_own = rows_from_columns(proj_cols.reshape(-1, width), out_cols.reshape(-1, width))
+    qkv_own = slim_all[:, : slim_cuts[0]].reshape(dmodel, 3 * width)
+    proj_own, out_own = rows_from_columns(slim_all[:, slim_cuts[0] : slim_cuts[2]], slim_cuts[1] - slim_cuts[0])
+    small = slim_all[:, slim_cuts[2] :]
     small = small.reshape(slices, -1)[:, :small_size].astype(jnp.float32)
     cuts = [hb, hb + pb, hb + pb + 3 * nd, hb + pb + 6 * nd]
     highway_b, proj_b, gain, shift, inner_b = jnp.split(small, cuts, axis=1)
@@ -1082,8 +1157,6 @@
         gates = nn_dot(features, highway_own) + highway_b_own
     ffn_own, features = lax.optimization_barrier((ffn_own, features))
     ffn_all = lax.all_gather(ffn_own, "dp", axis=0, tiled=False)
-    inner_own = ffn_all[:, : inner_rows].reshape(dmodel, -1)
-    outer_own = ffn_all[:, inner_rows :].reshape(-1, dmodel)
     feature_own = acts.astype(jnp.float32)
     hidden_low = highway_mix(feature_own, gates).astype(jnp.bfloat16)
     base = position.astype(jnp.float32) + proj_b[None, :]
@@ -1115,6 +1188,9 @@
         blocks_of(nn_dot(attended, out_own)), first, gain[1:2], shift[1:2], EPS, 2
     )
     second_all = second_all.reshape(words, dmodel)
+    ffn_all, second_all = lax.optimization_barrier((ffn_all, second_all))
+    inner_own = ffn_all[:, :inner_rows].reshape(dmodel, -1)
+    outer_own = ffn_all[:, inner_rows:].reshape(-1, dmodel)
     inner = nn_dot(second_all, inner_own) + inner_b_own
     active = exact_gaussian_activation(inner).astype(jnp.bfloat16)
     top, d_res_two, d_gain_two, d_shift_two, d_outer = top_stage_call(
@@ -1166,7 +1242,7 @@
     d_packed = jnp.concatenate(
         [item.reshape(words, width) for item in (d_queries, d_keys, d_values)], axis=1
     ).astype(jnp.bfloat16)
-    grad_qkv = tn_dot(first_all, d_packed)
+    grad_qkv = tn_dot(first_all, d_packed).astype(jnp.bfloat16)
     d_summed, d_gain_zero, d_shift_zero, grad_proj_b, d_projected, *got = backward_stage_call(
         blocks_of(nt_dot(d_packed, qkv_own)), d_res_one, unit_zero, scale_zero, gain[0:1], 5, kinds[1], grad_ffn
     )
@@ -1177,13 +1253,7 @@
     grad_pos = jnp.sum(d_summed.reshape(seqs, quarter, dmodel), axis=0)
     d_projected = d_projected.reshape(words, dmodel)
     grad_proj = tn_dot(hidden_low, d_projected)
-    grad_slim = jnp.concatenate(
-        [
-            item.astype(jnp.bfloat16).reshape(slices, -1, dmodel)
-            for item in (grad_qkv, *columns_from_rows(grad_proj, grad_out))
-        ],
-        axis=1,
-    )
+    grad_both = columns_from_rows(grad_proj, grad_out)
     d_hidden = nt_dot(d_projected, proj_own)
     d_in, d_gates = jax.vjp(highway_mix, feature_own, gates)[1](d_hidden)
     d_gates = d_gates.astype(jnp.bfloat16)
@@ -1195,34 +1265,6 @@
         d_partial = nt_dot(d_gates, highway_own)
     d_partial = d_partial.astype(jnp.bfloat16)
     groups = table.shape[0] // depth
-    if fast:
-        conv_sums, table_sums, wide_all, slim_all, ffn_all = epilogue_call(
-            d_partial,
-            d_in,
-            ids,
-            embed,
-            lse,
-            weight,
-            back,
-            limit,
-            count,
-            grad_highway.reshape(4, 2, -1, 2 * filters),
-            grad_slim.reshape(4, 2, -1, dmodel),
-            grad_ffn,
-            letters,
-            depth,
-            groups,
-            6,
-        )
-    else:
-        d_features = scatter_channels_call(d_partial, d_in, 6)
-        conv_sums, table_sums = conv_backward_call(
-            ids, embed, lse, d_features, weight, back, limit, count, groups, letters, depth
-        )
-        wide_all = jnp.stack(join_parts(reduce_rows(grad_highway)))
-        slim_all = jnp.stack(join_parts(reduce_rows(grad_slim.reshape(-1, dmodel))))
-        ffn_all = jnp.stack(join_parts(reduce_rows(grad_ffn.reshape(-1, dmodel))))
-    table_sums = table_sums.reshape(2, groups * depth, -1).sum(0)
 
     def place_columns(own, blocks):
         piece = own.reshape(blocks, 1, -1)
@@ -1240,25 +1282,44 @@
     ]
     rows = jnp.concatenate(pieces, axis=1)
     if fast:
-        table_rows = -(-table_sums.shape[0] // slices)
-        table_rows = -(-table_rows // 8) * 8
-        padded = jnp.pad(table_sums, ((0, table_rows * slices - table_sums.shape[0]), (0, 0)))
-        small_rows = -(-rows.shape[1] // 1024) * 8
-        packed_rows = jnp.pad(rows, ((0, 0), (0, small_rows * 128 - rows.shape[1])))
-        few = jnp.concatenate(
-            [padded.reshape(slices, table_rows, 128), packed_rows.reshape(slices, small_rows, 128)], axis=1
+        few_rows = -(-rows.shape[1] // 1024) * 8
+        few = jnp.pad(rows, ((0, 0), (0, few_rows * 128 - rows.shape[1]))).reshape(slices, few_rows, 128)
+        wide_all, slim_all, both_all, ffn_all, conv_all, table_all, pos_all, few = epilogue_call(
+            d_partial,
+            d_in,
+            ids,
+            embed,
+            lse,
+            weight,
+            back,
+            limit,
+            count,
+            grad_highway.reshape(4, 2, -1, 2 * filters),
+            grad_qkv.reshape(4, 2, -1, 3 * width),
+            grad_both.reshape(4, 2, -1, dmodel),
+            grad_ffn,
+            grad_pos.reshape(slices, -1, 128),
+            few,
+            letters,
+            depth,
+            groups,
+            6,
         )
-        conv_rows = filters // slices
-        many = jnp.concatenate(
-            [conv_sums.reshape(slices, conv_rows, 128), grad_pos.reshape(slices, -1, 128)], axis=1
-        )
-        many, few = total_all_call(many, few, 7)
-        conv_all = many[:, :conv_rows].reshape(filters, 128).astype(jnp.float32)
-        grad_pos = many[:, conv_rows:].reshape(grad_pos.shape).astype(jnp.float32)
-        table_all = few[:, :table_rows].reshape(-1, 128)[: table_sums.shape[0]].astype(jnp.float32)
-        own = lax.dynamic_index_in_dim(few[:, table_rows:].reshape(slices, -1), slot, 0, keepdims=False)
+        conv_all = conv_all.reshape(filters, 128).astype(jnp.float32)
+        grad_pos = pos_all.reshape(grad_pos.shape).astype(jnp.float32)
+        table_all = table_all.reshape(-1, 128)[: groups * depth].astype(jnp.float32)
+        own = lax.dynamic_index_in_dim(few.reshape(slices, -1), slot, 0, keepdims=False)
         own = own[: rows.shape[1]].astype(jnp.float32)
     else:
+        d_features = scatter_channels_call(d_partial, d_in, 6)
+        conv_sums, table_sums = conv_backward_call(
+            ids, embed, lse, d_features, weight, back, limit, count, groups, letters, depth
+        )
+        wide_all = jnp.stack(join_parts(reduce_rows(grad_highway)))
+        slim_all = jnp.stack(join_parts(reduce_rows(grad_qkv)))
+        both_all = jnp.stack(join_parts(reduce_rows(grad_both.reshape(-1, dmodel))))
+        ffn_all = jnp.stack(join_parts(reduce_rows(grad_ffn.reshape(-1, dmodel))))
+        table_sums = table_sums.reshape(2, groups * depth, -1).sum(0)
         conv_all = lax.psum(conv_sums, "dp")
         table_all, sums = lax.psum((table_sums, rows), ("dp", "filt"))
         grad_pos = lax.psum(grad_pos, "dp")
@@ -1269,20 +1330,29 @@
     conv_grad_b = conv_all[:, tap_rows]
     g_table = table_all.reshape(groups, depth, 128).transpose(0, 2, 1).reshape(-1, depth)
     g_table = g_table[: char_table.shape[0]]
-
     g_highway_b, g_proj_b, g_gain, g_shift, g_inner_b = jnp.split(own, cuts)
 
-    def join_columns(array, blocks, rows_here):
-        split = array.reshape(parts, rows_here, blocks, -1).transpose(1, 2, 0, 3)
-        return split.reshape(rows_here, -1).astype(jnp.float32)
-
-    g_outer = ffn_all[:, inner_rows:].reshape(-1, dmodel).astype(jnp.float32)
-    g_inner = join_columns(ffn_all[:, :inner_rows], slices, inner_rows)
-    slim_list = jnp.split(slim_all, slim_cuts[:2], axis=1)
-    g_qkv = join_columns(slim_list[0], 3, query_key_value_weight.shape[0])
-    g_proj = join_columns(slim_list[1], 1, proj_weight.shape[0])
-    g_out = join_columns(slim_list[2], 1, attention_output_weight.shape[0])
-    g_highway = join_columns(wide_all, 2, highway_weight.shape[1])
+    if fast:
+        g_highway, g_qkv, g_proj, g_out, g_inner, g_outer = assemble_call(
+            wide_all, slim_all, both_all, ffn_all, inner_rows, attention_output_weight.shape[0]
+        )
+    else:
+
+        def join_columns(array, blocks, rows_here):
+            split = array.reshape(parts, rows_here, blocks, -1).transpose(1, 2, 0, 3)
+            return split.reshape(rows_here, -1).astype(jnp.float32)
+
+        def join_groups(array):
+            split = array.reshape(parts, array.shape[1], parts, width).transpose(2, 1, 0, 3)
+            return split.reshape(-1, dmodel).astype(jnp.float32)
+
+        split = proj_weight.shape[0] // parts
+        g_outer = ffn_all[:, inner_rows:].reshape(-1, dmodel).astype(jnp.float32)
+        g_inner = join_columns(ffn_all[:, :inner_rows], slices, inner_rows)
+        g_qkv = join_columns(slim_all, 3, query_key_value_weight.shape[0])
+        g_proj = join_groups(both_all[:, :split])
+        g_out = join_groups(both_all[:, split:])
+        g_highway = join_columns(wide_all, 2, highway_weight.shape[1])
     return (
         encoded,
         g_table,

time: 543 us -> 481 us (0.89)
  waiting for transfers between devices: 28.8 us -> 3.88 us
  local copies, waits for them, and re-layouts: 81.5 us -> 61.7 us
  Pallas kernels: 326 us -> 316 us
  other arithmetic: 26.9 us -> 19.9 us
    all_gather x1, waiting for transfers between devices: 28.7 us -> 0.01 us  [per_device(): ffn_all = lax.all_gather(ffn_own, 'dp', axis=0, tiled=False)]
    convert_element_type x17 -> x3, local copies, waits for them, and re-layouts: 32.1 us -> 4.46 us  [the longest x1 2.61 us: per_device(): grad_qkv = tn_dot(first_all, d_packed).astype(jnp.bfloat16)]
    pallas_call x4 -> x3, Pallas kernels: 82.5 us -> 55.5 us  [comm_call(): pl.pallas_call(kernel, out_shape=out_shape, in_specs=[vmem] * len(args),...]
    reshape x2 -> x10, local copies, waits for them, and re-layouts: 2.4 us -> 19.9 us  [the longest x4 7.12 us: columns_from_rows(): item.astype(jnp.bfloat16).reshape(slices // parts, parts, -1, parts, width)]
    pallas_call x1 -> x2, Pallas kernels: 108 us -> 120 us  [the longest x1 116 us: epilogue_call(): pl.pallas_call(functools.partial(epilogue, letters, depth, block), in_spe...]
    convert_element_type x6 -> x1, other arithmetic: 7.54 us -> 0.92 us  [per_device(): conv_all = conv_all.reshape(filters, 128).astype(jnp.float32)]
    unnamed x173 -> x120, local copies, waits for them, and re-layouts: 13.9 us -> 13.2 us
  transfers between devices with their start and end apart: 4 -> 4, of which waited for: 1 -> 1; matrix products, arithmetic and copies ran while one was open for 8% -> 12% of each run, Pallas kernels for 16% -> 26%
where the time goes in v1:
time: 481 us; the launch traced here: 474 us
  Pallas kernels  316 us (66%)
  local copies, waits for them, and re-layouts  61.7 us (13%)
  matrix products  48 us (10%)
  other arithmetic  19.9 us (4%)
  between operations  16.2 us (3%)
  starting transfers between devices  8.97 us (2%)
    pallas_call x1, Pallas kernels, epilogue_call(): pl.pallas_call(functools.partial(epilogue, letters, depth, block), in_spe...  116 us
    pallas_call x1, Pallas kernels, prologue_call(): pl.pallas_call(functools.partial(prologue, letters, depth, block, chunks,...  83.9 us
    pallas_call x2, Pallas kernels, backward_stage_call(): pl.pallas_call(functools.partial(backward_stage, kind), out_shape=out_sha...  56.4 us
    pallas_call x3, Pallas kernels, comm_call(): pl.pallas_call(kernel, out_shape=out_shape, in_specs=[vmem] * len(args),...  55.5 us
    dot_general x7, matrix products, nn_dot(): return jnp.dot(left, right, preferred_element_type=jnp.float32)  17.7 us
    dot_general x6, matrix products, tn_dot(): lax.dot_general(left, right, (((0,), (0,)), ((), ())), preferred_element_...  13.4 us
    unnamed x120, local copies, waits for them, and re-layouts  13.2 us
    dot_general x7, matrix products, nt_dot(): lax.dot_general(left, right, (((1,), (1,)), ((), ())), preferred_element_...  13.1 us
  transfers between devices with their start and end apart: 4, of which 1 were waited for; matrix products, arithmetic and copies ran while one was open for 12% of the time, Pallas kernels for 26%

profile of v1, /device:TPU:0, one launch (start us, length us, event | category | flops | bytes accessed | tf_op | source)
XLA Modules:
  0.0 474.5 jit_solution(14065269980204006154)
XLA Ops:
  16.4 83.9 %prologue.1 = (bf16[512,512]{1,0:T(8,128)(2,1)S(1)}, f32[512,512]{1,0:T(8,128)S(1)}, bf16[800,512]{1,0:T(8,128)(2,1)S(1)}, bf16[512,2048]{1,0:T(8,128)(2,1)S(1)}, bf16[2,4,2,256,512]{4,3,2,1,0:T(8,128)(2,1)}) custom-call(s32[56,512]{1,0:T(8,128)S(1)} %pad_bitcast_fusion.chars_ref.refs_2_, bf16[48,128]{1,0:T(8,128)(2,1)S(1)} %bitcast.182, ...), custom_call_target="tpu_custom_call" | custom-call | tf_op jit(solution)/shard_map/prologue/pallas_call | solution.py:659
  104.5 2.6 fusion.49
  108.6 2.2 fusion.54
  112.6 2.3 slice.151
  114.9 4.6 all-to-all-start
  120.0 2.4 reshape.503
  123.0 3.0 maximum_add_fusion
  126.0 4.7 fusion.14
  130.6 3.8 all-to-all-done
  134.4 3.3 reshape.497
  138.1 2.3 copy.136
  140.4 3.4 reshape.498
  144.6 2.0 convolution_convert_fusion.9
  146.6 18.1 %forward_stage.2 = (f32[128,768]{1,0:T(8,128)S(1)}, f32[128,768]{1,0:T(8,128)S(1)}, f32[128,1]{1,0:T(8,128)S(1)}, bf16[4,128,768]{2,1,0:T(8,128)(2,1)S(1)}) custom-call(bf16[4,128,768]{2,1,0:T(8,128)(2,1)S(1)} %bitcast.176, f32[128,768]{1,0:T(8,128)S(1)} %convert_add_fusion.1.base_ref, f32[1,768]{1,0:T(1,128)S(1)} %slice.121.gain_ref, ...), custom_call_target="tpu_custom_call" | custom-call | tf_op jit(solution)/shard_map/forward_stage/pallas_call | solution.py:217
  169.8 19.3 %forward_stage.3 = (f32[128,768]{1,0:T(8,128)S(1)}, f32[128,768]{1,0:T(8,128)S(1)}, f32[128,1]{1,0:T(8,128)S(1)}, bf16[4,128,768]{2,1,0:T(8,128)(2,1)S(1)}) custom-call(bf16[4,128,768]{2,1,0:T(8,128)(2,1)S(1)} %bitcast.175, f32[128,768]{1,0:T(8,128)S(1)} %get-tuple-element.68.base_ref, f32[1,768]{1,0:T(1,128)S(1)} %slice.130.gain_ref, ...), custom_call_target="tpu_custom_call" | custom-call | tf_op jit(solution)/shard_map/forward_stage/pallas_call | solution.py:217
  191.8 10.4 %multiply_convert_fusion.1 = (bf16[512,768]{1,0:T(8,128)(2,1)S(1)}, f32[512,768]{1,0:T(8,128)S(1)}, f32[512,768]{1,0:T(8,128)S(1)}) fusion(f32[768]{0:T(1024)S(1)} %add.276, bf16[512,768]{1,0:T(8,128)(2,1)S(1)} %bitcast.185, bf16[768,768]{1,0:T(8,128)(2,1)S(1)} %bitcast.218), kind=kOutput, calls=%fused_computation.21 | convolution fusion | flops 629932032 | bytes 5901312 | tf_op jit(solution)/shard_map/dot_general | solution.py:21
  203.2 18.1 %top_stage.1 = (bf16[128,768]{1,0:T(8,128)(2,1)S(1)}, f32[128,768]{1,0:T(8,128)S(1)}, f32[1,768]{1,0:T(1,128)S(1)}, f32[1,768]{1,0:T(1,128)S(1)}, bf16[4,128,768]{2,1,0:T(8,128)(2,1)S(1)}) custom-call(bf16[4,128,768]{2,1,0:T(8,128)(2,1)S(1)} %bitcast.178, f32[128,768]{1,0:T(8,128)S(1)} %get-tuple-element.72.base_ref, bf16[128,768]{1,0:T(8,128)(2,1)S(1)} %bitcast.181, ...), custom_call_target="tpu_custom_call" | custom-call | tf_op jit(solution)/shard_map/top_stage/pallas_call | solution.py:217
  225.1 29.2 %backward_stage.2 = (f32[128,768]{1,0:T(8,128)S(1)}, f32[1,768]{1,0:T(1,128)S(1)}, f32[1,768]{1,0:T(1,128)S(1)}, f32[1,768]{1,0:T(1,128)}, bf16[4,128,768]{2,1,0...) custom-call(bf16[4,128,768]{2,1,0:T(8,128)(2,1)S(1)} %bitcast.179, f32[128,768]{1,0:T(8,128)S(1)} %get-tuple-element.75.base_ref, ...), custom_call_target="tpu_custom_call" | custom-call | tf_op jit(solution)/shard_map/backward_stage/pallas_call | solution.py:357
  262.7 27.2 %backward_stage.3 = (f32[128,768]{1,0:T(8,128)S(1)}, f32[1,768]{1,0:T(1,128)S(1)}, f32[1,768]{1,0:T(1,128)S(1)}, f32[1,768]{1,0:T(1,128)S(1)}, bf16[4,128,768]{2...) custom-call(bf16[4,128,768]{2,1,0:T(8,128)(2,1)S(1)} %bitcast.177, f32[128,768]{1,0:T(8,128)S(1)} %get-tuple-element.79.base_ref, ...), custom_call_target="tpu_custom_call" | custom-call | tf_op jit(solution)/shard_map/backward_stage/pallas_call | solution.py:357
  291.2 2.9 convolution_convert_fusion.6
  294.1 4.1 multiply_add_fusion
  300.0 3.4 reshape.527
  303.4 3.0 copy.178
  306.5 3.0 reshape.528
  310.5 2.2 pad_maximum_fusion.1
  312.7 4.3 all-to-all-start.1
  317.0 3.2 fusion.28
  320.2 2.6 add_convert_fusion.refs_0_
  323.5 2.6 copy.145
  327.8 6.2 %convolution_convert_fusion = bf16[2048,1024]{1,0:T(8,128)(2,1)} fusion(bf16[512,2048]{1,0:T(8,128)(2,1)} %copy-done.15, bf16[512,1024]{1,0:T(8,128)(2,1)} %get-tuple-element.121), kind=kOutput, calls=%fused_computation.1 | convolution fusion | flops 2149580800 | bytes 7340032 | tf_op jit(solution)/shard_map/dot_general | solution.py:993
  334.0 116.3 %epilogue.1 = (bf16[4,256,1024]{2,1,0:T(8,128)(2,1)}, bf16[4,96,576]{2,1,0:T(8,128)(2,1)}, bf16[4,88,768]{2,1,0:T(8,128)(2,1)}, bf16[4,192,768]{2,1,0:T(8,128)(2...) custom-call(bf16[512,2048]{1,0:T(8,128)(2,1)} %add_convert_fusion.re, ...), custom_call_target="tpu_custom_call" | custom-call | tf_op jit(solution)/shard_map/epilogue/pallas_call | solution.py:916
  462.9 3.9 assemble.1
  (255 shorter events, 57.9 us)
Async XLA Ops:
  7.2 95.1 %copy-start = (bf16[384,768]{1,0:T(8,128)(2,1)S(1)}, bf16[384,768]{1,0:T(8,128)(2,1)}, u32[]{:S(2)}) copy-start(bf16[384,768]{1,0:T(8,128)(2,1)} %param.34) | copy-start | bytes 1769476
  7.2 3.0 copy-start.42
  7.2 104.3 %all-gather.8.cloned.1.call-start = ((), (), s32[]{:S(2)}) async-start(), calls=%async_computation.3 | async-start | bytes 2322432 | tf_op jit(solution)/shard_map/all_gather | solution.py:1120
  7.3 3.5 copy-start.44
  10.4 3.2 copy-start.46
  10.4 3.3 copy-start.47
  10.4 3.3 copy-start.41
  12.5 177.5 %all-gather.6.cloned.1.call-start = ((), (), s32[]{:S(2)}) async-start(), calls=%async_computation.2 | async-start | bytes 2654208 | tf_op jit(solution)/shard_map/all_gather | solution.py:1159
  13.7 2.7 copy-start.5
  16.0 84.3 %copy-start.8 = (s32[56,512]{1,0:T(8,128)}, s32[56,512]{1,0:T(8,128)S(1)}, u32[]{:S(2)}) copy-start(s32[56,512]{1,0:T(8,128)S(1)} %pad_bitcast_fusion.chars_ref.refs_2_) | copy-start | bytes 344068
  16.2 84.1 %copy-start.2 = (s32[512,1]{1,0:T(8,128)}, s32[512,1]{1,0:T(8,128)S(1)}, u32[]{:S(2)}) copy-start(s32[512,1]{1,0:T(8,128)S(1)} %broadcast_subtract_fusion.limit_ref.refs_7_) | copy-start | bytes 6148
  16.4 85.9 %copy-start.3 = (f32[512,1]{1,0:T(8,128)}, f32[512,1]{1,0:T(8,128)S(1)}, u32[]{:S(2)}) copy-start(f32[512,1]{1,0:T(8,128)S(1)} %convert_log_fusion.count_ref.refs_8_) | copy-start | bytes 6148
  104.5 2.9 copy-start.16
  107.1 3.7 copy-start.27
  114.9 5.1 %slice-start = ((bf16[8,163,768]{2,1,0:T(8,128)(2,1)}), bf16[8,72,768]{2,1,0:T(8,128)(2,1)S(1)}, s32[]{:S(2)}) async-start(bf16[8,163,768]{2,1,0:T(8,128)(2,1)} %all-gather.8.cloned.1.call-done), calls=%async_computation.4 | async-start | bytes 1769472 | tf_op jit(solution)/shard_map/slice | solution.py:1121
  114.9 19.5 %all-to-all-start = ((bf16[4,176,768]{2,1,0:T(8,128)(2,1)}), bf16[4,176,768]{2,1,0:T(8,128)(2,1)}, u32[]{:S(2)}, u32[]{:S(2)}) async-start(bf16[4,176,768]{2,1,0:T(8,128)(2,1)} %bitcast.11), calls=%async_computation | async-start | bytes 2162688 | tf_op jit(solution)/shard_map/all_to_all | solution.py:1079
  123.0 3.0 copy-start.43
  144.6 20.1 %copy-start.39 = (bf16[768,576]{1,0:T(8,128)(2,1)S(1)}, bf16[768,576]{1,0:T(8,128)(2,1)}, u32[]{:S(2)}) copy-start(bf16[768,576]{1,0:T(8,128)(2,1)} %reshape.503) | copy-start | bytes 2654212
  165.4 3.1 copy-start.35
  225.1 29.7 %copy-start.22 = (f32[3,512,512]{1,2,0:T(8,128)S(1)}, f32[3,512,512]{1,2,0:T(8,128)}, u32[]{:S(2)}) copy-start(f32[3,512,512]{1,2,0:T(8,128)} %copy-done.21) | copy-start | bytes 9437188
  225.1 29.7 %copy-start.36 = (bf16[512,192]{0,1:T(8,128)(2,1)S(1)}, bf16[512,192]{0,1:T(8,128)(2,1)}, u32[]{:S(2)}) copy-start(bf16[512,192]{0,1:T(8,128)(2,1)} %copy-done.35) | copy-start | bytes 589828
  291.2 2.9 copy-start.20
  291.2 2.9 copy-start.38
  303.4 6.0 %copy-start.37 = (bf16[192,768]{1,0:T(8,128)(2,1)S(1)}, bf16[192,768]{1,0:T(8,128)(2,1)}, u32[]{:S(2)}) copy-start(bf16[192,768]{1,0:T(8,128)(2,1)} %convolution_convert_fusion.11) | copy-start | bytes 884740
  312.7 21.4 %all-to-all-start.1 = ((bf16[4,176,768]{2,1,0:T(8,128)(2,1)}), bf16[4,176,768]{2,1,0:T(8,128)(2,1)}, u32[]{:S(2)}, u32[]{:S(2)}) async-start(bf16[4,176,768]{2,1,0:T(8,128)(2,1)} %bitcast.199), calls=%async_computation.1 | async-start | bytes 2162688 | tf_op jit(solution)/shard_map/all_to_all | solution.py:1092
  316.9 3.2 copy-start.26
  316.9 3.2 copy-start.28
  450.3 8.2 %copy-start.48 = (bf16[8,8,128]{2,1,0:T(8,128)(2,1)S(1)}, bf16[8,8,128]{2,1,0:T(8,128)(2,1)}, u32[]{:S(2)}) copy-start(bf16[8,8,128]{2,1,0:T(8,128)(2,1)} %get-tuple-element.96) | copy-start | bytes 49156
  450.3 10.2 %copy-start.4 = (bf16[4,256,1024]{2,1,0:T(8,128)(2,1)S(1)}, bf16[4,256,1024]{2,1,0:T(8,128)(2,1)}, u32[]{:S(2)}) copy-start(bf16[4,256,1024]{2,1,0:T(8,128)(2,1)} %get-tuple-element.98.wide_ref) | copy-start | bytes 6291460
  450.3 10.2 %copy-start.10 = (bf16[4,88,768]{2,1,0:T(8,128)(2,1)S(1)}, bf16[4,88,768]{2,1,0:T(8,128)(2,1)}, u32[]{:S(2)}) copy-start(bf16[4,88,768]{2,1,0:T(8,128)(2,1)} %get-tuple-element.100.both_ref) | copy-start | bytes 1622020
  460.5 6.9 %copy-start.1 = (bf16[384,768]{1,0:T(8,128)(2,1)S(1)}, bf16[384,768]{1,0:T(8,128)(2,1)}, u32[]{:S(2)}) copy-start(bf16[384,768]{1,0:T(8,128)(2,1)} %param.34) | copy-start | bytes 1769476
  462.9 3.9 copy-start.13
  (28 other events, 42.1 us)
Sparse Core Ops, SparseCore 0:
  12.6 78.2 all-gather.7
  104.5 55.9 all-gather.5

commit v2 on v1

--- a/solution.py
+++ b/solution.py
@@ -16,6 +16,9 @@
 
 def nt_dot(left, right):
     return lax.dot_general(left, right, (((1,), (1,)), ((), ())), preferred_element_type=jnp.float32)
+
+def tn_dot(left, right):
+    return lax.dot_general(left, right, (((0,), (0,)), ((), ())), preferred_element_type=jnp.float32)
 
 def nn_dot(left, right):
     return jnp.dot(left, right, preferred_element_type=jnp.float32)
@@ -282,29 +285,6 @@
     down_ref[...] = down
     gather_blocks(down.astype(jnp.bfloat16), all_ref, send.at[pl.ds(3, 3)], recv.at[pl.ds(3, 3)], me)
 
-def backward_stage(kind, part_ref, base_ref, unit_ref, scale_ref, gain_ref, *refs):
-    job_in, job_out, job_send, job_recv = None, None, None, None
-    if kind is not None:
-        (job_in, down_ref, dgain_ref, dshift_ref, dlow_ref, all_ref, job_out, inbox, send, recv, job_send, job_recv) = refs
-    else:
-        (down_ref, dgain_ref, dshift_ref, dlow_ref, all_ref, inbox, send, recv) = refs
-    me = lax.axis_index("filt")
-    slot = lax.axis_index("dp")
-    others = [] if kind is None else [{"dp": slot ^ hop} for hop in job_hops(kind)]
-    greet([{"filt": me ^ hop} for hop in (1, 2, 3)] + others)
-    copies = [] if kind is None else start_job(kind, job_in, job_out, job_send, job_recv)
-    up = scatter_sum(part_ref, inbox, send, recv, me) + base_ref[...]
-    unit = unit_ref[...]
-    dgain_ref[...] = jnp.sum(up * unit, axis=0, keepdims=True)
-    dshift_ref[...] = jnp.sum(up, axis=0, keepdims=True)
-    down = norm_back(up, unit, scale_ref[...], gain_ref[...])
-    down_ref[...] = down
-    low = down.astype(jnp.bfloat16)
-    dlow_ref[...] = jnp.sum(low.astype(jnp.float32), axis=0, keepdims=True)
-    gather_blocks(low, all_ref, send.at[pl.ds(3, 3)], recv.at[pl.ds(3, 3)], me)
-    for copy in copies:
-        copy.wait()
-
 def start_job(kind, source, target, send, recv):
     slot = lax.axis_index("dp")
     ring, side = slot // 2, slot % 2
@@ -322,6 +302,31 @@
 def job_hops(kind):
     return (1,) if kind == "side" else (2, 4, 6)
 
+def backward_stage(kinds, part_ref, base_ref, unit_ref, scale_ref, gain_ref, *refs):
+    many = len(kinds)
+    job_in, refs = refs[:many], refs[many:]
+    (down_ref, dgain_ref, dshift_ref, dlow_ref, all_ref), refs = refs[:5], refs[5:]
+    job_out, refs = refs[:many], refs[many:]
+    inbox, send, recv = refs[:3]
+    me = lax.axis_index("filt")
+    slot = lax.axis_index("dp")
+    hops = sorted({hop for kind in kinds for hop in job_hops(kind)})
+    greet([{"filt": me ^ hop} for hop in (1, 2, 3)] + [{"dp": slot ^ hop} for hop in hops])
+    copies = []
+    for index, kind in enumerate(kinds):
+        copies += start_job(kind, job_in[index], job_out[index], refs[3].at[index], refs[4].at[index])
+    up = scatter_sum(part_ref, inbox, send, recv, me) + base_ref[...]
+    unit = unit_ref[...]
+    dgain_ref[...] = jnp.sum(up * unit, axis=0, keepdims=True)
+    dshift_ref[...] = jnp.sum(up, axis=0, keepdims=True)
+    down = norm_back(up, unit, scale_ref[...], gain_ref[...])
+    down_ref[...] = down
+    low = down.astype(jnp.bfloat16)
+    dlow_ref[...] = jnp.sum(low.astype(jnp.float32), axis=0, keepdims=True)
+    gather_blocks(low, all_ref, send.at[pl.ds(3, 3)], recv.at[pl.ds(3, 3)], me)
+    for copy in copies:
+        copy.wait()
+
 def stage_scratch(block):
     return [pltpu.VMEM((3,) + block, jnp.bfloat16), DMA((6,)), DMA((6,))]
 
@@ -340,25 +345,22 @@
         (bf16(rows, cols), f32(rows, cols), f32(1, cols), f32(1, cols), bf16(parts, rows, cols)), stage_scratch((rows, cols)), ident,
         part, base, up, gain, shift, name="top_stage")
 
-def backward_stage_call(part, base, unit, scale, gain, ident, kind=None, job=None):
+def backward_stage_call(part, base, unit, scale, gain, ident, kinds=(), jobs=()):
     parts, rows, cols = part.shape
     vmem = pl.BlockSpec(memory_space=pltpu.VMEM)
     hbm = pl.BlockSpec(memory_space=pl.ANY)
-    args = (part, base, unit, scale, gain)
     out_shape = [f32(rows, cols), f32(1, cols), f32(1, cols), f32(1, cols), bf16(parts, rows, cols)]
-    in_specs, out_specs, scratch = [vmem] * 5, [vmem] * 5, stage_scratch((rows, cols))
-    if kind is not None:
+    scratch = stage_scratch((rows, cols))
+    for kind, job in zip(kinds, jobs):
         ring = job.shape[0]
-        args += (job,)
-        in_specs.append(hbm)
-        out_specs.append(hbm)
         out_shape.append(bf16(ring, *job.shape[2:]) if kind == "side" else bf16(ring - 1, *job.shape[1:]))
-        scratch += [DMA((3,)), DMA((3,))]
+    if kinds:
+        scratch += [DMA((len(kinds), 3)), DMA((len(kinds), 3))]
     return pl.pallas_call(
-        functools.partial(backward_stage, kind), out_shape=out_shape, in_specs=in_specs, out_specs=out_specs,
-        scratch_shapes=scratch,
+        functools.partial(backward_stage, kinds), out_shape=out_shape, in_specs=[vmem] * 5 + [hbm] * len(kinds),
+        out_specs=[vmem] * 5 + [hbm] * len(kinds), scratch_shapes=scratch,
         compiler_params=pltpu.CompilerParams(collective_id=ident, has_side_effects=True, vmem_limit_bytes=24 << 20),
-        name="backward_stage")(*args)
+        name="backward_stage")(part, base, unit, scale, gain, *jobs)
 
 def gather_channels(own_ref, all_ref, send, recv, *, chunks):
     me = lax.axis_index("filt")
@@ -669,8 +671,156 @@
     )(ids, table, weight, limit, count, shard)
 
 
+def sigmoid(values):
+    return 1.0 / (1.0 + jnp.exp(-values))
+
+
+def highway_stage(eps, slim_ref, feats_ref, wide_ref, bias_ref, acts_ref, base_ref, gain_ref, shift_ref,
+                  gates_ref, hidden_ref, proj_ref, out_ref, value_ref, unit_ref, scale_ref, all_ref,
+                  abox, part_ref, inbox, send, recv, asend, arecv):
+    me = lax.axis_index("filt")
+    greet([{"filt": me ^ hop} for hop in (1, 2, 3)])
+    parts, sides, rows, dmodel = abox.shape
+    copies = []
+    for hop in (2, 3, 1):
+        source = slim_ref.at[pl.ds(sides * (me ^ hop), sides), pl.ds(0, rows), :]
+        copy = remote(source, abox.at[me], asend.at[hop - 1], arecv.at[hop - 1], {"filt": me ^ hop})
+        copy.start()
+        copies.append(copy)
+    own = pltpu.make_async_copy(slim_ref.at[pl.ds(sides * me, sides), pl.ds(0, rows), :], abox.at[me], asend.at[3])
+    own.start()
+    words, filters = acts_ref.shape
+    block = 256
+
+    def mix(index, carry):
+        span = pl.ds(pl.multiple_of(index * block, block), block)
+        feats = feats_ref[span, :]
+        turn = nn_dot(feats, wide_ref[0]) + bias_ref[:, :filters]
+        gates_ref[span, :filters] = turn
+        gate = nn_dot(feats, wide_ref[1]) + bias_ref[:, filters:]
+        gates_ref[span, filters:] = gate
+        keep = sigmoid(gate)
+        mixed = keep * acts_ref[span, :].astype(jnp.float32) + (1.0 - keep) * (turn * normal_cdf(turn))
+        hidden_ref[span, :] = mixed.astype(jnp.bfloat16)
+        return carry
+
+    lax.fori_loop(0, words // block, mix, 0)
+    own.wait()
+    for copy in copies:
+        copy.wait()
+    width = dmodel // parts
+    size, small = proj_ref.shape[0] // (sides * parts), out_ref.shape[0] // (sides * (parts - 1))
+    for part in range(parts):
+        cols = slice(part * width, (part + 1) * width)
+        for side in range(sides):
+            for group in range(parts):
+                lanes = slice(group * width, (group + 1) * width)
+                start = (side * parts + group) * size
+                proj_ref[start : start + size, cols] = abox[part, side, :size, lanes]
+                if group < parts - 1:
+                    start = (side * (parts - 1) + group) * small
+                    out_ref[start : start + small, cols] = abox[part, side, size:, lanes]
+
+    def project(index, carry):
+        span = pl.ds(pl.multiple_of(index * 128, 128), 128)
+        part_ref[index] = nn_dot(hidden_ref[span, :], proj_ref[...]).astype(jnp.bfloat16)
+        return carry
+
+    lax.fori_loop(0, parts, project, 0)
+    total = scatter_sum(part_ref, inbox, send, recv, me) + base_ref[...]
+    value, unit, scale = norm(total, gain_ref[...], shift_ref[...], eps)
+    value_ref[...] = value
+    unit_ref[...] = unit
+    scale_ref[...] = scale
+    gather_blocks(value.astype(jnp.bfloat16), all_ref, send.at[pl.ds(3, 3)], recv.at[pl.ds(3, 3)], me)
+
+
+def highway_stage_call(slim, feats, wide, bias, acts, base, gain, shift, out_rows, po_rows, eps, ident):
+    words, filters = acts.shape
+    rows, dmodel = base.shape
+    parts = words // rows
+    vmem = pl.BlockSpec(memory_space=pltpu.VMEM)
+    hbm = pl.BlockSpec(memory_space=pl.ANY)
+    return pl.pallas_call(
+        functools.partial(highway_stage, eps), in_specs=[hbm] + [vmem] * 7, out_specs=[vmem] * 8,
+        out_shape=[f32(words, 2 * filters), bf16(words, filters), bf16(filters, dmodel), bf16(out_rows, dmodel), f32(rows, dmodel),
+                   f32(rows, dmodel), f32(rows, 1), bf16(parts, rows, dmodel)],
+        scratch_shapes=[pltpu.VMEM((parts, 2, po_rows, dmodel), jnp.bfloat16), pltpu.VMEM((parts, rows, dmodel), jnp.bfloat16)]
+        + stage_scratch((rows, dmodel)) + [DMA((4,)), DMA((3,))],
+        compiler_params=pltpu.CompilerParams(collective_id=ident, has_side_effects=True, vmem_limit_bytes=48 << 20),
+        name="highway_stage",
+    )(slim, feats, wide, bias, acts, base, gain, shift)
+
+
+def highway_back(dproj_ref, proj_ref, hidden_ref, gates_ref, acts_ref, feats_ref, wide_ref, attended_ref, dmixed_ref,
+                 part_ref, din_ref, grad_ref, both_ref, bias_ref, dgates_ref):
+    words, filters = acts_ref.shape
+    block = 128
+    bias_ref[...] = jnp.zeros(bias_ref.shape, jnp.float32)
+
+    def mix(index, carry):
+        span = pl.ds(pl.multiple_of(index * block, block), block)
+        dhidden = nt_dot(dproj_ref[span, :], proj_ref[...])
+        turn = gates_ref[span, :filters]
+        keep = sigmoid(gates_ref[span, filters:])
+        below = normal_cdf(turn)
+        slope = below + turn * (DENSITY * jnp.exp(-0.5 * turn * turn))
+        fresh = dhidden * (1.0 - keep)
+        din_ref[span, :] = dhidden * keep
+        dturn = (fresh * slope).astype(jnp.bfloat16)
+        dkeep = (fresh * keep * (acts_ref[span, :].astype(jnp.float32) - turn * below)).astype(jnp.bfloat16)
+        dgates_ref[span, :filters] = dturn
+        dgates_ref[span, filters:] = dkeep
+        bias_ref[:, :filters] += jnp.sum(dturn.astype(jnp.float32), axis=0, keepdims=True)
+        bias_ref[:, filters:] += jnp.sum(dkeep.astype(jnp.float32), axis=0, keepdims=True)
+        return carry
+
+    lax.fori_loop(0, words // block, mix, 0)
+    piece = 512
+
+    def grads(index, carry):
+        cols = pl.ds(pl.multiple_of(index * piece, piece), piece)
+        grad_ref[cols, :] = tn_dot(feats_ref[:, cols], dgates_ref[...]).astype(jnp.bfloat16)
+        down = nt_dot(dgates_ref[:, :filters], wide_ref[0, cols, :]) + nt_dot(dgates_ref[:, filters:], wide_ref[1, cols, :])
+        part_ref[:, cols] = down.astype(jnp.bfloat16)
+        return carry
+
+    lax.fori_loop(0, feats_ref.shape[1] // piece, grads, 0)
+    parts, sides, rows, dmodel = both_ref.shape
+    width = dmodel // parts
+    gproj = tn_dot(hidden_ref[...], dproj_ref[...]).astype(jnp.bfloat16)
+    gout = tn_dot(attended_ref[...], dmixed_ref[...]).astype(jnp.bfloat16)
+    size, small = gproj.shape[0] // (sides * parts), gout.shape[0] // (sides * (parts - 1))
+    for part in range(parts):
+        cols = slice(part * width, (part + 1) * width)
+        for side in range(sides):
+            for group in range(parts):
+                lanes = slice(group * width, (group + 1) * width)
+                start = (side * parts + group) * size
+                both_ref[part, side, :size, lanes] = gproj[start : start + size, cols]
+                if group < parts - 1:
+                    start = (side * (parts - 1) + group) * small
+                    both_ref[part, side, size:, lanes] = gout[start : start + small, cols]
+                else:
+                    both_ref[part, side, size:, lanes] = jnp.zeros((rows - size, width), jnp.bfloat16)
+
+
+def highway_back_call(dproj, proj, hidden, gates, acts, feats, wide, attended, dmixed, parts, po_rows):
+    words, filters = acts.shape
+    dmodel = dproj.shape[1]
+    vmem = pl.BlockSpec(memory_space=pltpu.VMEM)
+    return pl.pallas_call(
+        highway_back, in_specs=[vmem] * 9, out_specs=[vmem] * 5,
+        out_shape=[bf16(words, feats.shape[1]), f32(words, filters), bf16(feats.shape[1], 2 * filters), bf16(parts, 2, po_rows, dmodel), f32(1, 2 * filters)],
+        scratch_shapes=[pltpu.VMEM((words, 2 * filters), jnp.bfloat16)],
+        compiler_params=pltpu.CompilerParams(vmem_limit_bytes=56 << 20), name="highway_back",
+        cost_estimate=pl.CostEstimate(flops=5_200_000_000, bytes_accessed=20_000_000, transcendentals=1_000_000),
+    )(dproj, proj, hidden, gates, acts, feats, wide, attended, dmixed)
+
+
 class RowReduce:
-    def __init__(self, grad, yin, pair, zin, joined, span, sems):
+    def __init__(self, grad, yin, pair, zin, joined, span, sems, base=0):
+        self.base, self.ready, self.after = base, [], None
         self.grad, self.yin, self.pair, self.zin, self.joined = grad, yin, pair, zin, joined
         self.span, self.sems = span, sems
         self.me, self.slot = lax.axis_index("filt"), lax.axis_index("dp")
@@ -686,6 +836,8 @@
 
     def across(self):
         span = self.span
+        for copy in self.ready:
+            copy.wait_recv()
         self.first = self.push(
             self.grad.at[:, 1 - self.side, span, :], self.yin.at[:, span, :], 0, {"dp": self.slot ^ 1}
         )
@@ -697,19 +849,26 @@
             self.after.across()
         both = self.grad[:, self.side, span, :].astype(jnp.float32) + self.yin[:, span, :].astype(jnp.float32)
         self.pair[:, span, :] = both.astype(jnp.bfloat16)
+        self.ring_out()
+
+    def local(self):
+        return pl.ds(self.span.start - self.base, self.span.size)
+
+    def ring_out(self):
+        span = self.local()
         self.rest = [
             self.push(self.pair.at[self.ring ^ hop, span, :], self.zin.at[hop - 1, span, :], hop, {"dp": self.slot ^ (2 * hop)})
             for hop in (2, 3, 1)
         ]
 
     def join(self):
-        span = self.span
+        span = self.local()
         for copy in self.rest:
             copy.wait_recv()
         total = self.pair[self.ring, span, :].astype(jnp.float32)
         for hop in (1, 2, 3):
             total = total + self.zin[hop - 1, span, :].astype(jnp.float32)
-        self.joined[self.me, span, :] = total.astype(jnp.bfloat16)
+        self.joined[self.me, self.span, :] = total.astype(jnp.bfloat16)
         self.share()
 
     def share(self):
@@ -734,11 +893,11 @@
 
 def epilogue(letters, depth, block, *refs):
     (part_ref, base_ref, chars_ref, embed_ref, lse_ref, weight_ref, back_ref, limit_ref, count_ref, wide_ref, slim_ref,
-     rows_ref, ffn_ref, pos_ref, few_ref,
+     cross_ref, ffn_ref, pair_ref, pos_ref, few_ref,
      wide_out, slim_out, rows_out, ffn_out, conv_out, table_out, pos_out, few_out,
      inbox, merged, up_ref, patch_ref, down_ref, pull_ref, wgrad_ref, tgrad_ref, wide_y, wide_p, wide_z, slim_y, slim_p, slim_z,
-     rows_y, rows_p, rows_z, conv_low, conv_in, table_low, table_in, table_side, pos_low, pos_in, few_low, few_in, few_side,
-     csend, crecv, rsend, rrecv, tsend, trecv) = refs
+     rows_ref, rows_y, rows_p, rows_z, late_z, conv_low, conv_in, table_low, table_in, table_side, pos_low, pos_in, few_low, few_in, few_side,
+     csend, crecv, rsend, rrecv, tsend, trecv, asend, arecv) = refs
     me = lax.axis_index("filt")
     greet_all()
     pos = Total(pos_low, pos_in, pos_out, tsend.at[0], trecv.at[0])
@@ -752,23 +911,33 @@
         RowReduce(wide_ref, wide_y, wide_p, wide_z, wide_out, pl.ds(index * wide_rows, wide_rows), (rsend.at[index], rrecv.at[index]))
         for index in range(4)
     ]
-    ffn = RowReduce(None, None, None, None, ffn_out, pl.ds(0, ffn_out.shape[1]), (rsend.at[5], rrecv.at[5]))
+    early = ffn_ref.shape[0]
+    ffn = RowReduce(None, None, None, None, ffn_out, pl.ds(0, early), (rsend.at[5], rrecv.at[5]))
+    late = RowReduce(None, None, pair_ref, late_z, ffn_out, pl.ds(early, pair_ref.shape[1]), (rsend.at[7], rrecv.at[7]), early)
+    swaps = [
+        remote(cross_ref.at[me ^ hop], rows_ref.at[me], asend.at[hop - 1], arecv.at[hop - 1], {"filt": me ^ hop}) for hop in (2, 3, 1)
+    ]
+    both.ready = swaps
     pos.start(pos_ref[...])
     few.start(few_ref[...])
-    queue = [slim, both] + wide
+    for copy in swaps:
+        copy.start()
+    rows_ref[me] = cross_ref[me]
+    queue = [slim, wide[0], both] + wide[1:]
     for index, item in enumerate(queue):
         item.after = queue[index + AHEAD] if index + AHEAD < len(queue) else None
     for item in queue[:AHEAD]:
         item.across()
-    ffn_out[me] = ffn_ref[...]
+    ffn_out[me, :early, :] = ffn_ref[...]
+    late.ring_out()
     scatter = ChannelScatter(part_ref, base_ref, up_ref, inbox, merged, csend, crecv)
     scatter.run()
     pos.combine()
     few.combine()
     ffn.share()
     steps = iter([
-        [slim.along, ffn.relay], [], [both.along, slim.join], [slim.relay], [wide[0].along, both.join],
-        [both.relay, few.across], [wide[1].along, wide[0].join], [wide[0].relay], [], [],
+        [slim.along, ffn.relay], [late.join], [wide[0].along, slim.join], [late.relay, slim.relay], [both.along, wide[0].join],
+        [wide[0].relay, few.across], [wide[1].along, both.join], [both.relay], [], [],
     ])
 
     def advance():
@@ -844,7 +1013,9 @@
         wide[2].relay, table_total.across, wide[3].join, wide[3].relay,
     ):
         step()
-    for item in [ffn, slim, both, pos, few, conv_total, table_total] + wide:
+    for copy in swaps:
+        copy.wait_send()
+    for item in [ffn, late, slim, both, pos, few, conv_total, table_total] + wide:
         item.finish()
 
 
@@ -889,9 +1060,9 @@
             copy.wait_send()
 
 
-def epilogue_call(part, base, ids, embed, lse, weight, back, limit, count, wide, slim, both, ffn, pos, few, letters, depth, groups, ident, block=256):
+def epilogue_call(part, base, ids, embed, lse, weight, back, limit, count, wide, slim, both, ffn, pair, pos, few, letters, depth, groups, ident, block=256):
     filters, words = lse.shape
-    args = (part, base, ids, embed, lse, weight, back, limit, count, wide, slim, both, ffn, pos, few)
+    args = (part, base, ids, embed, lse, weight, back, limit, count, wide, slim, both, ffn, pair, pos, few)
     parts = part.shape[1] // filters
     slices = pos.shape[0]
     pieces = 4
@@ -911,7 +1082,7 @@
 
     conv_shape = (slices, filters // slices, 128)
     table_shape = (slices, table_size, 128)
-    out_shape = [bf16(parts, *wide.shape[2:]), bf16(parts, *slim.shape[2:]), bf16(parts, *both.shape[2:]), bf16(parts, *ffn.shape), bf16(*conv_shape), bf16(*table_shape), bf16(*pos.shape), bf16(*few.shape)]
+    out_shape = [bf16(parts, *wide.shape[2:]), bf16(parts, *slim.shape[2:]), bf16(parts, *both.shape[2:]), bf16(parts, ffn.shape[0] + pair.shape[1], ffn.shape[1]), bf16(*conv_shape), bf16(*table_shape), bf16(*pos.shape), bf16(*few.shape)]
     padded = (letters + KW - 1) * depth
     return pl.pallas_call(
         functools.partial(epilogue, letters, depth, block),
@@ -921,18 +1092,21 @@
         scratch_shapes=[space((3, words, filters)), space((words, filters)), space((words, filters)), space((padded, block)),
                         space((padded, block), jnp.float32), space((filters, block), jnp.float32),
                         space((filters, 128), jnp.float32), space((2 * groups * depth, 128), jnp.float32)]
-        + stages(wide) + stages(slim) + stages(both)
+        + stages(wide) + stages(slim) + [space(both.shape)] + stages(both) + [space((3,) + pair.shape[1:])]
         + totals(conv_shape, False) + totals(table_shape, True) + totals(pos.shape, False) + totals(few.shape, True)
-        + [DMA((3, pieces)), DMA((3, pieces)), DMA((7, 7)), DMA((7, 7)), DMA((4, 3, slices - 1)), DMA((4, 3, slices - 1))],
+        + [DMA((3, pieces)), DMA((3, pieces)), DMA((8, 7)), DMA((8, 7)), DMA((4, 3, slices - 1)), DMA((4, 3, slices - 1)),
+           DMA((3,)), DMA((3,))],
         compiler_params=pltpu.CompilerParams(collective_id=ident, has_side_effects=True, vmem_limit_bytes=56 << 20),
         name="epilogue",
     )(*args)
 
 
-def assemble(wide_ref, slim_ref, both_ref, ffn_ref, wide_out, slim_out, proj_out, out_out, inner_out, outer_out):
+def assemble(depth, wide_ref, slim_ref, both_ref, ffn_ref, conv_ref, table_ref, pos_ref, few_ref, limit_ref,
+             wide_out, slim_out, proj_out, out_out, inner_out, outer_out, conv_out, cbias_out, table_out, pos_out,
+             hbias_out, pbias_out, gain_out, shift_out, ibias_out):
     parts = wide_ref.shape[0]
     inner_rows = inner_out.shape[0]
-    proj_rows, out_rows = proj_out.shape[0] // parts, out_out.shape[0] // parts
+    proj_rows, out_rows = proj_out.shape[0] // parts, out_out.shape[0] // (parts - 1)
     filters = wide_ref.shape[2] // 2
     width = slim_ref.shape[2] // 3
     for part in range(parts):
@@ -946,25 +1120,49 @@
         for block in range(parts):
             lanes = slice(block * width, (block + 1) * width)
             proj_out[block * proj_rows : (block + 1) * proj_rows, cols] = both_ref[part, :proj_rows, lanes].astype(jnp.float32)
-            out_out[block * out_rows : (block + 1) * out_rows, cols] = both_ref[part, proj_rows:, lanes].astype(jnp.float32)
+            if block < parts - 1:
+                out_out[block * out_rows : (block + 1) * out_rows, cols] = both_ref[part, proj_rows:, lanes].astype(jnp.float32)
         units = ffn_ref.shape[1] - inner_rows
         outer_out[part * units : (part + 1) * units, :] = ffn_ref[part, inner_rows:, :].astype(jnp.float32)
         for block in range(inner_out.shape[1] // (parts * units)):
             start = (block * parts + part) * units
             inner_out[:, start : start + units] = ffn_ref[part, :inner_rows, block * units : (block + 1) * units].astype(jnp.float32)
-
-
-def assemble_call(wide, slim, both, ffn, inner_rows, out_rows):
-    args = (wide, slim, both, ffn)
+    slices, conv_rows = conv_ref.shape[:2]
+    taps = conv_out.shape[0]
+    turned = conv_ref[...].reshape(slices * conv_rows, 128).astype(jnp.float32).T
+    tap = lax.broadcasted_iota(jnp.int32, (taps, 1), 0) // depth
+    conv_out[...] = jnp.where(tap < limit_ref[...], turned[:taps], 0.0)
+    cbias_out[...] = turned[taps : taps + 1]
+    table = table_ref[...].reshape(-1, 128).astype(jnp.float32)
+    vocab = table_out.shape[0]
+    for group in range(-(-vocab // 128)):
+        stop = min(128, vocab - group * 128)
+        table_out[group * 128 : group * 128 + stop, :] = table[group * depth : (group + 1) * depth].T[:stop]
+    pos_out[...] = pos_ref[...].reshape(pos_out.shape).astype(jnp.float32)
+    own = few_ref[lax.axis_index("dp")].astype(jnp.float32)
+    size = gain_out.shape[1]
+    hbias_out[...] = own[0:1, : hbias_out.shape[1]]
+    pbias_out[...] = own[1:2, : pbias_out.shape[1]]
+    gain_out[...] = own[2:5, :size]
+    shift_out[...] = own[5:8, :size]
+    ibias_out[...] = own[8:9, : ibias_out.shape[1]]
+
+
+def assemble_call(wide, slim, both, ffn, conv, table, pos, few, widths, inner_rows, out_rows, taps, vocab, depth, sizes):
+    args = (wide, slim, both, ffn, conv, table, pos, few, widths)
     parts = wide.shape[0]
     vmem = pl.BlockSpec(memory_space=pltpu.VMEM)
     units = ffn.shape[1] - inner_rows
     dmodel = both.shape[2]
+    hb, pb, nd, ib = sizes
+    proj_rows = both.shape[1] - out_rows // (parts - 1)
     out_shape = [f32(wide.shape[1], wide.shape[2] * parts), f32(slim.shape[1], slim.shape[2] * parts),
-                 f32(both.shape[1] * parts - out_rows, dmodel), f32(out_rows, dmodel), f32(inner_rows, dmodel * parts), f32(units * parts, dmodel)]
+                 f32(proj_rows * parts, dmodel), f32(out_rows, dmodel), f32(inner_rows, dmodel * parts), f32(units * parts, dmodel),
+                 f32(taps, widths.shape[1]), f32(1, widths.shape[1]), f32(vocab, depth), f32(pos.shape[0] * pos.shape[1], pos.shape[2]),
+                 f32(1, hb), f32(1, pb), f32(3, nd), f32(3, nd), f32(1, ib)]
     return pl.pallas_call(
-        assemble, in_specs=[vmem] * 4, out_specs=[vmem] * 6, out_shape=out_shape,
-        compiler_params=pltpu.CompilerParams(vmem_limit_bytes=32 << 20), name="assemble",
+        functools.partial(assemble, depth), in_specs=[vmem] * len(args), out_specs=[vmem] * len(out_shape), out_shape=out_shape,
+        compiler_params=pltpu.CompilerParams(vmem_limit_bytes=40 << 20), name="assemble",
     )(*args)
 
 
@@ -987,10 +1185,6 @@
     width = hidden.shape[1]
     carry_gate = jax.nn.sigmoid(gates[:, width:])
     return carry_gate * hidden + (1.0 - carry_gate) * exact_gaussian_activation(gates[:, :width])
-
-
-def tn_dot(left, right):
-    return lax.dot_general(left, right, (((0,), (0,)), ((), ())), preferred_element_type=jnp.float32)
 
 
 def swap(array, axis, bit):
@@ -1074,23 +1268,25 @@
     def gather_rows(array):
         return lax.all_gather(array, "dp", axis=0, tiled=True)
 
-    def rows_from_columns(both, split):
-        rows = both.shape[1]
+    def groups_of(array, groups):
+        array = array.reshape(groups, -1, width).transpose(1, 0, 2).reshape(-1, groups * width)
+        return jnp.pad(array, ((0, 0), (0, dmodel - groups * width)))
+
+    def rows_from_columns(both):
         both = lax.all_to_all(both.reshape(parts, -1, dmodel), "filt", split_axis=0, concat_axis=0, tiled=True)
-        both = both.reshape(parts, slices // parts, rows, parts, width)
-        return [
-            item.transpose(1, 2, 3, 0, 4).reshape(-1, dmodel) for item in (both[:, :, :split], both[:, :, split:])
-        ]
+        both = both.reshape(parts, slices // parts, po_rows, parts, width)
+        both = [both[:, :, :split], both[:, :, split:, : parts - 1]]
+        return [item.transpose(1, 3, 2, 0, 4).reshape(-1, dmodel) for item in both]
 
     def columns_from_rows(*grads):
-        items = [
-            item.astype(jnp.bfloat16).reshape(slices // parts, parts, -1, parts, width).transpose(3, 0, 2, 1, 4)
-            for item in grads
-        ]
-        both = jnp.concatenate([item.reshape(parts, slices // parts, -1, dmodel) for item in items], axis=2)
-        rows = both.shape[2]
+        items = []
+        for item, groups in zip(grads, (parts, parts - 1)):
+            item = item.astype(jnp.bfloat16).reshape(slices // parts, groups, -1, parts, width)
+            item = item.transpose(3, 0, 2, 1, 4).reshape(parts, slices // parts, -1, groups * width)
+            items.append(jnp.pad(item, ((0, 0), (0, 0), (0, 0), (0, dmodel - groups * width))))
+        both = jnp.concatenate(items, axis=2)
         both = lax.all_to_all(both.reshape(parts, -1, dmodel), "filt", split_axis=0, concat_axis=0, tiled=True)
-        return both.reshape(slices, rows, dmodel)
+        return both.reshape(slices * po_rows, dmodel)
 
     fast = slices == 8 and parts == 4
     hb, pb, nd = highway_bias.shape[1], proj_bias.shape[0], norm_gain.shape[1]
@@ -1106,21 +1302,17 @@
     small_size = small.shape[0]
     small = jnp.pad(small, (0, -small_size % dmodel))
     slim_parts = [
-        item.reshape(-1, dmodel)
-        for item in (
-            own_columns(query_key_value_weight, 3),
-            own_columns(proj_weight, 1),
-            own_columns(attention_output_weight, 1),
-            small,
-        )
+        groups_of(own_columns(proj_weight, 1), parts),
+        groups_of(own_columns(attention_output_weight, 1), parts - 1),
+        own_columns(query_key_value_weight, 3).reshape(-1, dmodel),
+        small.reshape(-1, dmodel),
     ]
-    slim_cuts = [slim_parts[0].shape[0]]
-    for item in slim_parts[1:3]:
-        slim_cuts.append(slim_cuts[-1] + item.shape[0])
+    split = slim_parts[0].shape[0]
+    po_rows = split + slim_parts[1].shape[0]
+    qkv_rows = slim_parts[2].shape[0]
     slim_all = lax.all_gather(jnp.concatenate(slim_parts, axis=0), "dp", axis=0, tiled=False)
-    qkv_own = slim_all[:, : slim_cuts[0]].reshape(dmodel, 3 * width)
-    proj_own, out_own = rows_from_columns(slim_all[:, slim_cuts[0] : slim_cuts[2]], slim_cuts[1] - slim_cuts[0])
-    small = slim_all[:, slim_cuts[2] :]
+    qkv_own = slim_all[:, po_rows : po_rows + qkv_rows].reshape(dmodel, 3 * width)
+    small = slim_all[:, po_rows + qkv_rows :]
     small = small.reshape(slices, -1)[:, :small_size].astype(jnp.float32)
     cuts = [hb, hb + pb, hb + pb + 3 * nd, hb + pb + 6 * nd]
     highway_b, proj_b, gain, shift, inner_b = jnp.split(small, cuts, axis=1)
@@ -1149,20 +1341,36 @@
             ids, table, weight, limit, count, highway_weight[0], parts, letters, depth, 0
         )
         highway_own = highway_own.reshape(2, -1, filters)
-        gates = jnp.concatenate([nn_dot(features, item) for item in highway_own], axis=1) + highway_b_own
     else:
         acts, lse, embed = conv_forward_call(ids, table, weight, limit, count, letters, depth)
         features = gather_channels_call(acts, parts, 0)
         highway_own = gather_rows(own_columns(highway_weight[0], 2))
-        gates = nn_dot(features, highway_own) + highway_b_own
+        proj_own, out_own = rows_from_columns(slim_all[:, :po_rows])
     ffn_own, features = lax.optimization_barrier((ffn_own, features))
     ffn_all = lax.all_gather(ffn_own, "dp", axis=0, tiled=False)
-    feature_own = acts.astype(jnp.float32)
-    hidden_low = highway_mix(feature_own, gates).astype(jnp.bfloat16)
     base = position.astype(jnp.float32) + proj_b[None, :]
-    first, unit_zero, scale_zero, first_all = forward_stage_call(
-        blocks_of(nn_dot(hidden_low, proj_own)), base, gain[0:1], shift[0:1], EPS, 1
-    )
+    if fast:
+        gates, hidden_low, proj_own, out_own, first, unit_zero, scale_zero, first_all = highway_stage_call(
+            slim_all,
+            features,
+            highway_own,
+            highway_b_own,
+            acts,
+            base,
+            gain[0:1],
+            shift[0:1],
+            attention_output_weight.shape[0] * slices // parts,
+            po_rows,
+            EPS,
+            1,
+        )
+    else:
+        gates = nn_dot(features, highway_own) + highway_b_own
+        feature_own = acts.astype(jnp.float32)
+        hidden_low = highway_mix(feature_own, gates).astype(jnp.bfloat16)
+        first, unit_zero, scale_zero, first_all = forward_stage_call(
+            blocks_of(nn_dot(hidden_low, proj_own)), base, gain[0:1], shift[0:1], EPS, 1
+        )
     first_all = first_all.reshape(words, dmodel)
     packed = nn_dot(first_all, qkv_own).astype(jnp.bfloat16)
     queries, keys, values = (
@@ -1211,18 +1419,26 @@
     grad_ffn = jnp.concatenate(
         [item.astype(jnp.bfloat16).reshape(slices, -1, dmodel) for item in (grad_inner, grad_outer)], axis=1
     )
-    kinds = ("side", "ring") if fast else (None, None)
     if fast:
+        early = grad_ffn.shape[1] * 2 // 3
         grad_ffn = grad_ffn.reshape(4, 2, -1, dmodel)
+        grad_early, grad_late = grad_ffn[:, :, :early], grad_ffn[:, :, early:]
+        jobs = ("side",), (grad_early,)
+    else:
+        jobs = (), ()
+
+    def pair_sum(grad, got):
+        keep = lax.dynamic_index_in_dim(grad, slot % 2, 1, keepdims=False)
+        return (keep.astype(jnp.float32) + got.astype(jnp.float32)).astype(jnp.bfloat16)
+
     grad_inner_b = jnp.sum(d_inner.astype(jnp.float32), axis=0)
     d_res_one, d_gain_one, d_shift_one, unused_sum, d_mixed, *got = backward_stage_call(
-        blocks_of(nt_dot(d_inner, inner_own)), d_res_two, unit_one, scale_one, gain[1:2], 4, kinds[0], grad_ffn
+        blocks_of(nt_dot(d_inner, inner_own)), d_res_two, unit_one, scale_one, gain[1:2], 4, *jobs
     )
     if fast:
-        keep = lax.dynamic_index_in_dim(grad_ffn, slot % 2, 1, keepdims=False)
-        grad_ffn = (keep.astype(jnp.float32) + got[0].astype(jnp.float32)).astype(jnp.bfloat16)
+        grad_early = pair_sum(grad_early, got[0])
+        jobs = ("side", "ring"), (grad_late, grad_early)
     d_mixed = d_mixed.reshape(words, dmodel)
-    grad_out = tn_dot(attended, d_mixed)
     d_attended = nt_dot(d_mixed, out_own).astype(jnp.bfloat16)
     d_attended = d_attended.reshape(seqs, full_len, heads, HD)
     d_values = jnp.einsum(
@@ -1244,26 +1460,27 @@
     ).astype(jnp.bfloat16)
     grad_qkv = tn_dot(first_all, d_packed).astype(jnp.bfloat16)
     d_summed, d_gain_zero, d_shift_zero, grad_proj_b, d_projected, *got = backward_stage_call(
-        blocks_of(nt_dot(d_packed, qkv_own)), d_res_one, unit_zero, scale_zero, gain[0:1], 5, kinds[1], grad_ffn
+        blocks_of(nt_dot(d_packed, qkv_own)), d_res_one, unit_zero, scale_zero, gain[0:1], 5, *jobs
     )
     if fast:
-        keep = lax.dynamic_index_in_dim(grad_ffn, slot // 2, 0, keepdims=False)
-        grad_ffn = sum([item.astype(jnp.float32) for item in got[0]], keep.astype(jnp.float32))
-        grad_ffn = grad_ffn.astype(jnp.bfloat16)
+        grad_late = pair_sum(grad_late, got[0])
+        keep = lax.dynamic_index_in_dim(grad_early, slot // 2, 0, keepdims=False)
+        grad_early = sum([item.astype(jnp.float32) for item in got[1]], keep.astype(jnp.float32))
+        grad_early = grad_early.astype(jnp.bfloat16)
     grad_pos = jnp.sum(d_summed.reshape(seqs, quarter, dmodel), axis=0)
     d_projected = d_projected.reshape(words, dmodel)
-    grad_proj = tn_dot(hidden_low, d_projected)
-    grad_both = columns_from_rows(grad_proj, grad_out)
-    d_hidden = nt_dot(d_projected, proj_own)
-    d_in, d_gates = jax.vjp(highway_mix, feature_own, gates)[1](d_hidden)
-    d_gates = d_gates.astype(jnp.bfloat16)
-    grad_highway = tn_dot(features, d_gates).astype(jnp.bfloat16)
-    grad_highway_b = jnp.sum(d_gates.astype(jnp.float32), axis=0)
     if fast:
-        d_partial = nt_dot(d_gates[:, :filters], highway_own[0]) + nt_dot(d_gates[:, filters:], highway_own[1])
+        d_partial, d_in, grad_highway, grad_both, grad_highway_b = highway_back_call(
+            d_projected, proj_own, hidden_low, gates, acts, features, highway_own, attended, d_mixed, parts, po_rows
+        )
     else:
-        d_partial = nt_dot(d_gates, highway_own)
-    d_partial = d_partial.astype(jnp.bfloat16)
+        grad_both = columns_from_rows(tn_dot(hidden_low, d_projected), tn_dot(attended, d_mixed))
+        d_hidden = nt_dot(d_projected, proj_own)
+        d_in, d_gates = jax.vjp(highway_mix, feature_own, gates)[1](d_hidden)
+        d_gates = d_gates.astype(jnp.bfloat16)
+        grad_highway = tn_dot(features, d_gates).astype(jnp.bfloat16)
+        grad_highway_b = jnp.sum(d_gates.astype(jnp.float32), axis=0)
+        d_partial = nt_dot(d_gates, highway_own).astype(jnp.bfloat16)
     groups = table.shape[0] // depth
 
     def place_columns(own, blocks):
@@ -1274,16 +1491,16 @@
     d_gain = jnp.concatenate([d_gain_zero, d_gain_one, d_gain_two])
     d_shift = jnp.concatenate([d_shift_zero, d_shift_one, d_shift_two])
     pieces = [
-        place_columns(grad_highway_b, 2).reshape(slices, -1),
-        grad_proj_b.reshape(slices, -1),
-        d_gain.reshape(3, slices, nd).transpose(1, 0, 2).reshape(slices, -1),
-        d_shift.reshape(3, slices, nd).transpose(1, 0, 2).reshape(slices, -1),
-        place_columns(grad_inner_b, slices).reshape(slices, -1),
+        place_columns(grad_highway_b, 2).reshape(slices, 1, -1),
+        grad_proj_b.reshape(slices, 1, -1),
+        d_gain.reshape(3, slices, nd).transpose(1, 0, 2),
+        d_shift.reshape(3, slices, nd).transpose(1, 0, 2),
+        place_columns(grad_inner_b, slices).reshape(slices, 1, -1),
     ]
-    rows = jnp.concatenate(pieces, axis=1)
     if fast:
-        few_rows = -(-rows.shape[1] // 1024) * 8
-        few = jnp.pad(rows, ((0, 0), (0, few_rows * 128 - rows.shape[1]))).reshape(slices, few_rows, 128)
+        few = [jnp.pad(item, ((0, 0), (0, 0), (0, hb - item.shape[2]))) for item in pieces]
+        few.append(jnp.zeros((slices, 7, hb), jnp.float32))
+        few = jnp.concatenate(few, axis=1)
         wide_all, slim_all, both_all, ffn_all, conv_all, table_all, pos_all, few = epilogue_call(
             d_partial,
             d_in,
@@ -1296,20 +1513,36 @@
             count,
             grad_highway.reshape(4, 2, -1, 2 * filters),
             grad_qkv.reshape(4, 2, -1, 3 * width),
-            grad_both.reshape(4, 2, -1, dmodel),
-            grad_ffn,
-            grad_pos.reshape(slices, -1, 128),
+            grad_both,
+            grad_early,
+            grad_late,
+            grad_pos.reshape(slices, -1, dmodel),
             few,
             letters,
             depth,
             groups,
             6,
         )
-        conv_all = conv_all.reshape(filters, 128).astype(jnp.float32)
-        grad_pos = pos_all.reshape(grad_pos.shape).astype(jnp.float32)
-        table_all = table_all.reshape(-1, 128)[: groups * depth].astype(jnp.float32)
-        own = lax.dynamic_index_in_dim(few.reshape(slices, -1), slot, 0, keepdims=False)
-        own = own[: rows.shape[1]].astype(jnp.float32)
+        outs = assemble_call(
+            wide_all,
+            slim_all,
+            both_all,
+            ffn_all,
+            conv_all,
+            table_all,
+            pos_all,
+            few,
+            widths[None, :],
+            inner_rows,
+            attention_output_weight.shape[0],
+            conv_weight.shape[0],
+            char_table.shape[0],
+            depth,
+            (hb, pb, nd, feedforward_input_bias.shape[0]),
+        )
+        g_highway, g_qkv, g_proj, g_out, g_inner, g_outer, conv_grad_w, conv_grad_b, g_table, grad_pos = outs[:10]
+        g_highway_b, g_proj_b, g_gain, g_shift, g_inner_b = outs[10:]
+        conv_grad_b, g_proj_b, g_inner_b = conv_grad_b[0], g_proj_b[0], g_inner_b[0]
     else:
         d_features = scatter_channels_call(d_partial, d_in, 6)
         conv_sums, table_sums = conv_backward_call(
@@ -1317,41 +1550,35 @@
         )
         wide_all = jnp.stack(join_parts(reduce_rows(grad_highway)))
         slim_all = jnp.stack(join_parts(reduce_rows(grad_qkv)))
-        both_all = jnp.stack(join_parts(reduce_rows(grad_both.reshape(-1, dmodel))))
+        both_all = jnp.stack(join_parts(reduce_rows(grad_both)))
         ffn_all = jnp.stack(join_parts(reduce_rows(grad_ffn.reshape(-1, dmodel))))
         table_sums = table_sums.reshape(2, groups * depth, -1).sum(0)
         conv_all = lax.psum(conv_sums, "dp")
+        rows = jnp.concatenate([item.reshape(slices, -1) for item in pieces], axis=1)
         table_all, sums = lax.psum((table_sums, rows), ("dp", "filt"))
         grad_pos = lax.psum(grad_pos, "dp")
         own = lax.dynamic_index_in_dim(sums, slot, 0, keepdims=False)
-    tap_rows = conv_weight.shape[0]
-    tap_keep = (jnp.arange(tap_rows, dtype=jnp.int32) // depth)[:, None] < widths[None, :]
-    conv_grad_w = jnp.where(tap_keep, conv_all[:, :tap_rows].T, 0.0)
-    conv_grad_b = conv_all[:, tap_rows]
-    g_table = table_all.reshape(groups, depth, 128).transpose(0, 2, 1).reshape(-1, depth)
-    g_table = g_table[: char_table.shape[0]]
-    g_highway_b, g_proj_b, g_gain, g_shift, g_inner_b = jnp.split(own, cuts)
-
-    if fast:
-        g_highway, g_qkv, g_proj, g_out, g_inner, g_outer = assemble_call(
-            wide_all, slim_all, both_all, ffn_all, inner_rows, attention_output_weight.shape[0]
-        )
-    else:
+        tap_rows = conv_weight.shape[0]
+        tap_keep = (jnp.arange(tap_rows, dtype=jnp.int32) // depth)[:, None] < widths[None, :]
+        conv_grad_w = jnp.where(tap_keep, conv_all[:, :tap_rows].T, 0.0)
+        conv_grad_b = conv_all[:, tap_rows]
+        g_table = table_all.reshape(groups, depth, 128).transpose(0, 2, 1).reshape(-1, depth)
+        g_table = g_table[: char_table.shape[0]]
+        g_highway_b, g_proj_b, g_gain, g_shift, g_inner_b = jnp.split(own, cuts)
 
         def join_columns(array, blocks, rows_here):
-            split = array.reshape(parts, rows_here, blocks, -1).transpose(1, 2, 0, 3)
-            return split.reshape(rows_here, -1).astype(jnp.float32)
-
-        def join_groups(array):
-            split = array.reshape(parts, array.shape[1], parts, width).transpose(2, 1, 0, 3)
-            return split.reshape(-1, dmodel).astype(jnp.float32)
-
-        split = proj_weight.shape[0] // parts
+            array = array.reshape(parts, rows_here, blocks, -1).transpose(1, 2, 0, 3)
+            return array.reshape(rows_here, -1).astype(jnp.float32)
+
+        def join_groups(array, many):
+            array = array.reshape(parts, array.shape[1], parts, width).transpose(2, 1, 0, 3)
+            return array[:many].reshape(-1, dmodel).astype(jnp.float32)
+
         g_outer = ffn_all[:, inner_rows:].reshape(-1, dmodel).astype(jnp.float32)
         g_inner = join_columns(ffn_all[:, :inner_rows], slices, inner_rows)
         g_qkv = join_columns(slim_all, 3, query_key_value_weight.shape[0])
-        g_proj = join_groups(both_all[:, :split])
-        g_out = join_groups(both_all[:, split:])
+        g_proj = join_groups(both_all[:, :split], parts)
+        g_out = join_groups(both_all[:, split:], parts - 1)
         g_highway = join_columns(wide_all, 2, highway_weight.shape[1])
     return (
         encoded,
@@ -1359,7 +1586,7 @@
         conv_grad_w,
         conv_grad_b,
         g_highway[None],
-        g_highway_b[None],
+        g_highway_b.reshape(1, hb),
         g_proj,
         g_proj_b,
         grad_pos,

time: 481 us -> 444 us (0.923)
  Pallas kernels: 316 us -> 352 us
  matrix products: 48 us -> 22.4 us
  local copies, waits for them, and re-layouts: 61.7 us -> 38.7 us
  other arithmetic: 19.9 us -> 7.64 us
  starting transfers between devices: 8.97 us -> 0.08 us
    pallas_call x3 -> x5, Pallas kernels: 60.3 us -> 102 us  [the longest x2 43.5 us: backward_stage_call(): pl.pallas_call(functools.partial(backward_stage, kinds), out_shape=out_sh...]
    reshape x21 -> x10, local copies, waits for them, and re-layouts: 22.4 us -> 3.76 us  [the longest x1 2.41 us: per_device(): qkv_own = slim_all[:, po_rows:po_rows + qkv_rows].reshape(dmodel, 3 * width)]
    pallas_call x3 -> x2, Pallas kernels: 55.5 us -> 37.4 us  [comm_call(): pl.pallas_call(kernel, out_shape=out_shape, in_specs=[vmem] * len(args),...]
    pallas_call x1, Pallas kernels: 116 us -> 128 us  [epilogue_call(): pl.pallas_call(functools.partial(epilogue, letters, depth, block), in_spe...]
    dot_general x6 -> x3, matrix products: 13.4 us -> 3.15 us  [tn_dot(): lax.dot_general(left, right, (((0,), (0,)), ((), ())), preferred_element_...]
    dot_general x7 -> x4, matrix products: 13.1 us -> 3.22 us  [nt_dot(): lax.dot_general(left, right, (((1,), (1,)), ((), ())), preferred_element_...]
    all_to_all x2 -> x0, starting transfers between devices: 8.89 us -> none  [the longest x1 4.63 us: rows_from_columns(): lax.all_to_all(both.reshape(parts, -1, dmodel), 'filt', split_axis=0, con...]
    unnamed x120 -> x113, local copies, waits for them, and re-layouts: 13.2 us -> 20.9 us
  transfers between devices with their start and end apart: 4 -> 2, of which waited for: 1 -> 0; matrix products, arithmetic and copies ran while one was open for 12% -> 3% of each run, Pallas kernels for 26% -> 33%
where the time goes in v2:
time: 444 us; the launch traced here: 437 us
  Pallas kernels  352 us (79%)
  local copies, waits for them, and re-layouts  38.7 us (9%)
  matrix products  22.4 us (5%)
  between operations  16 us (4%)
  other arithmetic  7.64 us (2%)
    pallas_call x1, Pallas kernels, epilogue_call(): pl.pallas_call(functools.partial(epilogue, letters, depth, block), in_spe...  128 us
    pallas_call x1, Pallas kernels, prologue_call(): pl.pallas_call(functools.partial(prologue, letters, depth, block, chunks,...  84.1 us
    pallas_call x2, Pallas kernels, backward_stage_call(): pl.pallas_call(functools.partial(backward_stage, kinds), out_shape=out_sh...  43.5 us
    pallas_call x1, Pallas kernels, highway_stage_call(): pl.pallas_call(functools.partial(highway_stage, eps), in_specs=[hbm] + [v...  40.3 us
    pallas_call x2, Pallas kernels, comm_call(): pl.pallas_call(kernel, out_shape=out_shape, in_specs=[vmem] * len(args),...  37.4 us
    unnamed x113, local copies, waits for them, and re-layouts  20.9 us
    pallas_call x1, Pallas kernels, highway_back_call(): pl.pallas_call(highway_back, in_specs=[vmem] * 9, out_specs=[vmem] * 5, o...  14.4 us
    dot_general x4, matrix products, nn_dot(): return jnp.dot(left, right, preferred_element_type=jnp.float32)  12.3 us
  transfers between devices with their start and end apart: 2, of which 0 were waited for; matrix products, arithmetic and copies ran while one was open for 3% of the time, Pallas kernels for 33%

profile of v2, /device:TPU:0, one launch (start us, length us, event | category | flops | bytes accessed | tf_op | source)
XLA Modules:
  0.0 436.9 jit_solution(13029701434715299418)
XLA Ops:
  7.3 1.7 reshape.465
  9.0 1.0 dynamic-slice_reduce_fusion.1
  13.2 1.2 dynamic-slice_reduce_fusion
  16.3 84.1 %prologue.1 = (bf16[512,512]{1,0:T(8,128)(2,1)S(1)}, f32[512,512]{1,0:T(8,128)S(1)}, bf16[800,512]{1,0:T(8,128)(2,1)S(1)}, bf16[512,2048]{1,0:T(8,128)(2,1)S(1)}, bf16[2,4,2,256,512]{4,3,2,1,0:T(8,128)(2,1)}) custom-call(s32[56,512]{1,0:T(8,128)S(1)} %pad_bitcast_fusion.chars_ref.refs_2_, bf16[48,128]{1,0:T(8,128)(2,1)S(1)} %bitcast.138, ...), custom_call_target="tpu_custom_call" | custom-call | tf_op jit(solution)/shard_map/prologue/pallas_call | solution.py:661
  100.5 1.3 copy-done.5
  101.8 1.0 copy-done.8
  105.2 1.0 slice_bitcast_fusion
  106.9 2.4 reshape.476
  109.9 40.3 %highway_stage.1 = (f32[512,1024]{1,0:T(8,128)}, bf16[512,512]{1,0:T(8,128)(2,1)S(1)}, bf16[512,768]{1,0:T(8,128)(2,1)S(1)}, bf16[192,768]{1,0:T(8,128)(2,1)S(1)...) custom-call(bf16[8,171,768]{2,1,0:T(8,128)(2,1)} %all-gather.8.clone, ...), custom_call_target="tpu_custom_call" | custom-call | tf_op jit(solution)/shard_map/highway_stage/pallas_call | solution.py:744
  153.1 0.9 copy-done.28
  154.7 1.1 copy-done.30
  157.5 19.1 %forward_stage.1 = (f32[128,768]{1,0:T(8,128)S(1)}, f32[128,768]{1,0:T(8,128)S(1)}, f32[128,1]{1,0:T(8,128)S(1)}, bf16[4,128,768]{2,1,0:T(8,128)(2,1)S(1)}) custom-call(bf16[4,128,768]{2,1,0:T(8,128)(2,1)S(1)} %bitcast.129, f32[128,768]{1,0:T(8,128)S(1)} %get-tuple-element.89.base_ref, f32[1,768]{1,0:T(1,128)S(1)} %slice.80.gain_ref, ...), custom_call_target="tpu_custom_call" | custom-call | tf_op jit(solution)/shard_map/forward_stage/pallas_call | solution.py:220
  176.6 1.8 fusion.43
  178.4 10.4 %multiply_convert_fusion.1 = (bf16[512,768]{1,0:T(8,128)(2,1)S(1)}, f32[512,768]{1,0:T(8,128)S(1)}, f32[512,768]{1,0:T(8,128)S(1)}) fusion(f32[768]{0:T(1024)S(1)} %add.295, bf16[512,768]{1,0:T(8,128)(2,1)S(1)} %bitcast.143, bf16[768,768]{1,0:T(8,128)(2,1)S(1)} %bitcast.168), kind=kOutput, calls=%fused_computation.16 | convolution fusion | flops 629932032 | bytes 5901312 | tf_op jit(solution)/shard_map/dot_general | solution.py:24
  189.7 18.4 %top_stage.1 = (bf16[128,768]{1,0:T(8,128)(2,1)S(1)}, f32[128,768]{1,0:T(8,128)S(1)}, f32[1,768]{1,0:T(1,128)S(1)}, f32[1,768]{1,0:T(1,128)S(1)}, bf16[4,128,768]{2,1,0:T(8,128)(2,1)S(1)}) custom-call(bf16[4,128,768]{2,1,0:T(8,128)(2,1)S(1)} %bitcast.134, f32[128,768]{1,0:T(8,128)S(1)} %get-tuple-element.93.base_ref, bf16[128,768]{1,0:T(8,128)(2,1)S(1)} %bitcast.137, ...), custom_call_target="tpu_custom_call" | custom-call | tf_op jit(solution)/shard_map/top_stage/pallas_call | solution.py:220
  208.9 1.2 convert_reduce_fusion
  211.9 20.7 %backward_stage.2 = (f32[128,768]{1,0:T(8,128)S(1)}, f32[1,768]{1,0:T(1,128)S(1)}, f32[1,768]{1,0:T(1,128)S(1)}, f32[1,768]{1,0:T(1,128)}, bf16[4,128,768]{2,1,0...) custom-call(bf16[4,128,768]{2,1,0:T(8,128)(2,1)S(1)} %bitcast.133, f32[128,768]{1,0:T(8,128)S(1)} %get-tuple-element.96.base_ref, ...), custom_call_target="tpu_custom_call" | custom-call | tf_op jit(solution)/shard_map/backward_stage/pallas_call | solution.py:359
  233.0 1.1 multiply_reduce_fusion
  238.9 1.5 convolution_convert_fusion.2
  240.6 22.8 %backward_stage.3 = (f32[128,768]{1,0:T(8,128)S(1)}, f32[1,768]{1,0:T(1,128)S(1)}, f32[1,768]{1,0:T(1,128)S(1)}, f32[1,768]{1,0:T(1,128)S(1)}, bf16[4,128,768]{2...) custom-call(bf16[4,128,768]{2,1,0:T(8,128)(2,1)S(1)} %bitcast.132, ...), custom_call_target="tpu_custom_call" | custom-call | tf_op jit(solution)/shard_map/backward_stage/pallas_call | solution.py:359
  266.1 14.4 %highway_back.1 = (bf16[512,2048]{1,0:T(8,128)(2,1)}, f32[512,512]{1,0:T(8,128)}, bf16[2048,1024]{1,0:T(8,128)(2,1)}, bf16[4,2,96,768]{3,2,1,0:T(8,128)(2,1)}, f32[1,1024]{1,0:T(1,128)}) custom-call(bf16[512,768]{1,0:T(8,128)(2,1)} %bitcast.142, bf16[512,768]{1,0:T(8,128)(2,1)} %copy-done.23, bf16[512,512]{1,0:T(8,128)(2,1)} %copy-done.27, ...), custom_call_target="tpu_custom_call" | custom-call | flops 5200000000 | bytes 20000000 | tf_op jit(solution)/shard_map/highway_back/pallas_call | solution.py:812
  282.5 2.4 copy.163
  285.7 1.4 concatenate.43.refs_15_
  287.2 128.2 %epilogue.1 = (bf16[4,256,1024]{2,1,0:T(8,128)(2,1)}, bf16[4,96,576]{2,1,0:T(8,128)(2,1)}, bf16[4,96,768]{2,1,0:T(8,128)(2,1)}, bf16[4,192,768]{2,1,0:T(8,128)(2...) custom-call(bf16[512,2048]{1,0:T(8,128)(2,1)} %get-tuple-element.108, ...), custom_call_target="tpu_custom_call" | custom-call | tf_op jit(solution)/shard_map/epilogue/pallas_call | solution.py:1087
  415.4 1.6 copy-done.4
  417.1 1.3 copy-done.7
  418.4 1.1 copy-done.12
  419.4 1.0 copy-done.14
  420.4 0.9 copy-done.18
  421.4 0.9 copy-done.20
  422.3 0.9 copy-done.21
  423.9 3.9 assemble.1
  (211 shorter events, 29.7 us)
Async XLA Ops:
  7.2 96.5 %copy-start = (bf16[384,768]{1,0:T(8,128)(2,1)S(1)}, bf16[384,768]{1,0:T(8,128)(2,1)}, u32[]{:S(2)}) copy-start(bf16[384,768]{1,0:T(8,128)(2,1)} %param.34) | copy-start | bytes 1769476
  7.2 3.0 copy-start.41
  7.2 98.0 %all-gather.8.cloned.1.call-start = ((), (), s32[]{:S(2)}) async-start(), calls=%async_computation.1 | async-start | bytes 2433024 | tf_op jit(solution)/shard_map/all_gather | solution.py:1313
  7.3 3.5 copy-start.43
  10.0 1.4 copy-start.51
  10.0 1.5 copy-start.47
  10.0 1.5 copy-start.48
  10.0 1.5 copy-start.52
  10.2 2.2 copy-start.40
  11.6 3.1 copy-start.49
  11.6 3.2 copy-start.44
  12.4 3.4 copy-start.45
  12.4 3.4 copy-start.46
  12.4 164.2 %all-gather.6.cloned.1.call-start = ((), (), s32[]{:S(2)}) async-start(), calls=%async_computation | async-start | bytes 2654208 | tf_op jit(solution)/shard_map/all_gather | solution.py:1350
  15.8 84.7 %copy-start.6 = (bf16[512,128]{1,0:T(8,128)(2,1)}, bf16[512,128]{1,0:T(8,128)(2,1)S(1)}, u32[]{:S(2)}) copy-start(bf16[512,128]{1,0:T(8,128)(2,1)S(1)} %copy.147.weight_ref.refs_5_) | copy-start | bytes 393220
  15.9 84.6 %copy-start.9 = (s32[56,512]{1,0:T(8,128)}, s32[56,512]{1,0:T(8,128)S(1)}, u32[]{:S(2)}) copy-start(s32[56,512]{1,0:T(8,128)S(1)} %pad_bitcast_fusion.chars_ref.refs_2_) | copy-start | bytes 344068
  16.1 84.4 %copy-start.2 = (s32[512,1]{1,0:T(8,128)}, s32[512,1]{1,0:T(8,128)S(1)}, u32[]{:S(2)}) copy-start(s32[512,1]{1,0:T(8,128)S(1)} %broadcast_subtract_fusion.limit_ref.refs_7_) | copy-start | bytes 6148
  16.3 87.4 %copy-start.3 = (f32[512,1]{1,0:T(8,128)}, f32[512,1]{1,0:T(8,128)S(1)}, u32[]{:S(2)}) copy-start(f32[512,1]{1,0:T(8,128)S(1)} %convert_log_fusion.count_ref.refs_8_) | copy-start | bytes 6148
  100.5 1.3 copy-start.5
  103.6 6.2 %copy-start.13 = (bf16[512,512]{1,0:T(8,128)(2,1)}, bf16[512,512]{1,0:T(8,128)(2,1)S(1)}, u32[]{:S(2)}) copy-start(bf16[512,512]{1,0:T(8,128)(2,1)S(1)} %get-tuple-element.86.acts_ref) | copy-start | bytes 1572868
  105.2 1.7 slice-start
  106.9 2.9 copy-start.42
  109.9 40.4 %copy-start.38 = (bf16[768,576]{1,0:T(8,128)(2,1)S(1)}, bf16[768,576]{1,0:T(8,128)(2,1)}, u32[]{:S(2)}) copy-start(bf16[768,576]{1,0:T(8,128)(2,1)} %reshape.476) | copy-start | bytes 2654212
  151.6 3.1 copy-start.36
  152.4 1.7 copy-start.28
  211.8 21.1 %copy-start.29 = (f32[3,512,512]{1,2,0:T(8,128)S(1)}, f32[3,512,512]{1,2,0:T(8,128)}, u32[]{:S(2)}) copy-start(f32[3,512,512]{1,2,0:T(8,128)} %copy-done.28) | copy-start | bytes 9437188
  211.9 21.1 %copy-start.37 = (bf16[512,192]{0,1:T(8,128)(2,1)S(1)}, bf16[512,192]{0,1:T(8,128)(2,1)}, u32[]{:S(2)}) copy-start(bf16[512,192]{0,1:T(8,128)(2,1)} %copy-done.36) | copy-start | bytes 589828
  232.6 1.5 copy-start.11
  235.0 1.5 copy-start.31
  266.1 15.6 %copy-start.17 = (bf16[4,64,768]{2,1,0:T(8,128)(2,1)S(1)}, bf16[4,64,768]{2,1,0:T(8,128)(2,1)}, u32[]{:S(2)}) copy-start(bf16[4,64,768]{2,1,0:T(8,128)(2,1)} %copy-done.16) | copy-start | bytes 1179652
  415.4 14.4 %copy-start.1 = (bf16[384,768]{1,0:T(8,128)(2,1)S(1)}, bf16[384,768]{1,0:T(8,128)(2,1)}, u32[]{:S(2)}) copy-start(bf16[384,768]{1,0:T(8,128)(2,1)} %param.34) | copy-start | bytes 1769476
  415.4 1.7 copy-start.4
  (24 other events, 23.6 us)
Sparse Core Ops, SparseCore 0:
  12.5 80.5 all-gather.7
  104.6 55.9 all-gather.5

commit v3 on v2

--- a/solution.py
+++ b/solution.py
@@ -682,12 +682,14 @@
     greet([{"filt": me ^ hop} for hop in (1, 2, 3)])
     parts, sides, rows, dmodel = abox.shape
     copies = []
-    for hop in (2, 3, 1):
-        source = slim_ref.at[pl.ds(sides * (me ^ hop), sides), pl.ds(0, rows), :]
-        copy = remote(source, abox.at[me], asend.at[hop - 1], arecv.at[hop - 1], {"filt": me ^ hop})
-        copy.start()
-        copies.append(copy)
-    own = pltpu.make_async_copy(slim_ref.at[pl.ds(sides * me, sides), pl.ds(0, rows), :], abox.at[me], asend.at[3])
+    size, small = proj_ref.shape[0] // (sides * parts), out_ref.shape[0] // (sides * (parts - 1))
+    for index, span in enumerate((pl.ds(0, size), pl.ds(size, rows - size))):
+        for hop in (2, 3, 1):
+            source = slim_ref.at[pl.ds(sides * (me ^ hop), sides), span, :]
+            copy = remote(source, abox.at[me, :, span, :], asend.at[index, hop - 1], arecv.at[index, hop - 1], {"filt": me ^ hop})
+            copy.start()
+            copies.append(copy)
+    own = pltpu.make_async_copy(slim_ref.at[pl.ds(sides * me, sides), pl.ds(0, rows), :], abox.at[me], asend.at[0, 3])
     own.start()
     words, filters = acts_ref.shape
     block = 256
@@ -706,10 +708,9 @@
 
     lax.fori_loop(0, words // block, mix, 0)
     own.wait()
-    for copy in copies:
+    for copy in copies[:3]:
         copy.wait()
     width = dmodel // parts
-    size, small = proj_ref.shape[0] // (sides * parts), out_ref.shape[0] // (sides * (parts - 1))
     for part in range(parts):
         cols = slice(part * width, (part + 1) * width)
         for side in range(sides):
@@ -717,9 +718,6 @@
                 lanes = slice(group * width, (group + 1) * width)
                 start = (side * parts + group) * size
                 proj_ref[start : start + size, cols] = abox[part, side, :size, lanes]
-                if group < parts - 1:
-                    start = (side * (parts - 1) + group) * small
-                    out_ref[start : start + small, cols] = abox[part, side, size:, lanes]
 
     def project(index, carry):
         span = pl.ds(pl.multiple_of(index * 128, 128), 128)
@@ -733,6 +731,14 @@
     unit_ref[...] = unit
     scale_ref[...] = scale
     gather_blocks(value.astype(jnp.bfloat16), all_ref, send.at[pl.ds(3, 3)], recv.at[pl.ds(3, 3)], me)
+    for copy in copies[3:]:
+        copy.wait()
+    for part in range(parts):
+        cols = slice(part * width, (part + 1) * width)
+        for side in range(sides):
+            for group in range(parts - 1):
+                start = (side * (parts - 1) + group) * small
+                out_ref[start : start + small, cols] = abox[part, side, size:, group * width : (group + 1) * width]
 
 
 def highway_stage_call(slim, feats, wide, bias, acts, base, gain, shift, out_rows, po_rows, eps, ident):
@@ -746,76 +752,10 @@
         out_shape=[f32(words, 2 * filters), bf16(words, filters), bf16(filters, dmodel), bf16(out_rows, dmodel), f32(rows, dmodel),
                    f32(rows, dmodel), f32(rows, 1), bf16(parts, rows, dmodel)],
         scratch_shapes=[pltpu.VMEM((parts, 2, po_rows, dmodel), jnp.bfloat16), pltpu.VMEM((parts, rows, dmodel), jnp.bfloat16)]
-        + stage_scratch((rows, dmodel)) + [DMA((4,)), DMA((3,))],
+        + stage_scratch((rows, dmodel)) + [DMA((2, 4)), DMA((2, 3))],
         compiler_params=pltpu.CompilerParams(collective_id=ident, has_side_effects=True, vmem_limit_bytes=48 << 20),
         name="highway_stage",
     )(slim, feats, wide, bias, acts, base, gain, shift)
-
-
-def highway_back(dproj_ref, proj_ref, hidden_ref, gates_ref, acts_ref, feats_ref, wide_ref, attended_ref, dmixed_ref,
-                 part_ref, din_ref, grad_ref, both_ref, bias_ref, dgates_ref):
-    words, filters = acts_ref.shape
-    block = 128
-    bias_ref[...] = jnp.zeros(bias_ref.shape, jnp.float32)
-
-    def mix(index, carry):
-        span = pl.ds(pl.multiple_of(index * block, block), block)
-        dhidden = nt_dot(dproj_ref[span, :], proj_ref[...])
-        turn = gates_ref[span, :filters]
-        keep = sigmoid(gates_ref[span, filters:])
-        below = normal_cdf(turn)
-        slope = below + turn * (DENSITY * jnp.exp(-0.5 * turn * turn))
-        fresh = dhidden * (1.0 - keep)
-        din_ref[span, :] = dhidden * keep
-        dturn = (fresh * slope).astype(jnp.bfloat16)
-        dkeep = (fresh * keep * (acts_ref[span, :].astype(jnp.float32) - turn * below)).astype(jnp.bfloat16)
-        dgates_ref[span, :filters] = dturn
-        dgates_ref[span, filters:] = dkeep
-        bias_ref[:, :filters] += jnp.sum(dturn.astype(jnp.float32), axis=0, keepdims=True)
-        bias_ref[:, filters:] += jnp.sum(dkeep.astype(jnp.float32), axis=0, keepdims=True)
-        return carry
-
-    lax.fori_loop(0, words // block, mix, 0)
-    piece = 512
-
-    def grads(index, carry):
-        cols = pl.ds(pl.multiple_of(index * piece, piece), piece)
-        grad_ref[cols, :] = tn_dot(feats_ref[:, cols], dgates_ref[...]).astype(jnp.bfloat16)
-        down = nt_dot(dgates_ref[:, :filters], wide_ref[0, cols, :]) + nt_dot(dgates_ref[:, filters:], wide_ref[1, cols, :])
-        part_ref[:, cols] = down.astype(jnp.bfloat16)
-        return carry
-
-    lax.fori_loop(0, feats_ref.shape[1] // piece, grads, 0)
-    parts, sides, rows, dmodel = both_ref.shape
-    width = dmodel // parts
-    gproj = tn_dot(hidden_ref[...], dproj_ref[...]).astype(jnp.bfloat16)
-    gout = tn_dot(attended_ref[...], dmixed_ref[...]).astype(jnp.bfloat16)
-    size, small = gproj.shape[0] // (sides * parts), gout.shape[0] // (sides * (parts - 1))
-    for part in range(parts):
-        cols = slice(part * width, (part + 1) * width)
-        for side in range(sides):
-            for group in range(parts):
-                lanes = slice(group * width, (group + 1) * width)
-                start = (side * parts + group) * size
-                both_ref[part, side, :size, lanes] = gproj[start : start + size, cols]
-                if group < parts - 1:
-                    start = (side * (parts - 1) + group) * small
-                    both_ref[part, side, size:, lanes] = gout[start : start + small, cols]
-                else:
-                    both_ref[part, side, size:, lanes] = jnp.zeros((rows - size, width), jnp.bfloat16)
-
-
-def highway_back_call(dproj, proj, hidden, gates, acts, feats, wide, attended, dmixed, parts, po_rows):
-    words, filters = acts.shape
-    dmodel = dproj.shape[1]
-    vmem = pl.BlockSpec(memory_space=pltpu.VMEM)
-    return pl.pallas_call(
-        highway_back, in_specs=[vmem] * 9, out_specs=[vmem] * 5,
-        out_shape=[bf16(words, feats.shape[1]), f32(words, filters), bf16(feats.shape[1], 2 * filters), bf16(parts, 2, po_rows, dmodel), f32(1, 2 * filters)],
-        scratch_shapes=[pltpu.VMEM((words, 2 * filters), jnp.bfloat16)],
-        compiler_params=pltpu.CompilerParams(vmem_limit_bytes=56 << 20), name="highway_back",
-        cost_estimate=pl.CostEstimate(flops=5_200_000_000, bytes_accessed=20_000_000, transcendentals=1_000_000),
-    )(dproj, proj, hidden, gates, acts, feats, wide, attended, dmixed)
 
 
 class RowReduce:
@@ -892,10 +832,10 @@
 
 
 def epilogue(letters, depth, block, *refs):
-    (part_ref, base_ref, chars_ref, embed_ref, lse_ref, weight_ref, back_ref, limit_ref, count_ref, wide_ref, slim_ref,
-     cross_ref, ffn_ref, pair_ref, pos_ref, few_ref,
+    (dproj_ref, proj_ref, hidden_ref, gates_ref, acts_ref, feats_ref, high_ref, attended_ref, dmixed_ref, chars_ref, embed_ref, lse_ref, weight_ref, back_ref, limit_ref, count_ref, slim_ref,
+     ffn_ref, pair_ref, pos_ref, few_ref,
      wide_out, slim_out, rows_out, ffn_out, conv_out, table_out, pos_out, few_out,
-     inbox, merged, up_ref, patch_ref, down_ref, pull_ref, wgrad_ref, tgrad_ref, wide_y, wide_p, wide_z, slim_y, slim_p, slim_z,
+     bias_ref, part_ref, base_ref, dgates_ref, wide_ref, cross_ref, inbox, merged, up_ref, patch_ref, down_ref, pull_ref, wgrad_ref, tgrad_ref, wide_y, wide_p, wide_z, slim_y, slim_p, slim_z,
      rows_ref, rows_y, rows_p, rows_z, late_z, conv_low, conv_in, table_low, table_in, table_side, pos_low, pos_in, few_low, few_in, few_side,
      csend, crecv, rsend, rrecv, tsend, trecv, asend, arecv) = refs
     me = lax.axis_index("filt")
@@ -919,25 +859,36 @@
     ]
     both.ready = swaps
     pos.start(pos_ref[...])
-    few.start(few_ref[...])
+    queue = [slim, wide[0], wide[1], both, wide[2], wide[3]]
+    for index, item in enumerate(queue):
+        item.after = queue[index + AHEAD] if index + AHEAD < len(queue) else None
+    slim.across()
+    ffn_out[me, :early, :] = ffn_ref[...]
+    late.ring_out()
+    highway_mix_back(dproj_ref, proj_ref, hidden_ref, gates_ref, acts_ref, base_ref, dgates_ref, bias_ref)
+    highway_grads(feats_ref, dgates_ref, wide_ref)
+    for item in queue[1:AHEAD]:
+        item.across()
+    extra = few_ref[...]
+    place, row = lax.broadcasted_iota(jnp.int32, extra.shape, 0), lax.broadcasted_iota(jnp.int32, extra.shape, 1)
+    lanes = extra.shape[2]
+    extra = jnp.where((row == 0) & (place == me), bias_ref[:, :lanes][None], extra)
+    extra = jnp.where((row == 0) & (place == me + 4), bias_ref[:, lanes:][None], extra)
+    few.start(extra)
+    highway_down(dgates_ref, high_ref, part_ref)
+    scatter = ChannelScatter(part_ref, base_ref, up_ref, inbox, merged, csend, crecv)
+    scatter.begin()
+    row_grads(hidden_ref, dproj_ref, attended_ref, dmixed_ref, cross_ref)
+    rows_ref[me] = cross_ref[me]
+    scatter.finish()
+    pos.combine()
+    few.combine()
     for copy in swaps:
         copy.start()
-    rows_ref[me] = cross_ref[me]
-    queue = [slim, wide[0], both] + wide[1:]
-    for index, item in enumerate(queue):
-        item.after = queue[index + AHEAD] if index + AHEAD < len(queue) else None
-    for item in queue[:AHEAD]:
-        item.across()
-    ffn_out[me, :early, :] = ffn_ref[...]
-    late.ring_out()
-    scatter = ChannelScatter(part_ref, base_ref, up_ref, inbox, merged, csend, crecv)
-    scatter.run()
-    pos.combine()
-    few.combine()
     ffn.share()
     steps = iter([
-        [slim.along, ffn.relay], [late.join], [wide[0].along, slim.join], [late.relay, slim.relay], [both.along, wide[0].join],
-        [wide[0].relay, few.across], [wide[1].along, both.join], [both.relay], [], [],
+        [slim.along], [wide[0].along, ffn.relay], [late.join, slim.join], [wide[1].along, wide[0].join], [late.relay, slim.relay, few.across],
+        [wide[0].relay, both.along], [wide[1].join], [wide[1].relay], [wide[2].along, both.join], [both.relay],
     ])
 
     def advance():
@@ -1009,8 +960,8 @@
     sums = jnp.concatenate([sums, jnp.zeros((slices * size - table_rows, sums.shape[1]), jnp.float32)], axis=0)
     table_total.start(sums.reshape(table_low.shape))
     for step in (
-        wide[2].along, wide[1].join, wide[1].relay, wide[3].along, conv_total.combine, table_total.combine, wide[2].join,
-        wide[2].relay, table_total.across, wide[3].join, wide[3].relay,
+        wide[3].along, conv_total.combine, table_total.combine, wide[2].join, wide[2].relay, table_total.across,
+        wide[3].join, wide[3].relay,
     ):
         step()
     for copy in swaps:
@@ -1025,7 +976,7 @@
         self.sems = (send, recv)
         self.me = lax.axis_index("filt")
 
-    def run(self):
+    def begin(self):
         me = self.me
         rows, cols = self.base.shape
         pieces = self.sems[0].shape[1]
@@ -1041,9 +992,14 @@
             copy.start()
             return copy
 
-        spans = [pl.ds(piece * size, size) for piece in range(pieces)]
+        self.lanes, self.hop = lanes, hop
+        self.spans = spans = [pl.ds(piece * size, size) for piece in range(pieces)]
         first = [hop(self.part.at[span, lanes(me ^ 3)], 0, piece, me ^ 1) for piece, span in enumerate(spans)]
         second = [hop(self.part.at[span, lanes(me ^ 1)], 1, piece, me ^ 1) for piece, span in enumerate(spans)]
+        self.first, self.second = first, second
+
+    def finish(self):
+        me, lanes, hop, first, second, spans = self.me, self.lanes, self.hop, self.first, self.second, self.spans
         third = []
         for piece, span in enumerate(spans):
             first[piece].wait_recv()
@@ -1060,20 +1016,96 @@
             copy.wait_send()
 
 
-def epilogue_call(part, base, ids, embed, lse, weight, back, limit, count, wide, slim, both, ffn, pair, pos, few, letters, depth, groups, ident, block=256):
+def highway_mix_back(dproj_ref, proj_ref, hidden_ref, gates_ref, acts_ref, din_ref, dgates_ref, bias_ref):
+    words, filters = acts_ref.shape
+    block = 128
+    bias_ref[...] = jnp.zeros(bias_ref.shape, jnp.float32)
+
+    def mix(index, carry):
+        span = pl.ds(pl.multiple_of(index * block, block), block)
+        dhidden = nt_dot(dproj_ref[span, :], proj_ref[...])
+        turn = gates_ref[span, :filters]
+        keep = sigmoid(gates_ref[span, filters:])
+        below = normal_cdf(turn)
+        slope = below + turn * (DENSITY * jnp.exp(-0.5 * turn * turn))
+        fresh = dhidden * (1.0 - keep)
+        din_ref[span, :] = dhidden * keep
+        dturn = (fresh * slope).astype(jnp.bfloat16)
+        dkeep = (fresh * keep * (acts_ref[span, :].astype(jnp.float32) - turn * below)).astype(jnp.bfloat16)
+        dgates_ref[span, :filters] = dturn
+        dgates_ref[span, filters:] = dkeep
+        bias_ref[:, :filters] += jnp.sum(dturn.astype(jnp.float32), axis=0, keepdims=True)
+        bias_ref[:, filters:] += jnp.sum(dkeep.astype(jnp.float32), axis=0, keepdims=True)
+        return carry
+
+    lax.fori_loop(0, words // block, mix, 0)
+
+
+def highway_grads(feats_ref, dgates_ref, grad_ref):
+    rings, sides, rows, cols = grad_ref.shape
+    piece = sides * rows
+
+    def grads(index, carry):
+        lanes = pl.ds(pl.multiple_of(index * piece, piece), piece)
+        grad = tn_dot(feats_ref[:, lanes], dgates_ref[...]).astype(jnp.bfloat16)
+        grad_ref[index] = grad.reshape(sides, rows, cols)
+        return carry
+
+    lax.fori_loop(0, rings, grads, 0)
+
+
+def highway_down(dgates_ref, high_ref, part_ref):
+    filters = high_ref.shape[2]
+    piece = 512
+
+    def down(index, carry):
+        lanes = pl.ds(pl.multiple_of(index * piece, piece), piece)
+        both = nt_dot(dgates_ref[:, :filters], high_ref[0, lanes, :]) + nt_dot(dgates_ref[:, filters:], high_ref[1, lanes, :])
+        part_ref[:, lanes] = both.astype(jnp.bfloat16)
+        return carry
+
+    lax.fori_loop(0, part_ref.shape[1] // piece, down, 0)
+
+
+def row_grads(hidden_ref, dproj_ref, attended_ref, dmixed_ref, both_ref):
+    parts, sides, rows, dmodel = both_ref.shape
+    width = dmodel // parts
+    gproj = tn_dot(hidden_ref[...], dproj_ref[...]).astype(jnp.bfloat16)
+    gout = tn_dot(attended_ref[...], dmixed_ref[...]).astype(jnp.bfloat16)
+    size, small = gproj.shape[0] // (sides * parts), gout.shape[0] // (sides * (parts - 1))
+    for part in range(parts):
+        cols = slice(part * width, (part + 1) * width)
+        for side in range(sides):
+            for group in range(parts):
+                lanes = slice(group * width, (group + 1) * width)
+                start = (side * parts + group) * size
+                both_ref[part, side, :size, lanes] = gproj[start : start + size, cols]
+                if group < parts - 1:
+                    start = (side * (parts - 1) + group) * small
+                    both_ref[part, side, size:, lanes] = gout[start : start + small, cols]
+                else:
+                    both_ref[part, side, size:, lanes] = jnp.zeros((rows - size, width), jnp.bfloat16)
+
+
+def epilogue_call(dproj, proj, hidden, gates, acts, feats, high, attended, dmixed, ids, embed, lse, weight, back, limit, count,
+                  slim, ffn, pair, pos, few, po_rows, letters, depth, groups, ident, block=256):
     filters, words = lse.shape
-    args = (part, base, ids, embed, lse, weight, back, limit, count, wide, slim, both, ffn, pair, pos, few)
-    parts = part.shape[1] // filters
+    args = (dproj, proj, hidden, gates, acts, feats, high, attended, dmixed, ids, embed, lse, weight, back, limit, count,
+            slim, ffn, pair, pos, few)
+    channels, dmodel = feats.shape[1], dproj.shape[1]
+    parts = channels // filters
     slices = pos.shape[0]
     pieces = 4
     vmem = pl.BlockSpec(memory_space=pltpu.VMEM)
     table_size = -(-(-(-groups * depth // slices)) // 8) * 8
+    wide_shape = (slices // 2, 2, channels // slices, 2 * filters)
+    both_shape = (slices // 2, 2, po_rows, dmodel)
 
     def space(shape, dtype=jnp.bfloat16):
         return pltpu.VMEM(tuple(shape), dtype)
 
-    def stages(array):
-        ring, side, rows, cols = array.shape
+    def stages(shape):
+        ring, side, rows, cols = shape
         return [space((ring, rows, cols)), space((ring, rows, cols)), space((ring - 1, rows, cols))]
 
     def totals(shape, sides):
@@ -1082,21 +1114,24 @@
 
     conv_shape = (slices, filters // slices, 128)
     table_shape = (slices, table_size, 128)
-    out_shape = [bf16(parts, *wide.shape[2:]), bf16(parts, *slim.shape[2:]), bf16(parts, *both.shape[2:]), bf16(parts, ffn.shape[0] + pair.shape[1], ffn.shape[1]), bf16(*conv_shape), bf16(*table_shape), bf16(*pos.shape), bf16(*few.shape)]
+    out_shape = [bf16(parts, *wide_shape[2:]), bf16(parts, *slim.shape[2:]), bf16(parts, *both_shape[2:]),
+                 bf16(parts, ffn.shape[0] + pair.shape[1], ffn.shape[1]), bf16(*conv_shape), bf16(*table_shape), bf16(*pos.shape),
+                 bf16(*few.shape)]
     padded = (letters + KW - 1) * depth
     return pl.pallas_call(
         functools.partial(epilogue, letters, depth, block),
         in_specs=[vmem] * len(args),
         out_specs=[vmem] * len(out_shape),
         out_shape=out_shape,
-        scratch_shapes=[space((3, words, filters)), space((words, filters)), space((words, filters)), space((padded, block)),
+        scratch_shapes=[space((1, 2 * filters), jnp.float32), space((words, channels)), space((words, filters), jnp.float32), space((words, 2 * filters)), space(wide_shape),
+                        space(both_shape), space((3, words, filters)), space((words, filters)), space((words, filters)), space((padded, block)),
                         space((padded, block), jnp.float32), space((filters, block), jnp.float32),
                         space((filters, 128), jnp.float32), space((2 * groups * depth, 128), jnp.float32)]
-        + stages(wide) + stages(slim) + [space(both.shape)] + stages(both) + [space((3,) + pair.shape[1:])]
+        + stages(wide_shape) + stages(slim.shape) + [space(both_shape)] + stages(both_shape) + [space((3,) + pair.shape[1:])]
         + totals(conv_shape, False) + totals(table_shape, True) + totals(pos.shape, False) + totals(few.shape, True)
         + [DMA((3, pieces)), DMA((3, pieces)), DMA((8, 7)), DMA((8, 7)), DMA((4, 3, slices - 1)), DMA((4, 3, slices - 1)),
            DMA((3,)), DMA((3,))],
-        compiler_params=pltpu.CompilerParams(collective_id=ident, has_side_effects=True, vmem_limit_bytes=56 << 20),
+        compiler_params=pltpu.CompilerParams(collective_id=ident, has_side_effects=True, vmem_limit_bytes=60 << 20),
         name="epilogue",
     )(*args)
 
@@ -1167,11 +1202,12 @@
 
 
 def exact_gaussian_activation(values):
-    return jax.nn.gelu(values, approximate=False)
+    return values * normal_cdf(values)
 
 
 def gelu_back(values, upstream):
-    return jax.vjp(exact_gaussian_activation, values)[1](upstream)[0]
+    density = DENSITY * jnp.exp(-0.5 * values * values)
+    return upstream * (normal_cdf(values) + values * density)
 
 
 def channel_widths(channels):
@@ -1469,11 +1505,7 @@
         grad_early = grad_early.astype(jnp.bfloat16)
     grad_pos = jnp.sum(d_summed.reshape(seqs, quarter, dmodel), axis=0)
     d_projected = d_projected.reshape(words, dmodel)
-    if fast:
-        d_partial, d_in, grad_highway, grad_both, grad_highway_b = highway_back_call(
-            d_projected, proj_own, hidden_low, gates, acts, features, highway_own, attended, d_mixed, parts, po_rows
-        )
-    else:
+    if not fast:
         grad_both = columns_from_rows(tn_dot(hidden_low, d_projected), tn_dot(attended, d_mixed))
         d_hidden = nt_dot(d_projected, proj_own)
         d_in, d_gates = jax.vjp(highway_mix, feature_own, gates)[1](d_hidden)
@@ -1490,8 +1522,12 @@
 
     d_gain = jnp.concatenate([d_gain_zero, d_gain_one, d_gain_two])
     d_shift = jnp.concatenate([d_shift_zero, d_shift_one, d_shift_two])
+    if fast:
+        highway_piece = jnp.zeros((slices, 1, hb), jnp.float32)
+    else:
+        highway_piece = place_columns(grad_highway_b, 2).reshape(slices, 1, -1)
     pieces = [
-        place_columns(grad_highway_b, 2).reshape(slices, 1, -1),
+        highway_piece,
         grad_proj_b.reshape(slices, 1, -1),
         d_gain.reshape(3, slices, nd).transpose(1, 0, 2),
         d_shift.reshape(3, slices, nd).transpose(1, 0, 2),
@@ -1502,8 +1538,15 @@
         few.append(jnp.zeros((slices, 7, hb), jnp.float32))
         few = jnp.concatenate(few, axis=1)
         wide_all, slim_all, both_all, ffn_all, conv_all, table_all, pos_all, few = epilogue_call(
-            d_partial,
-            d_in,
+            d_projected,
+            proj_own,
+            hidden_low,
+            gates,
+            acts,
+            features,
+            highway_own,
+            attended,
+            d_mixed,
             ids,
             embed,
             lse,
@@ -1511,13 +1554,12 @@
             back,
             limit,
             count,
-            grad_highway.reshape(4, 2, -1, 2 * filters),
             grad_qkv.reshape(4, 2, -1, 3 * width),
-            grad_both,
             grad_early,
             grad_late,
             grad_pos.reshape(slices, -1, dmodel),
             few,
+            po_rows,
             letters,
             depth,
             groups,

time: 444 us -> 412 us (0.928)
  Pallas kernels: 352 us -> 334 us
  matrix products: 22.4 us -> 13 us
    pallas_call x1 -> x0, Pallas kernels: 14.4 us -> none  [highway_back_call(): pl.pallas_call(highway_back, in_specs=[vmem] * 9, out_specs=[vmem] * 5, o...]
    dot_general x4, matrix products: 12.3 us -> 2.73 us  [nn_dot(): return jnp.dot(left, right, preferred_element_type=jnp.float32)]
    unnamed x113 -> x105, local copies, waits for them, and re-layouts: 20.9 us -> 18.7 us
  transfers between devices with their start and end apart: 2 -> 2, of which waited for: 0 -> 0; matrix products, arithmetic and copies ran while one was open for 3% -> 3% of each run, Pallas kernels for 33% -> 34%
where the time goes in v3:
time: 412 us; the launch traced here: 407 us
  Pallas kernels  334 us (81%)
  local copies, waits for them, and re-layouts  35.5 us (9%)
  between operations  16.2 us (4%)
  matrix products  13 us (3%)
  other arithmetic  7.65 us (2%)
    pallas_call x1, Pallas kernels, epilogue_call(): pl.pallas_call(functools.partial(epilogue, letters, depth, block), in_spe...  128 us
    pallas_call x1, Pallas kernels, prologue_call(): pl.pallas_call(functools.partial(prologue, letters, depth, block, chunks,...  84.2 us
    pallas_call x2, Pallas kernels, backward_stage_call(): pl.pallas_call(functools.partial(backward_stage, kinds), out_shape=out_sh...  43.8 us
    pallas_call x2, Pallas kernels, comm_call(): pl.pallas_call(kernel, out_shape=out_shape, in_specs=[vmem] * len(args),...  37.4 us
    pallas_call x1, Pallas kernels, highway_stage_call(): pl.pallas_call(functools.partial(highway_stage, eps), in_specs=[hbm] + [v...  36.6 us
    unnamed x105, local copies, waits for them, and re-layouts  18.7 us
  transfers between devices with their start and end apart: 2, of which 0 were waited for; matrix products, arithmetic and copies ran while one was open for 3% of the time, Pallas kernels for 34%

profile of v3, /device:TPU:0, one launch (start us, length us, event | category | flops | bytes accessed | tf_op | source)
XLA Modules:
  0.0 406.9 jit_solution(17348673331654993025)
XLA Ops:
  7.3 1.7 reshape.459
  9.0 1.0 dynamic-slice_reduce_fusion.1
  13.2 1.2 dynamic-slice_reduce_fusion
  16.3 84.2 %prologue.1 = (bf16[512,512]{1,0:T(8,128)(2,1)S(1)}, f32[512,512]{1,0:T(8,128)S(1)}, bf16[800,512]{1,0:T(8,128)(2,1)S(1)}, bf16[512,2048]{1,0:T(8,128)(2,1)S(1)}, bf16[2,4,2,256,512]{4,3,2,1,0:T(8,128)(2,1)}) custom-call(s32[56,512]{1,0:T(8,128)S(1)} %pad_bitcast_fusion.chars_ref.refs_9_, bf16[48,128]{1,0:T(8,128)(2,1)S(1)} %bitcast.137, ...), custom_call_target="tpu_custom_call" | custom-call | tf_op jit(solution)/shard_map/prologue/pallas_call | solution.py:661
  100.5 1.4 copy-done.2
  101.9 0.9 copy-done.12
  104.4 1.0 slice_bitcast_fusion
  106.1 2.4 reshape.470
  109.1 36.6 %highway_stage.1 = (f32[512,1024]{1,0:T(8,128)}, bf16[512,512]{1,0:T(8,128)(2,1)S(1)}, bf16[512,768]{1,0:T(8,128)(2,1)S(1)}, bf16[192,768]{1,0:T(8,128)(2,1)S(1)...) custom-call(bf16[8,171,768]{2,1,0:T(8,128)(2,1)} %all-gather.8.clone, ...), custom_call_target="tpu_custom_call" | custom-call | tf_op jit(solution)/shard_map/highway_stage/pallas_call | solution.py:750
  148.6 0.9 copy-done.28
  151.9 18.2 %forward_stage.1 = (f32[128,768]{1,0:T(8,128)S(1)}, f32[128,768]{1,0:T(8,128)S(1)}, f32[128,1]{1,0:T(8,128)S(1)}, bf16[4,128,768]{2,1,0:T(8,128)(2,1)S(1)}) custom-call(bf16[4,128,768]{2,1,0:T(8,128)(2,1)S(1)} %bitcast.129, f32[128,768]{1,0:T(8,128)S(1)} %get-tuple-element.84.base_ref, f32[1,768]{1,0:T(1,128)S(1)} %slice.80.gain_ref, ...), custom_call_target="tpu_custom_call" | custom-call | tf_op jit(solution)/shard_map/forward_stage/pallas_call | solution.py:220
  170.1 1.8 fusion.42
  171.9 0.9 multiply_convert_fusion.1
  173.7 19.2 %top_stage.1 = (bf16[128,768]{1,0:T(8,128)(2,1)S(1)}, f32[128,768]{1,0:T(8,128)S(1)}, f32[1,768]{1,0:T(1,128)S(1)}, f32[1,768]{1,0:T(1,128)S(1)}, bf16[4,128,768]{2,1,0:T(8,128)(2,1)S(1)}) custom-call(bf16[4,128,768]{2,1,0:T(8,128)(2,1)S(1)} %bitcast.133, f32[128,768]{1,0:T(8,128)S(1)} %get-tuple-element.88.base_ref, bf16[128,768]{1,0:T(8,128)(2,1)S(1)} %bitcast.136, ...), custom_call_target="tpu_custom_call" | custom-call | tf_op jit(solution)/shard_map/top_stage/pallas_call | solution.py:220
  193.7 1.1 convert_reduce_fusion
  196.6 20.6 %backward_stage.2 = (f32[128,768]{1,0:T(8,128)S(1)}, f32[1,768]{1,0:T(1,128)S(1)}, f32[1,768]{1,0:T(1,128)S(1)}, f32[1,768]{1,0:T(1,128)}, bf16[4,128,768]{2,1,0...) custom-call(bf16[4,128,768]{2,1,0:T(8,128)(2,1)S(1)} %bitcast.132, f32[128,768]{1,0:T(8,128)S(1)} %get-tuple-element.91.base_ref, ...), custom_call_target="tpu_custom_call" | custom-call | tf_op jit(solution)/shard_map/backward_stage/pallas_call | solution.py:359
  217.7 1.1 multiply_reduce_fusion
  218.8 0.9 multiply_convert_fusion
  223.4 1.5 convolution_convert_fusion.2
  225.9 23.2 %backward_stage.3 = (f32[128,768]{1,0:T(8,128)S(1)}, f32[1,768]{1,0:T(1,128)S(1)}, f32[1,768]{1,0:T(1,128)S(1)}, f32[1,768]{1,0:T(1,128)S(1)}, bf16[4,128,768]{2...) custom-call(bf16[4,128,768]{2,1,0:T(8,128)(2,1)S(1)} %bitcast.131, ...), custom_call_target="tpu_custom_call" | custom-call | tf_op jit(solution)/shard_map/backward_stage/pallas_call | solution.py:359
  249.1 0.9 copy-done.14
  252.2 2.2 copy.157
  255.2 1.4 concatenate.43.refs_20_
  256.7 128.5 %epilogue.1 = (bf16[4,256,1024]{2,1,0:T(8,128)(2,1)}, bf16[4,96,576]{2,1,0:T(8,128)(2,1)}, bf16[4,96,768]{2,1,0:T(8,128)(2,1)}, bf16[4,192,768]{2,1,0:T(8,128)(2...) custom-call(bf16[512,768]{1,0:T(8,128)(2,1)} %bitcast.130, ...), custom_call_target="tpu_custom_call" | custom-call | tf_op jit(solution)/shard_map/epilogue/pallas_call | solution.py:1121
  385.2 1.6 copy-done.7
  386.8 1.3 copy-done.9
  388.1 1.1 copy-done.15
  389.2 1.0 copy-done.17
  390.2 0.9 copy-done.21
  391.1 0.9 copy-done.23
  392.0 0.9 copy-done.24
  393.7 3.9 assemble.1
  (200 shorter events, 26.3 us)
Async XLA Ops:
  7.2 95.6 %copy-start = (bf16[384,768]{1,0:T(8,128)(2,1)S(1)}, bf16[384,768]{1,0:T(8,128)(2,1)}, u32[]{:S(2)}) copy-start(bf16[384,768]{1,0:T(8,128)(2,1)} %param.34) | copy-start | bytes 1769476
  7.2 3.0 copy-start.37
  7.2 97.2 %all-gather.8.cloned.1.call-start = ((), (), s32[]{:S(2)}) async-start(), calls=%async_computation.1 | async-start | bytes 2433024 | tf_op jit(solution)/shard_map/all_gather | solution.py:1349
  7.3 3.5 copy-start.39
  10.0 1.5 copy-start.43
  10.0 1.5 copy-start.44
  10.0 1.5 copy-start.48
  10.2 2.2 copy-start.36
  11.6 3.1 copy-start.45
  11.6 3.2 copy-start.40
  12.4 3.4 copy-start.41
  12.4 3.4 copy-start.42
  12.4 157.7 %all-gather.6.cloned.1.call-start = ((), (), s32[]{:S(2)}) async-start(), calls=%async_computation | async-start | bytes 2654208 | tf_op jit(solution)/shard_map/all_gather | solution.py:1386
  15.8 84.7 %copy-start.8 = (bf16[512,128]{1,0:T(8,128)(2,1)}, bf16[512,128]{1,0:T(8,128)(2,1)S(1)}, u32[]{:S(2)}) copy-start(bf16[512,128]{1,0:T(8,128)(2,1)S(1)} %copy.142.weight_ref.refs_12_) | copy-start | bytes 393220
  15.9 84.6 %copy-start.11 = (s32[56,512]{1,0:T(8,128)}, s32[56,512]{1,0:T(8,128)S(1)}, u32[]{:S(2)}) copy-start(s32[56,512]{1,0:T(8,128)S(1)} %pad_bitcast_fusion.chars_ref.refs_9_) | copy-start | bytes 344068
  16.1 84.4 %copy-start.4 = (s32[512,1]{1,0:T(8,128)}, s32[512,1]{1,0:T(8,128)S(1)}, u32[]{:S(2)}) copy-start(s32[512,1]{1,0:T(8,128)S(1)} %broadcast_subtract_fusion.limit_ref.refs_14_) | copy-start | bytes 6148
  16.3 86.5 %copy-start.5 = (f32[512,1]{1,0:T(8,128)}, f32[512,1]{1,0:T(8,128)S(1)}, u32[]{:S(2)}) copy-start(f32[512,1]{1,0:T(8,128)S(1)} %convert_log_fusion.count_ref.refs_15_) | copy-start | bytes 6148
  102.8 3.3 copy-start.10
  102.8 6.3 %copy-start.6 = (bf16[512,512]{1,0:T(8,128)(2,1)}, bf16[512,512]{1,0:T(8,128)(2,1)S(1)}, u32[]{:S(2)}) copy-start(bf16[512,512]{1,0:T(8,128)(2,1)S(1)} %get-tuple-element.81.acts_ref.refs_4_) | copy-start | bytes 1572868
  104.4 1.7 slice-start
  106.1 2.9 copy-start.38
  109.1 36.6 %copy-start.34 = (bf16[768,576]{1,0:T(8,128)(2,1)S(1)}, bf16[768,576]{1,0:T(8,128)(2,1)}, u32[]{:S(2)}) copy-start(bf16[768,576]{1,0:T(8,128)(2,1)} %reshape.470) | copy-start | bytes 2654212
  145.7 1.4 copy-start.26
  147.1 3.1 copy-start.32
  147.9 1.7 copy-start.28
  150.2 1.7 copy-start.30
  196.6 21.1 %copy-start.29 = (f32[3,512,512]{1,2,0:T(8,128)S(1)}, f32[3,512,512]{1,2,0:T(8,128)}, u32[]{:S(2)}) copy-start(f32[3,512,512]{1,2,0:T(8,128)} %copy-done.28) | copy-start | bytes 9437188
  196.6 21.0 %copy-start.33 = (bf16[512,192]{0,1:T(8,128)(2,1)S(1)}, bf16[512,192]{0,1:T(8,128)(2,1)}, u32[]{:S(2)}) copy-start(bf16[512,192]{0,1:T(8,128)(2,1)} %copy-done.32) | copy-start | bytes 589828
  217.2 1.6 copy-start.3
  219.6 1.4 copy-start.31
  385.2 14.4 %copy-start.1 = (bf16[384,768]{1,0:T(8,128)(2,1)S(1)}, bf16[384,768]{1,0:T(8,128)(2,1)}, u32[]{:S(2)}) copy-start(bf16[384,768]{1,0:T(8,128)(2,1)} %param.34) | copy-start | bytes 1769476
  385.2 1.7 copy-start.7
  (20 other events, 20.8 us)
Sparse Core Ops, SparseCore 0:
  12.5 80.6 all-gather.7
  103.8 55.8 all-gather.5

commit v4 on v3

--- a/solution.py
+++ b/solution.py
@@ -446,7 +446,8 @@
 
 
 class Total:
-    def __init__(self, low, inbox, out, send, recv, sides=None):
+    def __init__(self, low, inbox, out, send, recv, sides=None, shared=True):
+        self.shared, self.third = shared, []
         self.low, self.inbox, self.out, self.sides = low, inbox, out, sides
         self.send, self.recv = send, recv
         self.me, self.slot = lax.axis_index("filt"), lax.axis_index("dp")
@@ -472,8 +473,8 @@
         total = self.low[self.slot].astype(jnp.float32)
         for hop in range(1, self.count):
             total = total + self.inbox[hop - 1].astype(jnp.float32)
-        self.out[self.slot] = total.astype(jnp.bfloat16)
         if self.sides is None:
+            self.out[self.slot] = total.astype(jnp.bfloat16)
             self.spread()
             return
         self.sides[0] = total.astype(jnp.bfloat16)
@@ -484,8 +485,12 @@
             copy.wait_recv()
         left = self.sides[0].astype(jnp.float32) + self.sides[1].astype(jnp.float32)
         right = self.sides[2].astype(jnp.float32) + self.sides[3].astype(jnp.float32)
-        self.out[self.slot] = (left + right).astype(jnp.bfloat16)
-        self.spread()
+        total = (left + right).astype(jnp.bfloat16)
+        if self.shared:
+            self.out[self.slot] = total
+            self.spread()
+        else:
+            self.out[...] = total
 
     def spread(self):
         piece = self.out.at[self.slot]
@@ -760,7 +765,7 @@
 
 class RowReduce:
     def __init__(self, grad, yin, pair, zin, joined, span, sems, base=0):
-        self.base, self.ready, self.after = base, [], None
+        self.base, self.ready = base, []
         self.grad, self.yin, self.pair, self.zin, self.joined = grad, yin, pair, zin, joined
         self.span, self.sems = span, sems
         self.me, self.slot = lax.axis_index("filt"), lax.axis_index("dp")
@@ -785,8 +790,6 @@
     def along(self):
         span = self.span
         self.first.wait_recv()
-        if self.after is not None:
-            self.after.across()
         both = self.grad[:, self.side, span, :].astype(jnp.float32) + self.yin[:, span, :].astype(jnp.float32)
         self.pair[:, span, :] = both.astype(jnp.bfloat16)
         self.ring_out()
@@ -826,9 +829,6 @@
         self.last.wait_recv()
         for copy in self.copies:
             copy.wait_send()
-
-
-AHEAD = 2
 
 
 def epilogue(letters, depth, block, *refs):
@@ -841,7 +841,7 @@
     me = lax.axis_index("filt")
     greet_all()
     pos = Total(pos_low, pos_in, pos_out, tsend.at[0], trecv.at[0])
-    few = Total(few_low, few_in, few_out, tsend.at[1], trecv.at[1], few_side)
+    few = Total(few_low, few_in, few_out, tsend.at[1], trecv.at[1], few_side, False)
     conv_total = Total(conv_low, conv_in, conv_out, tsend.at[2], trecv.at[2])
     table_total = Total(table_low, table_in, table_out, tsend.at[3], trecv.at[3], table_side)
     wide_rows = wide_out.shape[1] // 4
@@ -859,16 +859,12 @@
     ]
     both.ready = swaps
     pos.start(pos_ref[...])
-    queue = [slim, wide[0], wide[1], both, wide[2], wide[3]]
-    for index, item in enumerate(queue):
-        item.after = queue[index + AHEAD] if index + AHEAD < len(queue) else None
     slim.across()
     ffn_out[me, :early, :] = ffn_ref[...]
     late.ring_out()
     highway_mix_back(dproj_ref, proj_ref, hidden_ref, gates_ref, acts_ref, base_ref, dgates_ref, bias_ref)
     highway_grads(feats_ref, dgates_ref, wide_ref)
-    for item in queue[1:AHEAD]:
-        item.across()
+    wide[0].across()
     extra = few_ref[...]
     place, row = lax.broadcasted_iota(jnp.int32, extra.shape, 0), lax.broadcasted_iota(jnp.int32, extra.shape, 1)
     lanes = extra.shape[2]
@@ -880,15 +876,20 @@
     scatter.begin()
     row_grads(hidden_ref, dproj_ref, attended_ref, dmixed_ref, cross_ref)
     rows_ref[me] = cross_ref[me]
+    wide[1].across()
+    slim.along()
     scatter.finish()
+    wide[2].across()
+    wide[0].along()
     pos.combine()
     few.combine()
     for copy in swaps:
         copy.start()
     ffn.share()
     steps = iter([
-        [slim.along], [wide[0].along, ffn.relay], [late.join, slim.join], [wide[1].along, wide[0].join], [late.relay, slim.relay, few.across],
-        [wide[0].relay, both.along], [wide[1].join], [wide[1].relay], [wide[2].along, both.join], [both.relay],
+        [wide[3].across, wide[1].along], [slim.join], [both.across], [wide[2].along, wide[0].join, late.join],
+        [slim.relay, ffn.relay, wide[0].relay, wide[1].join], [late.relay, few.across, wide[3].along], [wide[1].relay, wide[2].join],
+        [wide[2].relay], [], [],
     ])
 
     def advance():
@@ -960,8 +961,7 @@
     sums = jnp.concatenate([sums, jnp.zeros((slices * size - table_rows, sums.shape[1]), jnp.float32)], axis=0)
     table_total.start(sums.reshape(table_low.shape))
     for step in (
-        wide[3].along, conv_total.combine, table_total.combine, wide[2].join, wide[2].relay, table_total.across,
-        wide[3].join, wide[3].relay,
+        both.along, wide[3].join, table_total.combine, conv_total.combine, wide[3].relay, table_total.across, both.join, both.relay,
     ):
         step()
     for copy in swaps:
@@ -1116,7 +1116,7 @@
     table_shape = (slices, table_size, 128)
     out_shape = [bf16(parts, *wide_shape[2:]), bf16(parts, *slim.shape[2:]), bf16(parts, *both_shape[2:]),
                  bf16(parts, ffn.shape[0] + pair.shape[1], ffn.shape[1]), bf16(*conv_shape), bf16(*table_shape), bf16(*pos.shape),
-                 bf16(*few.shape)]
+                 bf16(*few.shape[1:])]
     padded = (letters + KW - 1) * depth
     return pl.pallas_call(
         functools.partial(epilogue, letters, depth, block),
@@ -1174,7 +1174,7 @@
         stop = min(128, vocab - group * 128)
         table_out[group * 128 : group * 128 + stop, :] = table[group * depth : (group + 1) * depth].T[:stop]
     pos_out[...] = pos_ref[...].reshape(pos_out.shape).astype(jnp.float32)
-    own = few_ref[lax.axis_index("dp")].astype(jnp.float32)
+    own = few_ref[...].astype(jnp.float32)
     size = gain_out.shape[1]
     hbias_out[...] = own[0:1, : hbias_out.shape[1]]
     pbias_out[...] = own[1:2, : pbias_out.shape[1]]
@@ -1186,7 +1186,10 @@
 def assemble_call(wide, slim, both, ffn, conv, table, pos, few, widths, inner_rows, out_rows, taps, vocab, depth, sizes):
     args = (wide, slim, both, ffn, conv, table, pos, few, widths)
     parts = wide.shape[0]
-    vmem = pl.BlockSpec(memory_space=pltpu.VMEM)
+
+    def whole(shape):
+        return pl.BlockSpec(shape, lambda step: (0,) * len(shape))
+
     units = ffn.shape[1] - inner_rows
     dmodel = both.shape[2]
     hb, pb, nd, ib = sizes
@@ -1196,8 +1199,9 @@
                  f32(taps, widths.shape[1]), f32(1, widths.shape[1]), f32(vocab, depth), f32(pos.shape[0] * pos.shape[1], pos.shape[2]),
                  f32(1, hb), f32(1, pb), f32(3, nd), f32(3, nd), f32(1, ib)]
     return pl.pallas_call(
-        functools.partial(assemble, depth), in_specs=[vmem] * len(args), out_specs=[vmem] * len(out_shape), out_shape=out_shape,
-        compiler_params=pltpu.CompilerParams(vmem_limit_bytes=40 << 20), name="assemble",
+        functools.partial(assemble, depth), grid=(1,), in_specs=[whole(item.shape) for item in args],
+        out_specs=[whole(item.shape) for item in out_shape], out_shape=out_shape,
+        compiler_params=pltpu.CompilerParams(vmem_limit_bytes=56 << 20), name="assemble",
     )(*args)
 
 

time: 412 us -> 395 us (0.959)
  Pallas kernels: 334 us -> 323 us
  local copies, waits for them, and re-layouts: 35.5 us -> 28 us
    pallas_call x1, Pallas kernels: 128 us -> 115 us  [epilogue_call(): pl.pallas_call(functools.partial(epilogue, letters, depth, block), in_spe...]
    unnamed x105 -> x89, local copies, waits for them, and re-layouts: 18.7 us -> 11.2 us
  transfers between devices with their start and end apart: 2 -> 2, of which waited for: 0 -> 0; matrix products, arithmetic and copies ran while one was open for 3% -> 4% of each run, Pallas kernels for 34% -> 36%
where the time goes in v4:
time: 395 us; the launch traced here: 389 us
  Pallas kernels  323 us (82%)
  local copies, waits for them, and re-layouts  28 us (7%)
  between operations  16.1 us (4%)
  matrix products  13 us (3%)
  other arithmetic  8.87 us (2%)
    pallas_call x1, Pallas kernels, epilogue_call(): pl.pallas_call(functools.partial(epilogue, letters, depth, block), in_spe...  115 us
    pallas_call x1, Pallas kernels, prologue_call(): pl.pallas_call(functools.partial(prologue, letters, depth, block, chunks,...  84.2 us
    pallas_call x2, Pallas kernels, backward_stage_call(): pl.pallas_call(functools.partial(backward_stage, kinds), out_shape=out_sh...  43.8 us
    pallas_call x2, Pallas kernels, comm_call(): pl.pallas_call(kernel, out_shape=out_shape, in_specs=[vmem] * len(args),...  37.4 us
    pallas_call x1, Pallas kernels, highway_stage_call(): pl.pallas_call(functools.partial(highway_stage, eps), in_specs=[hbm] + [v...  36.5 us
    unnamed x89, local copies, waits for them, and re-layouts  11.2 us
  transfers between devices with their start and end apart: 2, of which 0 were waited for; matrix products, arithmetic and copies ran while one was open for 4% of the time, Pallas kernels for 36%

profile of v4, /device:TPU:0, one launch (start us, length us, event | category | flops | bytes accessed | tf_op | source)
XLA Modules:
  0.0 389.1 jit_solution(14151131126771733156)
XLA Ops:
  7.3 1.7 reshape.459
  9.0 1.0 dynamic-slice_reduce_fusion.1
  13.2 1.2 dynamic-slice_reduce_fusion
  16.3 84.2 %prologue.1 = (bf16[512,512]{1,0:T(8,128)(2,1)S(1)}, f32[512,512]{1,0:T(8,128)S(1)}, bf16[800,512]{1,0:T(8,128)(2,1)S(1)}, bf16[512,2048]{1,0:T(8,128)(2,1)S(1)}, bf16[2,4,2,256,512]{4,3,2,1,0:T(8,128)(2,1)}) custom-call(s32[56,512]{1,0:T(8,128)S(1)} %pad_bitcast_fusion.chars_ref.refs_9_, bf16[48,128]{1,0:T(8,128)(2,1)S(1)} %bitcast.137, ...), custom_call_target="tpu_custom_call" | custom-call | tf_op jit(solution)/shard_map/prologue/pallas_call | solution.py:666
  100.5 1.4 copy-done.2
  101.9 0.9 copy-done.10
  105.0 1.0 slice_bitcast_fusion
  106.7 2.4 reshape.470
  109.7 36.5 %highway_stage.1 = (f32[512,1024]{1,0:T(8,128)}, bf16[512,512]{1,0:T(8,128)(2,1)S(1)}, bf16[512,768]{1,0:T(8,128)(2,1)S(1)}, bf16[192,768]{1,0:T(8,128)(2,1)S(1)...) custom-call(bf16[8,171,768]{2,1,0:T(8,128)(2,1)} %all-gather.8.clone, ...), custom_call_target="tpu_custom_call" | custom-call | tf_op jit(solution)/shard_map/highway_stage/pallas_call | solution.py:755
  149.2 0.9 copy-done.20
  151.1 0.8 copy.160.refs_7_
  152.4 18.2 %forward_stage.1 = (f32[128,768]{1,0:T(8,128)S(1)}, f32[128,768]{1,0:T(8,128)S(1)}, f32[128,1]{1,0:T(8,128)S(1)}, bf16[4,128,768]{2,1,0:T(8,128)(2,1)S(1)}) custom-call(bf16[4,128,768]{2,1,0:T(8,128)(2,1)S(1)} %bitcast.129, f32[128,768]{1,0:T(8,128)S(1)} %get-tuple-element.84.base_ref, f32[1,768]{1,0:T(1,128)S(1)} %slice.80.gain_ref, ...), custom_call_target="tpu_custom_call" | custom-call | tf_op jit(solution)/shard_map/forward_stage/pallas_call | solution.py:220
  170.6 1.8 fusion.42
  172.4 0.9 multiply_convert_fusion.1
  174.2 19.2 %top_stage.1 = (bf16[128,768]{1,0:T(8,128)(2,1)S(1)}, f32[128,768]{1,0:T(8,128)S(1)}, f32[1,768]{1,0:T(1,128)S(1)}, f32[1,768]{1,0:T(1,128)S(1)}, bf16[4,128,768]{2,1,0:T(8,128)(2,1)S(1)}) custom-call(bf16[4,128,768]{2,1,0:T(8,128)(2,1)S(1)} %bitcast.133, f32[128,768]{1,0:T(8,128)S(1)} %get-tuple-element.88.base_ref, bf16[128,768]{1,0:T(8,128)(2,1)S(1)} %bitcast.136, ...), custom_call_target="tpu_custom_call" | custom-call | tf_op jit(solution)/shard_map/top_stage/pallas_call | solution.py:220
  194.3 1.1 convert_reduce_fusion
  195.4 0.8 convolution_convert_fusion.1
  196.2 0.8 convolution_convert_fusion.3
  197.1 20.6 %backward_stage.2 = (f32[128,768]{1,0:T(8,128)S(1)}, f32[1,768]{1,0:T(1,128)S(1)}, f32[1,768]{1,0:T(1,128)S(1)}, f32[1,768]{1,0:T(1,128)}, bf16[4,128,768]{2,1,0...) custom-call(bf16[4,128,768]{2,1,0:T(8,128)(2,1)S(1)} %bitcast.132, f32[128,768]{1,0:T(8,128)S(1)} %get-tuple-element.91.base_ref, ...), custom_call_target="tpu_custom_call" | custom-call | tf_op jit(solution)/shard_map/backward_stage/pallas_call | solution.py:359
  218.2 1.1 multiply_reduce_fusion
  219.3 0.9 multiply_convert_fusion
  222.8 0.8 convolution_convert_fusion.5
  223.9 1.5 convolution_convert_fusion.2
  226.5 23.2 %backward_stage.3 = (f32[128,768]{1,0:T(8,128)S(1)}, f32[1,768]{1,0:T(1,128)S(1)}, f32[1,768]{1,0:T(1,128)S(1)}, f32[1,768]{1,0:T(1,128)S(1)}, bf16[4,128,768]{2...) custom-call(bf16[4,128,768]{2,1,0:T(8,128)(2,1)S(1)} %bitcast.131, ...), custom_call_target="tpu_custom_call" | custom-call | tf_op jit(solution)/shard_map/backward_stage/pallas_call | solution.py:359
  249.7 0.9 copy-done.12
  251.9 0.8 fusion.13.refs_18_
  252.8 2.2 copy.157
  255.8 1.4 concatenate.43.refs_20_
  257.3 114.5 %epilogue.1 = (bf16[4,256,1024]{2,1,0:T(8,128)(2,1)}, bf16[4,96,576]{2,1,0:T(8,128)(2,1)}, bf16[4,96,768]{2,1,0:T(8,128)(2,1)}, bf16[4,192,768]{2,1,0:T(8,128)(2...) custom-call(bf16[512,768]{1,0:T(8,128)(2,1)} %bitcast.130, ...), custom_call_target="tpu_custom_call" | custom-call | tf_op jit(solution)/shard_map/epilogue/pallas_call | solution.py:1121
  371.8 6.5 %assemble.1 = (f32[256,4096]{1,0:T(8,128)}, f32[96,2304]{1,0:T(8,128)}, f32[256,768]{1,0:T(8,128)}, f32[96,768]{1,0:T(8,128)}, f32[96,3072]{1,0:T(8,128)}, /*ind...) custom-call(bf16[4,256,1024]{2,1,0:T(8,128)(2,1)} %get-tuple-element, ...), custom_call_target="tpu_custom_call" | custom-call | tf_op jit(solution)/shard_map/assemble/pallas_call | solution.py:1201
  378.3 1.6 copy.162
  379.9 1.2 reduce.15
  (184 shorter events, 20.7 us)
Async XLA Ops:
  7.2 95.7 %copy-start = (bf16[384,768]{1,0:T(8,128)(2,1)S(1)}, bf16[384,768]{1,0:T(8,128)(2,1)}, u32[]{:S(2)}) copy-start(bf16[384,768]{1,0:T(8,128)(2,1)} %param.34) | copy-start | bytes 1769476
  7.2 3.0 copy-start.29
  7.2 97.8 %all-gather.8.cloned.1.call-start = ((), (), s32[]{:S(2)}) async-start(), calls=%async_computation.1 | async-start | bytes 2433024 | tf_op jit(solution)/shard_map/all_gather | solution.py:1353
  7.3 3.5 copy-start.31
  10.0 1.4 copy-start.39
  10.0 1.5 copy-start.35
  10.0 1.5 copy-start.36
  10.0 1.5 copy-start.40
  10.2 2.2 copy-start.28
  11.6 3.1 copy-start.37
  11.6 3.2 copy-start.32
  12.4 3.4 copy-start.33
  12.4 3.4 copy-start.34
  12.4 158.2 %all-gather.6.cloned.1.call-start = ((), (), s32[]{:S(2)}) async-start(), calls=%async_computation | async-start | bytes 2654208 | tf_op jit(solution)/shard_map/all_gather | solution.py:1390
  15.8 84.7 %copy-start.7 = (bf16[512,128]{1,0:T(8,128)(2,1)}, bf16[512,128]{1,0:T(8,128)(2,1)S(1)}, u32[]{:S(2)}) copy-start(bf16[512,128]{1,0:T(8,128)(2,1)S(1)} %copy.142.weight_ref.refs_12_) | copy-start | bytes 393220
  15.9 84.6 %copy-start.9 = (s32[56,512]{1,0:T(8,128)}, s32[56,512]{1,0:T(8,128)S(1)}, u32[]{:S(2)}) copy-start(s32[56,512]{1,0:T(8,128)S(1)} %pad_bitcast_fusion.chars_ref.refs_9_) | copy-start | bytes 344068
  16.1 84.4 %copy-start.4 = (s32[512,1]{1,0:T(8,128)}, s32[512,1]{1,0:T(8,128)S(1)}, u32[]{:S(2)}) copy-start(s32[512,1]{1,0:T(8,128)S(1)} %broadcast_subtract_fusion.limit_ref.refs_14_) | copy-start | bytes 6148
  16.3 86.6 %copy-start.5 = (f32[512,1]{1,0:T(8,128)}, f32[512,1]{1,0:T(8,128)S(1)}, u32[]{:S(2)}) copy-start(f32[512,1]{1,0:T(8,128)S(1)} %convert_log_fusion.count_ref.refs_15_) | copy-start | bytes 6148
  102.8 3.8 copy-start.8
  102.8 6.8 %copy-start.6 = (bf16[512,512]{1,0:T(8,128)(2,1)}, bf16[512,512]{1,0:T(8,128)(2,1)S(1)}, u32[]{:S(2)}) copy-start(bf16[512,512]{1,0:T(8,128)(2,1)S(1)} %get-tuple-element.81.acts_ref.refs_4_) | copy-start | bytes 1572868
  105.0 1.7 slice-start
  106.7 2.9 copy-start.30
  109.6 36.6 %copy-start.26 = (bf16[768,576]{1,0:T(8,128)(2,1)S(1)}, bf16[768,576]{1,0:T(8,128)(2,1)}, u32[]{:S(2)}) copy-start(bf16[768,576]{1,0:T(8,128)(2,1)} %reshape.470) | copy-start | bytes 2654212
  146.2 1.4 copy-start.18
  147.6 3.1 copy-start.24
  148.4 1.7 copy-start.20
  150.7 1.7 copy-start.22
  197.1 21.1 %copy-start.21 = (f32[3,512,512]{1,2,0:T(8,128)S(1)}, f32[3,512,512]{1,2,0:T(8,128)}, u32[]{:S(2)}) copy-start(f32[3,512,512]{1,2,0:T(8,128)} %copy-done.20) | copy-start | bytes 9437188
  197.1 21.1 %copy-start.25 = (bf16[512,192]{0,1:T(8,128)(2,1)S(1)}, bf16[512,192]{0,1:T(8,128)(2,1)}, u32[]{:S(2)}) copy-start(bf16[512,192]{0,1:T(8,128)(2,1)} %copy-done.24) | copy-start | bytes 589828
  217.7 1.6 copy-start.3
  220.2 1.4 copy-start.23
  371.8 10.1 %copy-start.1 = (bf16[384,768]{1,0:T(8,128)(2,1)S(1)}, bf16[384,768]{1,0:T(8,128)(2,1)}, u32[]{:S(2)}) copy-start(bf16[384,768]{1,0:T(8,128)(2,1)} %param.34) | copy-start | bytes 1769476
  (12 other events, 12.7 us)
Sparse Core Ops, SparseCore 0:
  12.5 80.5 all-gather.7
  103.8 55.8 all-gather.5

commit v5 on v4

--- a/solution.py
+++ b/solution.py
@@ -226,15 +226,21 @@
 DMA = pltpu.SemaphoreType.DMA
 
 def scatter_sum(part_ref, inbox, send, recv, me):
-    copies = []
-    for hop in (3, 2, 1):
-        copy = remote(part_ref.at[me ^ hop], inbox.at[hop - 1], send.at[hop - 1], recv.at[hop - 1], {"filt": me ^ hop})
-        copy.start()
-        copies.append(copy)
-    total = part_ref[me].astype(jnp.float32)
-    for copy, hop in reversed(list(zip(copies, (3, 2, 1)))):
-        copy.wait()
-        total = total + inbox[hop - 1].astype(jnp.float32)
+    first = remote(part_ref.at[me ^ 3], inbox.at[0], send.at[0], recv.at[0], {"filt": me ^ 1})
+    second = remote(part_ref.at[me ^ 1], inbox.at[1], send.at[1], recv.at[1], {"filt": me ^ 1})
+    third = remote(inbox.at[3], inbox.at[2], send.at[2], recv.at[2], {"filt": me ^ 2})
+    first.start()
+    second.start()
+    first.wait_recv()
+    inbox[3] = (part_ref[me ^ 2].astype(jnp.float32) + inbox[0].astype(jnp.float32)).astype(jnp.bfloat16)
+    third.start()
+    second.wait_recv()
+    total = part_ref[me].astype(jnp.float32) + inbox[1].astype(jnp.float32)
+    third.wait_recv()
+    total = total + inbox[2].astype(jnp.float32)
+    first.wait_send()
+    second.wait_send()
+    third.wait_send()
     return total
 
 def gather_blocks(low, all_ref, send, recv, me):
@@ -328,7 +334,7 @@
         copy.wait()
 
 def stage_scratch(block):
-    return [pltpu.VMEM((3,) + block, jnp.bfloat16), DMA((6,)), DMA((6,))]
+    return [pltpu.VMEM((4,) + block, jnp.bfloat16), DMA((6,)), DMA((6,))]
 
 def f32(*shape): return jax.ShapeDtypeStruct(shape, jnp.float32)
 def bf16(*shape): return jax.ShapeDtypeStruct(shape, jnp.bfloat16)

time: 395 us -> 386 us (0.977)
  Pallas kernels: 323 us -> 313 us
    pallas_call x1, Pallas kernels: 36.5 us -> 31.2 us  [highway_stage_call(): pl.pallas_call(functools.partial(highway_stage, eps), in_specs=[hbm] + [v...]
    pallas_call x2, Pallas kernels: 37.4 us -> 32.1 us  [comm_call(): pl.pallas_call(kernel, out_shape=out_shape, in_specs=[vmem] * len(args),...]
  transfers between devices with their start and end apart: 2 -> 2, of which waited for: 0 -> 0; matrix products, arithmetic and copies ran while one was open for 4% -> 4% of each run, Pallas kernels for 36% -> 35%
where the time goes in v5:
time: 386 us; the launch traced here: 379 us
  Pallas kernels  313 us (81%)
  local copies, waits for them, and re-layouts  28.2 us (7%)
  between operations  16.1 us (4%)
  matrix products  12.8 us (3%)
  other arithmetic  9.04 us (2%)
    pallas_call x1, Pallas kernels, epilogue_call(): pl.pallas_call(functools.partial(epilogue, letters, depth, block), in_spe...  116 us
    pallas_call x1, Pallas kernels, prologue_call(): pl.pallas_call(functools.partial(prologue, letters, depth, block, chunks,...  84.2 us
    pallas_call x2, Pallas kernels, backward_stage_call(): pl.pallas_call(functools.partial(backward_stage, kinds), out_shape=out_sh...  43.3 us
    pallas_call x2, Pallas kernels, comm_call(): pl.pallas_call(kernel, out_shape=out_shape, in_specs=[vmem] * len(args),...  32.1 us
    pallas_call x1, Pallas kernels, highway_stage_call(): pl.pallas_call(functools.partial(highway_stage, eps), in_specs=[hbm] + [v...  31.2 us
    unnamed x89, local copies, waits for them, and re-layouts  11.4 us
  transfers between devices with their start and end apart: 2, of which 0 were waited for; matrix products, arithmetic and copies ran while one was open for 4% of the time, Pallas kernels for 35%

profile of v5, /device:TPU:0, one launch (start us, length us, event | category | flops | bytes accessed | tf_op | source)
XLA Modules:
  0.0 379.2 jit_solution(257943113547247966)
XLA Ops:
  7.3 1.7 reshape.459
  9.0 1.0 dynamic-slice_reduce_fusion.1
  13.2 1.2 dynamic-slice_reduce_fusion
  16.3 84.2 %prologue.1 = (bf16[512,512]{1,0:T(8,128)(2,1)S(1)}, f32[512,512]{1,0:T(8,128)S(1)}, bf16[800,512]{1,0:T(8,128)(2,1)S(1)}, bf16[512,2048]{1,0:T(8,128)(2,1)S(1)}, bf16[2,4,2,256,512]{4,3,2,1,0:T(8,128)(2,1)}) custom-call(s32[56,512]{1,0:T(8,128)S(1)} %pad_bitcast_fusion.chars_ref.refs_9_, bf16[48,128]{1,0:T(8,128)(2,1)S(1)} %bitcast.137, ...), custom_call_target="tpu_custom_call" | custom-call | tf_op jit(solution)/shard_map/prologue/pallas_call | solution.py:672
  100.5 1.4 copy-done.2
  101.9 0.9 copy-done.10
  105.0 1.0 slice_bitcast_fusion
  106.7 2.4 reshape.470
  109.7 31.2 %highway_stage.1 = (f32[512,1024]{1,0:T(8,128)}, bf16[512,512]{1,0:T(8,128)(2,1)S(1)}, bf16[512,768]{1,0:T(8,128)(2,1)S(1)}, bf16[192,768]{1,0:T(8,128)(2,1)S(1)...) custom-call(bf16[8,171,768]{2,1,0:T(8,128)(2,1)} %all-gather.8.clone, ...), custom_call_target="tpu_custom_call" | custom-call | tf_op jit(solution)/shard_map/highway_stage/pallas_call | solution.py:761
  143.8 0.9 copy-done.20
  145.8 0.8 copy.160.refs_7_
  147.0 16.4 %forward_stage.1 = (f32[128,768]{1,0:T(8,128)S(1)}, f32[128,768]{1,0:T(8,128)S(1)}, f32[128,1]{1,0:T(8,128)S(1)}, bf16[4,128,768]{2,1,0:T(8,128)(2,1)S(1)}) custom-call(bf16[4,128,768]{2,1,0:T(8,128)(2,1)S(1)} %bitcast.129, f32[128,768]{1,0:T(8,128)S(1)} %get-tuple-element.84.base_ref, f32[1,768]{1,0:T(1,128)S(1)} %slice.80.gain_ref, ...), custom_call_target="tpu_custom_call" | custom-call | tf_op jit(solution)/shard_map/forward_stage/pallas_call | solution.py:220
  163.5 1.8 fusion.42
  165.3 0.9 multiply_convert_fusion.1
  167.1 15.7 %top_stage.1 = (bf16[128,768]{1,0:T(8,128)(2,1)S(1)}, f32[128,768]{1,0:T(8,128)S(1)}, f32[1,768]{1,0:T(1,128)S(1)}, f32[1,768]{1,0:T(1,128)S(1)}, bf16[4,128,768]{2,1,0:T(8,128)(2,1)S(1)}) custom-call(bf16[4,128,768]{2,1,0:T(8,128)(2,1)S(1)} %bitcast.133, f32[128,768]{1,0:T(8,128)S(1)} %get-tuple-element.88.base_ref, bf16[128,768]{1,0:T(8,128)(2,1)S(1)} %bitcast.136, ...), custom_call_target="tpu_custom_call" | custom-call | tf_op jit(solution)/shard_map/top_stage/pallas_call | solution.py:220
  182.8 0.8 convolution_convert_fusion
  183.7 1.1 convert_reduce_fusion
  185.6 0.8 convolution_convert_fusion.3
  186.5 20.6 %backward_stage.2 = (f32[128,768]{1,0:T(8,128)S(1)}, f32[1,768]{1,0:T(1,128)S(1)}, f32[1,768]{1,0:T(1,128)S(1)}, f32[1,768]{1,0:T(1,128)}, bf16[4,128,768]{2,1,0...) custom-call(bf16[4,128,768]{2,1,0:T(8,128)(2,1)S(1)} %bitcast.132, f32[128,768]{1,0:T(8,128)S(1)} %get-tuple-element.91.base_ref, ...), custom_call_target="tpu_custom_call" | custom-call | tf_op jit(solution)/shard_map/backward_stage/pallas_call | solution.py:365
  207.6 1.1 multiply_reduce_fusion
  208.7 1.0 multiply_convert_fusion
  212.3 0.8 convolution_convert_fusion.5
  213.5 1.5 convolution_convert_fusion.2
  216.0 22.8 %backward_stage.3 = (f32[128,768]{1,0:T(8,128)S(1)}, f32[1,768]{1,0:T(1,128)S(1)}, f32[1,768]{1,0:T(1,128)S(1)}, f32[1,768]{1,0:T(1,128)S(1)}, bf16[4,128,768]{2...) custom-call(bf16[4,128,768]{2,1,0:T(8,128)(2,1)S(1)} %bitcast.131, ...), custom_call_target="tpu_custom_call" | custom-call | tf_op jit(solution)/shard_map/backward_stage/pallas_call | solution.py:365
  238.8 0.9 copy-done.12
  241.0 0.8 fusion.13.refs_18_
  241.9 2.2 copy.157
  244.9 1.4 concatenate.43.refs_20_
  246.3 115.6 %epilogue.1 = (bf16[4,256,1024]{2,1,0:T(8,128)(2,1)}, bf16[4,96,576]{2,1,0:T(8,128)(2,1)}, bf16[4,96,768]{2,1,0:T(8,128)(2,1)}, bf16[4,192,768]{2,1,0:T(8,128)(2...) custom-call(bf16[512,768]{1,0:T(8,128)(2,1)} %bitcast.130, ...), custom_call_target="tpu_custom_call" | custom-call | tf_op jit(solution)/shard_map/epilogue/pallas_call | solution.py:1127
  361.9 6.5 %assemble.1 = (f32[256,4096]{1,0:T(8,128)}, f32[96,2304]{1,0:T(8,128)}, f32[256,768]{1,0:T(8,128)}, f32[96,768]{1,0:T(8,128)}, f32[96,3072]{1,0:T(8,128)}, /*ind...) custom-call(bf16[4,256,1024]{2,1,0:T(8,128)(2,1)} %get-tuple-element, ...), custom_call_target="tpu_custom_call" | custom-call | tf_op jit(solution)/shard_map/assemble/pallas_call | solution.py:1207
  368.5 1.6 copy.162
  370.1 1.2 reduce.15
  (184 shorter events, 20.7 us)
Async XLA Ops:
  7.2 95.7 %copy-start = (bf16[384,768]{1,0:T(8,128)(2,1)S(1)}, bf16[384,768]{1,0:T(8,128)(2,1)}, u32[]{:S(2)}) copy-start(bf16[384,768]{1,0:T(8,128)(2,1)} %param.34) | copy-start | bytes 1769476
  7.2 3.0 copy-start.29
  7.2 97.8 %all-gather.8.cloned.1.call-start = ((), (), s32[]{:S(2)}) async-start(), calls=%async_computation.1 | async-start | bytes 2433024 | tf_op jit(solution)/shard_map/all_gather | solution.py:1359
  7.3 3.5 copy-start.31
  10.0 1.4 copy-start.39
  10.0 1.5 copy-start.35
  10.0 1.5 copy-start.36
  10.0 1.5 copy-start.40
  10.2 2.2 copy-start.28
  11.6 3.1 copy-start.37
  11.6 3.2 copy-start.32
  12.4 3.4 copy-start.33
  12.4 3.4 copy-start.34
  12.4 151.1 %all-gather.6.cloned.1.call-start = ((), (), s32[]{:S(2)}) async-start(), calls=%async_computation | async-start | bytes 2654208 | tf_op jit(solution)/shard_map/all_gather | solution.py:1396
  15.8 84.7 %copy-start.7 = (bf16[512,128]{1,0:T(8,128)(2,1)}, bf16[512,128]{1,0:T(8,128)(2,1)S(1)}, u32[]{:S(2)}) copy-start(bf16[512,128]{1,0:T(8,128)(2,1)S(1)} %copy.142.weight_ref.refs_12_) | copy-start | bytes 393220
  15.9 84.6 %copy-start.9 = (s32[56,512]{1,0:T(8,128)}, s32[56,512]{1,0:T(8,128)S(1)}, u32[]{:S(2)}) copy-start(s32[56,512]{1,0:T(8,128)S(1)} %pad_bitcast_fusion.chars_ref.refs_9_) | copy-start | bytes 344068
  16.1 84.4 %copy-start.4 = (s32[512,1]{1,0:T(8,128)}, s32[512,1]{1,0:T(8,128)S(1)}, u32[]{:S(2)}) copy-start(s32[512,1]{1,0:T(8,128)S(1)} %broadcast_subtract_fusion.limit_ref.refs_14_) | copy-start | bytes 6148
  16.3 86.6 %copy-start.5 = (f32[512,1]{1,0:T(8,128)}, f32[512,1]{1,0:T(8,128)S(1)}, u32[]{:S(2)}) copy-start(f32[512,1]{1,0:T(8,128)S(1)} %convert_log_fusion.count_ref.refs_15_) | copy-start | bytes 6148
  102.8 3.8 %copy-start.8 = (f32[512,512]{1,0:T(8,128)}, f32[512,512]{1,0:T(8,128)S(1)}, u32[]{:S(2)}) copy-start(f32[512,512]{1,0:T(8,128)S(1)} %get-tuple-element.104.refs_11_) | copy-start | bytes 3145732
  102.8 6.8 %copy-start.6 = (bf16[512,512]{1,0:T(8,128)(2,1)}, bf16[512,512]{1,0:T(8,128)(2,1)S(1)}, u32[]{:S(2)}) copy-start(bf16[512,512]{1,0:T(8,128)(2,1)S(1)} %get-tuple-element.81.acts_ref.refs_4_) | copy-start | bytes 1572868
  105.0 1.7 slice-start
  106.7 2.9 copy-start.30
  109.6 31.2 %copy-start.26 = (bf16[768,576]{1,0:T(8,128)(2,1)S(1)}, bf16[768,576]{1,0:T(8,128)(2,1)}, u32[]{:S(2)}) copy-start(bf16[768,576]{1,0:T(8,128)(2,1)} %reshape.470) | copy-start | bytes 2654212
  140.9 1.4 copy-start.18
  142.3 3.1 copy-start.24
  143.1 1.7 copy-start.20
  145.4 1.7 copy-start.22
  186.5 21.1 %copy-start.21 = (f32[3,512,512]{1,2,0:T(8,128)S(1)}, f32[3,512,512]{1,2,0:T(8,128)}, u32[]{:S(2)}) copy-start(f32[3,512,512]{1,2,0:T(8,128)} %copy-done.20) | copy-start | bytes 9437188
  186.5 21.1 %copy-start.25 = (bf16[512,192]{0,1:T(8,128)(2,1)S(1)}, bf16[512,192]{0,1:T(8,128)(2,1)}, u32[]{:S(2)}) copy-start(bf16[512,192]{0,1:T(8,128)(2,1)} %copy-done.24) | copy-start | bytes 589828
  207.1 1.6 copy-start.3
  209.7 1.4 copy-start.23
  361.9 10.1 %copy-start.1 = (bf16[384,768]{1,0:T(8,128)(2,1)S(1)}, bf16[384,768]{1,0:T(8,128)(2,1)}, u32[]{:S(2)}) copy-start(bf16[384,768]{1,0:T(8,128)(2,1)} %param.34) | copy-start | bytes 1769476
  (12 other events, 12.7 us)
Sparse Core Ops, SparseCore 0:
  12.5 80.5 all-gather.7
  103.8 55.8 all-gather.5
